TPU v7x, 32 devices: a whole 2x2x4 slice. The times are simulated.
32 devices in a mesh: fsdp: 4 (over y, x), ctx: 2 (over core), tp: 4 (over z).
Axes of the slice: x: 2, y: 2, z: 4, core: 2. Of those that a mesh axis runs over, the one named last changes fastest.
Arguments:
- inputs: bfloat16 [4, 2048, 2048], P('fsdp', 'ctx'), may hold values from -6 to 6
- lengths: int32 [4], P('fsdp'), may hold values from 512 to 2048, as said below
- w_query: bfloat16 [2048, 2048], P('fsdp', 'tp'), may hold values from -0.125 to 0.125
- w_forget: bfloat16 [2048, 2048], P('fsdp', 'tp'), may hold values from -0.125 to 0.125
- w_input: bfloat16 [2048, 2048], P('fsdp', 'tp'), may hold values from -0.125 to 0.125
- w_outgate: bfloat16 [2048, 2048], P('fsdp', 'tp'), may hold values from -0.125 to 0.125
- w_output: bfloat16 [2048, 2048], P('tp', 'fsdp'), may hold values from -0.125 to 0.125
- w_gate: bfloat16 [2048, 5632], P('fsdp', 'tp'), may hold values from -0.125 to 0.125
- w_up: bfloat16 [2048, 5632], P('fsdp', 'tp'), may hold values from -0.125 to 0.125
- w_down: bfloat16 [5632, 2048], P('tp', 'fsdp'), may hold values from -0.078125 to 0.078125
- norm_gain: float32 [2048], replicated, may hold values from 0.5 to 1.5
- ffn_gain: float32 [2048], replicated, may hold values from 0.5 to 1.5
- head_gain: float32 [128], replicated, may hold values from 0.5 to 1.5
- forget_gap: float32 [2048], P('tp'), may hold values from 0.0002 to 0.06
- cotangent: bfloat16 [4, 2048, 2048], P('fsdp', 'ctx'), may hold values from -6 to 6
Outputs:
- output: bfloat16 [4, 2048, 2048], P('fsdp', 'ctx')
- input_grad: bfloat16 [4, 2048, 2048], P('fsdp', 'ctx')
- grad_w_query: float32 [2048, 2048], P(('fsdp', 'ctx'), 'tp')
- grad_w_forget: float32 [2048, 2048], P(('fsdp', 'ctx'), 'tp')
- grad_w_input: float32 [2048, 2048], P(('fsdp', 'ctx'), 'tp')
- grad_w_outgate: float32 [2048, 2048], P(('fsdp', 'ctx'), 'tp')
- grad_w_output: float32 [2048, 2048], P('tp', ('fsdp', 'ctx'))
- grad_w_gate: float32 [2048, 5632], P(('fsdp', 'ctx'), 'tp')
- grad_w_up: float32 [2048, 5632], P(('fsdp', 'ctx'), 'tp')
- grad_w_down: float32 [5632, 2048], P('tp', ('fsdp', 'ctx'))
- grad_norm_gain: float32 [2048], replicated
- grad_ffn_gain: float32 [2048], replicated
- grad_head_gain: float32 [128], replicated
- grad_forget_gap: float32 [2048], P('tp')
Inputs may be any that keep to these rules, and one draw needn't show every extreme that they name: `lengths`: valid slots of each sequence; slots from that length on are padding. Some sequence is full and some has 512 slots.
All inputs are finite; a program needn't handle non-finite values.
Results may differ from a plain program's by a relative error of at most 0.0095.
Values may be sent and summed in bfloat16 or wider, within the bound.
A program may use at most 320 MiB of HBM per device.

v0:
```python
import jax
import jax.numpy as jnp
from jax import lax
from jax.sharding import PartitionSpec as P

HEAD_DIM = 128


EPSILON = 1e-05
HIGHEST = lax.Precision.HIGHEST


def prefix(array, axis, combine, identity):
    length, mine = (lax.axis_size(axis), lax.axis_index(axis))
    everything = jax.tree.map(lambda part: lax.all_gather(part, axis), array)
    start = jax.tree.map(
        lambda part, zero: jnp.broadcast_to(jnp.asarray(zero, part.dtype), part.shape),
        array,
        identity,
    )

    def hop(k, before):
        reached = k < mine
        new = combine(before, jax.tree.map(lambda part: part[k], everything))
        return jax.tree.map(lambda a, b: jnp.where(reached, a, b), new, before)

    return lax.fori_loop(0, length, hop, start)


def prefix_2(array, axis, join, neutral):
    count = lax.axis_size(axis)
    place = lax.axis_index(axis)
    ahead = count - 1 - place
    gathered = jax.tree.map(
        lambda a, kind: lax.all_gather(a.astype(kind), axis), array, (jnp.bfloat16, jnp.bfloat16)
    )
    state = jax.tree.map(lambda a, e: jnp.zeros_like(a) + jnp.asarray(e, a.dtype), array, neutral)

    def one(hop, state):
        source = count - 1 - hop
        return join(
            state,
            jax.tree.map(
                lambda a, own: lax.dynamic_index_in_dim(a, source, 0, False).astype(own.dtype),
                gathered,
                array,
            ),
        )

    return lax.fori_loop(0, ahead, one, state)


def einsum_high(formula, left_side, right_side):
    return jnp.einsum(formula, left_side, right_side, precision=HIGHEST)


def forward_mm(left_side, right_side):
    return jnp.dot(left_side, right_side, preferred_element_type=jnp.float32)


def outer_rows(left_side, right_side):
    return lax.dot_general(
        left_side, right_side, (((0,), (0,)), ((), ())), preferred_element_type=jnp.float32
    )


def through_transpose(left_side, right_side):
    return lax.dot_general(
        left_side, right_side, (((1,), (1,)), ((), ())), preferred_element_type=jnp.float32
    )


def chain_pair(earlier_pair, later_pair):
    return (
        earlier_pair[0] * later_pair[0],
        later_pair[0][..., None] * earlier_pair[1] + later_pair[1],
    )


def norm_back(grad_out, scaled, inverse, gain_vec):
    weighted = grad_out * gain_vec
    return inverse * (weighted - scaled * jnp.mean(weighted * scaled, axis=-1, keepdims=True))


def silu_slope(pre_act, sig_value):
    return sig_value * (1.0 + pre_act * (1.0 - sig_value))


def per_device(
    inputs,
    lengths,
    w_query,
    w_forget,
    w_input,
    w_outgate,
    w_output,
    w_gate,
    w_up,
    w_down,
    norm_gain,
    ffn_gain,
    head_gain,
    forget_gap,
    cotangent,
):
    groups, span_len, model_width = inputs.shape
    row_count = groups * span_len
    local_width = forget_gap.shape[0]
    heads_here = local_width // HEAD_DIM
    block_len = min(64, span_len)
    block_count = span_len // block_len
    positions = lax.axis_index("ctx") * span_len + jnp.arange(span_len, dtype=jnp.int32)
    keep_mask = (positions[None, :] < lengths[:, None]).astype(jnp.float32).reshape(row_count, 1)
    gathered = (
        lax.all_gather(w_query, "fsdp", axis=0, tiled=True),
        lax.all_gather(w_forget, "fsdp", axis=0, tiled=True),
        lax.all_gather(w_input, "fsdp", axis=0, tiled=True),
        lax.all_gather(w_outgate, "fsdp", axis=0, tiled=True),
        lax.all_gather(w_output, "fsdp", axis=1, tiled=True),
        lax.all_gather(w_gate, "fsdp", axis=0, tiled=True),
        lax.all_gather(w_up, "fsdp", axis=0, tiled=True),
        lax.all_gather(w_down, "fsdp", axis=1, tiled=True),
    )
    (
        full_query,
        full_forget,
        full_input,
        full_outgate,
        full_output,
        full_gate,
        full_up,
        full_down,
    ) = gathered
    source = inputs.reshape(row_count, model_width).astype(jnp.float32)
    inverse_one = lax.rsqrt(jnp.mean(source * source, axis=-1, keepdims=True) + EPSILON)
    scaled_one = source * inverse_one
    normed = (scaled_one * norm_gain).astype(jnp.bfloat16)
    query_pre = forward_mm(normed, full_query)
    forget_pre = forward_mm(normed, full_forget)
    value_pre = forward_mm(normed, full_input)
    gate_pre = forward_mm(normed, full_outgate)
    query_sigma = jax.nn.sigmoid(query_pre)
    queries = query_pre * query_sigma
    closing = jax.nn.sigmoid(-forget_pre)
    remain = 1.0 - forget_gap * closing
    keys_live = forget_gap * closing * keep_mask
    decays = jnp.log(remain) * keep_mask

    def to_tokens(tensor):
        return tensor.reshape(groups, span_len, heads_here, HEAD_DIM)

    def to_blocks(tensor):
        return tensor.reshape(groups, block_count, block_len, heads_here, HEAD_DIM).transpose(
            1, 0, 3, 2, 4
        )

    def from_blocks(tensor):
        return tensor.transpose(1, 0, 3, 2, 4).reshape(groups, span_len, heads_here, HEAD_DIM)

    query_tok = to_tokens(queries)
    key_tok = to_tokens(keys_live)
    value_tok = to_tokens(value_pre)
    decay_tok = to_tokens(decays)
    lower_mask = jnp.tril(jnp.ones((block_len, block_len), jnp.float32))

    def forward_block(carried, block_data):
        query_block, key_block, value_block, decay_block = block_data
        cumulative = jnp.cumsum(decay_block, axis=2)
        growth = jnp.exp(cumulative)
        query_scaled = query_block * growth
        key_scaled = key_block * jnp.exp(-cumulative)
        scores = einsum_high("shtd,shud->shtu", query_scaled, key_scaled) * lower_mask
        outputs = einsum_high("shtu,shue->shte", scores, value_block) + einsum_high(
            "shtd,shde->shte", query_scaled, carried
        )
        final_growth = growth[:, :, -1, :]
        updated = final_growth[..., None] * carried + einsum_high(
            "shud,shue->shde", key_scaled * final_growth[:, :, None, :], value_block
        )
        return (updated, (outputs, carried))

    zero_state = jnp.zeros((groups, heads_here, HEAD_DIM, HEAD_DIM), jnp.float32)
    local_end, (local_out, block_starts) = lax.scan(
        forward_block,
        zero_state,
        (to_blocks(query_tok), to_blocks(key_tok), to_blocks(value_tok), to_blocks(decay_tok)),
    )
    running_decay = jnp.cumsum(decay_tok, axis=1)
    span_decay = jnp.exp(running_decay[:, -1])
    identity = (jnp.ones_like(span_decay), jnp.zeros_like(local_end))
    state_start = prefix((span_decay, local_end), "ctx", chain_pair, identity)[1]
    growth_tok = jnp.exp(running_decay)
    mixed_tok = from_blocks(local_out) + einsum_high(
        "sthd,shde->sthe", query_tok * growth_tok, state_start
    )
    state_end = local_end + span_decay[..., None] * state_start
    inverse_head = lax.rsqrt(jnp.mean(mixed_tok * mixed_tok, axis=-1, keepdims=True) + EPSILON)
    scaled_head = mixed_tok * inverse_head
    normed_head = (scaled_head * head_gain).reshape(row_count, local_width)
    gate_sigma = jax.nn.sigmoid(gate_pre)
    gate_act = gate_pre * gate_sigma
    gated = (normed_head * gate_act).astype(jnp.bfloat16)
    branch = lax.psum(forward_mm(gated, full_output), "tp")
    middle = source + branch
    inverse_two = lax.rsqrt(jnp.mean(middle * middle, axis=-1, keepdims=True) + EPSILON)
    scaled_two = middle * inverse_two
    normed_two = (scaled_two * ffn_gain).astype(jnp.bfloat16)
    gate_hidden = forward_mm(normed_two, full_gate)
    up_hidden = forward_mm(normed_two, full_up)
    hidden_sigma = jax.nn.sigmoid(gate_hidden)
    hidden_act = gate_hidden * hidden_sigma
    hidden = (hidden_act * up_hidden).astype(jnp.bfloat16)
    feed = lax.psum(forward_mm(hidden, full_down), "tp")
    result = (middle + feed).astype(jnp.bfloat16).reshape(groups, span_len, model_width)
    back_weights = (
        lax.all_gather(w_query, "fsdp", axis=0, tiled=True),
        lax.all_gather(w_forget, "fsdp", axis=0, tiled=True),
        lax.all_gather(w_input, "fsdp", axis=0, tiled=True),
        lax.all_gather(w_outgate, "fsdp", axis=0, tiled=True),
        lax.all_gather(w_output, "fsdp", axis=1, tiled=True),
        lax.all_gather(w_gate, "fsdp", axis=0, tiled=True),
        lax.all_gather(w_up, "fsdp", axis=0, tiled=True),
        lax.all_gather(w_down, "fsdp", axis=1, tiled=True),
    )
    (
        back_query,
        back_forget,
        back_input,
        back_outgate,
        back_output,
        back_gate,
        back_up,
        back_down,
    ) = back_weights
    grad_out = cotangent.reshape(row_count, model_width).astype(jnp.float32) * keep_mask
    grad_low = grad_out.astype(jnp.bfloat16)
    grad_w_down = outer_rows(hidden, grad_low)
    grad_hidden = through_transpose(grad_low, back_down)
    grad_gate_low = (grad_hidden * up_hidden * silu_slope(gate_hidden, hidden_sigma)).astype(
        jnp.bfloat16
    )
    grad_up_low = (grad_hidden * hidden_act).astype(jnp.bfloat16)
    grad_normed_two = lax.psum(
        through_transpose(grad_gate_low, back_gate) + through_transpose(grad_up_low, back_up), "tp"
    )
    grad_w_gate = outer_rows(normed_two, grad_gate_low)
    grad_w_up = outer_rows(normed_two, grad_up_low)
    grad_ffn_gain = jnp.sum(grad_normed_two * scaled_two, axis=0)
    grad_middle = grad_out + norm_back(grad_normed_two, scaled_two, inverse_two, ffn_gain)
    grad_branch = grad_middle.astype(jnp.bfloat16)
    grad_w_output = outer_rows(gated, grad_branch)
    grad_gated = through_transpose(grad_branch, back_output)
    grad_outgate_low = (grad_gated * normed_head * silu_slope(gate_pre, gate_sigma)).astype(
        jnp.bfloat16
    )
    grad_scaled = (grad_gated * gate_act).reshape(groups, span_len, heads_here, HEAD_DIM)
    head_gain_part = jnp.sum(grad_scaled * scaled_head, axis=(0, 1, 2))
    grad_mixed = norm_back(grad_scaled, scaled_head, inverse_head, head_gain)

    def backward_block(grad_state, block_data):
        query_block, key_block, value_block, decay_block, grad_block, start_block = block_data
        cumulative = jnp.cumsum(decay_block, axis=2)
        growth = jnp.exp(cumulative)
        shrink = jnp.exp(-cumulative)
        query_scaled = query_block * growth
        key_scaled = key_block * shrink
        final_growth = growth[:, :, -1, :]
        scores = einsum_high("shtd,shud->shtu", query_scaled, key_scaled) * lower_mask
        grad_scores = einsum_high("shte,shue->shtu", grad_block, value_block) * lower_mask
        grad_query = (
            einsum_high("shte,shde->shtd", grad_block, start_block)
            + einsum_high("shtu,shud->shtd", grad_scores, key_scaled)
        ) * growth
        key_back = einsum_high("shtu,shtd->shud", grad_scores, query_scaled) + final_growth[
            :, :, None, :
        ] * einsum_high("shde,shue->shud", grad_state, value_block)
        grad_key = key_back * shrink
        grad_value = einsum_high("shtu,shte->shue", scores, grad_block) + einsum_high(
            "shud,shde->shue", key_scaled * final_growth[:, :, None, :], grad_state
        )
        previous = final_growth[..., None] * grad_state + einsum_high(
            "shtd,shte->shde", query_scaled, grad_block
        )
        return (previous, (grad_query, grad_key, grad_value))

    local_begin, (query_grad_blocks, key_grad_blocks, value_grad_blocks) = lax.scan(
        backward_block,
        zero_state,
        (
            to_blocks(query_tok),
            to_blocks(key_tok),
            to_blocks(value_tok),
            to_blocks(decay_tok),
            to_blocks(grad_mixed),
            block_starts,
        ),
        reverse=True,
    )
    grad_end = prefix_2((span_decay, local_begin), "ctx", chain_pair, identity)[1]
    grad_query_tok = from_blocks(query_grad_blocks) + growth_tok * einsum_high(
        "sthe,shde->sthd", grad_mixed, state_start
    )
    tail_decay = jnp.exp(running_decay[:, -1:] - running_decay)
    grad_key_tok = from_blocks(key_grad_blocks) + tail_decay * einsum_high(
        "shde,sthe->sthd", grad_end, value_tok
    )
    grad_value_tok = from_blocks(value_grad_blocks) + einsum_high(
        "sthd,shde->sthe", key_tok * tail_decay, grad_end
    )
    local_terms = query_tok * grad_query_tok - key_tok * grad_key_tok
    suffix = jnp.flip(jnp.cumsum(jnp.flip(local_terms, axis=1), axis=1), axis=1)
    grad_decay_tok = suffix + jnp.sum(grad_end * state_end, axis=-1)[:, None]
    grad_decay = grad_decay_tok.reshape(row_count, local_width) * keep_mask
    grad_key = grad_key_tok.reshape(row_count, local_width) * keep_mask
    pressure = grad_key - grad_decay / remain
    grad_gap = jnp.sum(closing * pressure, axis=0)
    grad_forget_low = (-closing * (1.0 - closing) * forget_gap * pressure).astype(jnp.bfloat16)
    grad_query_low = (
        grad_query_tok.reshape(row_count, local_width) * silu_slope(query_pre, query_sigma)
    ).astype(jnp.bfloat16)
    grad_value_low = grad_value_tok.reshape(row_count, local_width).astype(jnp.bfloat16)
    grad_w_query = outer_rows(normed, grad_query_low)
    grad_w_forget = outer_rows(normed, grad_forget_low)
    grad_w_input = outer_rows(normed, grad_value_low)
    grad_w_outgate = outer_rows(normed, grad_outgate_low)
    normed_part = (
        through_transpose(grad_query_low, back_query)
        + through_transpose(grad_forget_low, back_forget)
        + through_transpose(grad_value_low, back_input)
        + through_transpose(grad_outgate_low, back_outgate)
    )
    grad_normed, grad_head_gain = lax.psum((normed_part, head_gain_part), "tp")
    grad_norm_gain = jnp.sum(grad_normed * scaled_one, axis=0)
    input_grad = (
        (grad_middle + norm_back(grad_normed, scaled_one, inverse_one, norm_gain))
        .astype(jnp.bfloat16)
        .reshape(groups, span_len, model_width)
    )
    weight_shards = (
        lax.psum_scatter(grad_w_query, ("fsdp", "ctx"), scatter_dimension=0, tiled=True),
        lax.psum_scatter(grad_w_forget, ("fsdp", "ctx"), scatter_dimension=0, tiled=True),
        lax.psum_scatter(grad_w_input, ("fsdp", "ctx"), scatter_dimension=0, tiled=True),
        lax.psum_scatter(grad_w_outgate, ("fsdp", "ctx"), scatter_dimension=0, tiled=True),
        lax.psum_scatter(grad_w_output, ("fsdp", "ctx"), scatter_dimension=1, tiled=True),
        lax.psum_scatter(grad_w_gate, ("fsdp", "ctx"), scatter_dimension=0, tiled=True),
        lax.psum_scatter(grad_w_up, ("fsdp", "ctx"), scatter_dimension=0, tiled=True),
        lax.psum_scatter(grad_w_down, ("fsdp", "ctx"), scatter_dimension=1, tiled=True),
    )
    gain_sums = lax.psum((grad_norm_gain, grad_ffn_gain, grad_head_gain, grad_gap), ("fsdp", "ctx"))
    return (
        result,
        input_grad,
        weight_shards[0],
        weight_shards[1],
        weight_shards[2],
        weight_shards[3],
        weight_shards[4],
        weight_shards[5],
        weight_shards[6],
        weight_shards[7],
        gain_sums[0],
        gain_sums[1],
        gain_sums[2],
        gain_sums[3],
    )


def solution(mesh):
    return jax.shard_map(
        per_device,
        mesh=mesh,
        in_specs=(
            P("fsdp", "ctx", None),
            P("fsdp"),
            P("fsdp", "tp"),
            P("fsdp", "tp"),
            P("fsdp", "tp"),
            P("fsdp", "tp"),
            P("tp", "fsdp"),
            P("fsdp", "tp"),
            P("fsdp", "tp"),
            P("tp", "fsdp"),
            P(),
            P(),
            P(),
            P("tp"),
            P("fsdp", "ctx", None),
        ),
        out_specs=(
            P("fsdp", "ctx", None),
            P("fsdp", "ctx", None),
            P(("fsdp", "ctx"), "tp"),
            P(("fsdp", "ctx"), "tp"),
            P(("fsdp", "ctx"), "tp"),
            P(("fsdp", "ctx"), "tp"),
            P("tp", ("fsdp", "ctx")),
            P(("fsdp", "ctx"), "tp"),
            P(("fsdp", "ctx"), "tp"),
            P("tp", ("fsdp", "ctx")),
            P(),
            P(),
            P(),
            P("tp"),
        ),
        check_vma=False,
    )
```

profile of v0, /device:TPU:0, one launch (start us, length us, event | category | flops | bytes accessed | tf_op | source)
XLA Modules:
  0.0 2565.7 jit_solution(15006675793846180328)
XLA Ops:
  14.4 33.3 %all-gather.11.cloned.1.call-done = bf16[2048,512]{1,0:T(8,128)(2,1)} async-done(((bf16[512,512]{1,0:T(8,128)(2,1)}), bf16[2048,512]{1,0:T(8,128)(2,1)}) %all-gather.11.cloned.1.call-update) | async-done | bytes 2097168 | tf_op jit(solution)/shard_map/all_gather | solution.py:116
  47.8 7.9 multiply_multiply_fusion
  75.9 8.9 all-gather.15.cloned.1.call-done
  84.8 6.9 fusion.121
  100.0 21.9 all-gather.13.cloned.1.call-done
  137.0 127.0 %while.66 = (s32[]{:T(128)}, f32[1,4,128,128]{3,2,1,0:T(8,128)S(1)}, f32[16,1,4,64,128]{4,3,0,2,1:T(8,128)}, f32[16,1,4,128,128]{4,3,2,1,0:T(8,128)}, f32[16,1,4...) while((s32[]{:T(128)}, ...), condition=%wide.region_3.4_spmd.clone, body=%wide.region_1.3_spmd.clone.sunk | while | flops 153673728 | bytes 3993729 | solution.py:183
  284.9 7.8 fusion.105
  292.7 7.5 fusion.157
  302.6 288.8 %all-reduce.6.cloned.1.call-done = f32[1024,2048]{1,0:T(8,128)} async-done(((f32[1024,2048]{1,0:T(8,128)}), f32[1024,2048]{1,0:T(8,128)}) %all-reduce.6.cloned.1.call-update) | async-done | bytes 8388624 | tf_op jit(solution)/shard_map/psum | solution.py:203
  591.4 5.7 multiply_reduce_fusion.2
  603.7 54.2 %all-gather.21.cloned.1.call-done = bf16[2048,1408]{1,0:T(8,128)(2,1)} async-done(((bf16[512,1408]{1,0:T(8,128)(2,1)}), bf16[2048,1408]{1,0:T(8,128)(2,1)}) %all-gather.21.cloned.1.call-update) | async-done | bytes 5767184 | tf_op jit(solution)/shard_map/all_gather | solution.py:120
  657.9 12.2 fusion.158
  670.1 55.4 %all-gather.23.cloned.1.call-done = bf16[2048,1408]{1,0:T(8,128)(2,1)} async-done(((bf16[512,1408]{1,0:T(8,128)(2,1)}), bf16[2048,1408]{1,0:T(8,128)(2,1)}) %all-gather.23.cloned.1.call-update) | async-done | bytes 5767184 | tf_op jit(solution)/shard_map/all_gather | solution.py:121
  725.4 11.7 fusion.159
  737.1 55.7 %all-gather.25.cloned.1.call-done = bf16[1408,2048]{1,0:T(8,128)(2,1)} async-done(((bf16[1408,512]{1,0:T(8,128)(2,1)}), bf16[1408,2048]{1,0:T(8,128)(2,1)}) %all-gather.25.cloned.1.call-update) | async-done | bytes 5767184 | tf_op jit(solution)/shard_map/all_gather | solution.py:122
  792.8 15.8 multiply_convert_fusion.1
  808.6 10.9 fusion.161
  819.5 9.0 convolution_add_fusion.3
  834.2 11.8 fusion.160
  846.0 273.6 %all-reduce.8.cloned.1.call-done = f32[1024,2048]{1,0:T(8,128)} async-done(((f32[1024,2048]{1,0:T(8,128)}), f32[1024,2048]{1,0:T(8,128)}) %all-reduce.8.cloned.1.call-update) | async-done | bytes 8388624 | tf_op jit(solution)/shard_map/psum | solution.py:243
  1119.5 7.6 multiply_reduce_fusion
  1134.5 9.8 fusion.107
  1158.1 206.2 %while.68 = (s32[]{:T(128)}, f32[1,4,128,128]{3,2,1,0:T(8,128)S(1)}, f32[16,1,4,64,128]{4,3,0,2,1:T(8,128)}, f32[16,1,4,64,128]{4,3,0,2,1:T(8,128)}, f32[16,1,4,...) while((s32[]{:T(128)}, ...), condition=%wide.region_17.18_spmd.clone.clone, body=%wide.region_15.17_spmd.clone.clone.sunk | while | flops 329949184 | bytes 6158524 | solution.py:286
  1376.1 10.1 multiply_subtract_fusion
  1395.8 10.2 rev.8
  1426.5 5.7 fusion.162
  1432.2 5.8 fusion.164
  1437.9 12.4 add_add_fusion
  1451.1 6.9 fusion.141
  1459.2 7.7 fusion.116
  1467.0 7.0 fusion.143
  1475.2 7.0 fusion.92
  1482.6 6.9 fusion.139
  1489.5 11.9 fusion.165
  1501.5 11.9 fusion.166
  1513.7 11.6 fusion.122
  1525.4 11.3 psum.69
  1536.7 475.3 %all-reduce.10.cloned.1.call-done = (f32[1024,2048]{1,0:T(8,128)}, f32[1024,2048]{1,0:T(8,128)}) async-done(((f32[1024,2048]{1,0:T(8,128)}, f32[1024,2048]{1,0:T(8,128)}), (f32[1024,2048]{1,0:T(8,128)}, f32[1024,2048]{1,0:T(8,128)})) %all-reduce.10.cloned.1.call-update) | async-done | bytes 16777232 | tf_op jit(solution)/shard_map/psum | solution.py:213
  2012.0 5.9 fusion.83
  2017.9 24.7 all-reduce
  2042.6 18.6 fusion.90
  2065.9 55.0 %reduce-scatter.17.cloned.1.call-done = f32[512,256]{1,0:T(8,128)} async-done(((f32[512,2048]{1,0:T(8,128)}), f32[512,256]{1,0:T(8,128)}) %reduce-scatter.17.cloned.1.call-update) | async-done | bytes 524304 | tf_op jit(solution)/shard_map/reduce_scatter | solution.py:344
  2120.9 55.0 %reduce-scatter.9.cloned.1.call-done = f32[256,512]{1,0:T(8,128)} async-done(((f32[2048,512]{1,0:T(8,128)}), f32[256,512]{1,0:T(8,128)}) %reduce-scatter.9.cloned.1.call-update) | async-done | bytes 524304 | tf_op jit(solution)/shard_map/reduce_scatter | solution.py:340
  2175.9 55.0 %reduce-scatter.13.cloned.1.call-done = f32[256,512]{1,0:T(8,128)} async-done(((f32[2048,512]{1,0:T(8,128)}), f32[256,512]{1,0:T(8,128)}) %reduce-scatter.13.cloned.1.call-update) | async-done | bytes 524304 | tf_op jit(solution)/shard_map/reduce_scatter | solution.py:342
  2230.8 55.0 %reduce-scatter.15.cloned.1.call-done = f32[256,512]{1,0:T(8,128)} async-done(((f32[2048,512]{1,0:T(8,128)}), f32[256,512]{1,0:T(8,128)}) %reduce-scatter.15.cloned.1.call-update) | async-done | bytes 524304 | tf_op jit(solution)/shard_map/reduce_scatter | solution.py:343
  2285.8 91.1 %reduce-scatter.19.cloned.1.call-done = f32[256,1408]{1,0:T(8,128)} async-done(((f32[2048,1408]{1,0:T(8,128)}), f32[256,1408]{1,0:T(8,128)}) %reduce-scatter.19.cloned.1.call-update) | async-done | bytes 1441808 | tf_op jit(solution)/shard_map/reduce_scatter | solution.py:345
  2376.9 91.1 %reduce-scatter.21.cloned.1.call-done = f32[256,1408]{1,0:T(8,128)} async-done(((f32[2048,1408]{1,0:T(8,128)}), f32[256,1408]{1,0:T(8,128)}) %reduce-scatter.21.cloned.1.call-update) | async-done | bytes 1441808 | tf_op jit(solution)/shard_map/reduce_scatter | solution.py:346
  2468.0 90.9 %reduce-scatter.23.cloned.1.call-done = f32[1408,256]{1,0:T(8,128)} async-done(((f32[1408,2048]{1,0:T(8,128)}), f32[1408,256]{1,0:T(8,128)}) %reduce-scatter.23.cloned.1.call-update) | async-done | bytes 1441808 | tf_op jit(solution)/shard_map/reduce_scatter | solution.py:347
  (605 shorter events, 487.8 us)
Async XLA Ops:
  7.2 40.6 %all-gather.11.cloned.1.call-start = ((), (), s32[]{:S(2)}) async-start(), calls=%async_computation.8 | async-start | bytes 2621440 | tf_op jit(solution)/shard_map/all_gather | solution.py:116
  7.9 76.9 %all-gather.15.cloned.1.call-start = ((), (), s32[]{:S(2)}) async-start(), calls=%async_computation.10 | async-start | bytes 2621440 | tf_op jit(solution)/shard_map/all_gather | solution.py:115
  8.7 113.2 %all-gather.13.cloned.1.call-start = ((), (), s32[]{:S(2)}) async-start(), calls=%async_computation.9 | async-start | bytes 2621440 | tf_op jit(solution)/shard_map/all_gather | solution.py:117
  9.4 275.5 %all-gather.17.cloned.1.call-start = ((), (), s32[]{:S(2)}) async-start(), calls=%async_computation.11 | async-start | bytes 2621440 | tf_op jit(solution)/shard_map/all_gather | solution.py:118
  10.0 282.7 %all-gather.19.cloned.1.call-start = ((), (), s32[]{:S(2)}) async-start(), calls=%async_computation.12 | async-start | bytes 2621440 | tf_op jit(solution)/shard_map/all_gather | solution.py:119
  10.6 580.8 %all-reduce.6.cloned.1.call-start = ((), (), s32[]{:S(2)}) async-start(), calls=%async_computation.13 | async-start | bytes 16777216 | tf_op jit(solution)/shard_map/psum | solution.py:203
  10.6 37.1 %copy-start.27 = (f32[2048]{0:T(1024)S(1)}, f32[2048]{0:T(1024)}, u32[]{:S(2)}) copy-start(f32[2048]{0:T(1024)} %param.33) | copy-start | bytes 24580
  10.6 37.1 %copy-start.31 = (f32[512]{0:T(512)S(1)}, f32[512]{0:T(512)}, u32[]{:S(2)}) copy-start(f32[512]{0:T(512)} %param.36) | copy-start | bytes 6148
  13.8 271.1 %copy-start.24 = (f32[1024]{0:T(1024)}, f32[1024]{0:T(1024)S(1)}, u32[]{:S(2)}) copy-start(f32[1024]{0:T(1024)S(1)} %add_rsqrt_fusion.2) | copy-start | bytes 12292
  67.0 3.4 copy-start.13
  264.1 12.1 copy-start.1
  266.2 3.7 copy-start.6
  273.8 4.6 copy-start.8
  278.8 4.3 copy-start.30
  300.3 357.6 %all-gather.21.cloned.1.call-start = ((), (), s32[]{:S(2)}) async-start(), calls=%async_computation.14 | async-start | bytes 7208960 | tf_op jit(solution)/shard_map/all_gather | solution.py:120
  301.0 424.4 %all-gather.23.cloned.1.call-start = ((), (), s32[]{:S(2)}) async-start(), calls=%async_computation.15 | async-start | bytes 7208960 | tf_op jit(solution)/shard_map/all_gather | solution.py:121
  301.8 491.1 %all-gather.25.cloned.1.call-start = ((), (), s32[]{:S(2)}) async-start(), calls=%async_computation.16 | async-start | bytes 7208960 | tf_op jit(solution)/shard_map/all_gather | solution.py:122
  302.5 298.4 %copy-start.23 = (f32[2048]{0:T(1024)S(1)}, f32[2048]{0:T(1024)}, u32[]{:S(2)}) copy-start(f32[2048]{0:T(1024)} %param.34) | copy-start | bytes 24580
  302.5 817.0 %all-reduce.8.cloned.1.call-start = ((), (), s32[]{:S(2)}) async-start(), calls=%async_computation.17 | async-start | bytes 16777216 | tf_op jit(solution)/shard_map/psum | solution.py:243
  597.1 3.8 copy-start
  808.6 10.9 copy-start.39
  808.6 10.9 copy-start.38
  808.6 10.9 copy-start.33
  828.5 1183.5 %all-reduce.10.cloned.1.call-start = ((), (), s32[]{:S(2)}) async-start(), calls=%async_computation.26 | async-start | bytes 33554432 | tf_op jit(solution)/shard_map/psum | solution.py:213
  1119.5 8.2 copy-start.3
  1119.5 9.4 copy-start.17
  1134.5 9.8 copy-start.4
  1146.9 3.0 copy-start.5
  1366.6 3.1 copy-start.12
  1372.9 3.2 copy-start.7
  1372.9 3.2 copy-start.29
  1391.2 2.6 copy-start.2
  1409.6 3.1 copy-start.10
  1416.9 3.1 copy-start.9
  1416.9 5.2 copy-start.19
  1422.1 10.1 copy-start.21
  1426.5 5.7 copy-start.36
  1432.2 5.8 copy-start.18
  1432.2 5.8 copy-start.20
  1450.4 615.5 %reduce-scatter.11.cloned.1.call-start = ((), (), s32[]{:S(2)}) async-start(), calls=%async_computation.19 | async-start | bytes 4718592 | tf_op jit(solution)/shard_map/reduce_scatter | solution.py:341
  1458.0 662.9 %reduce-scatter.17.cloned.1.call-start = ((), (), s32[]{:S(2)}) async-start(), calls=%async_computation.22 | async-start | bytes 4718592 | tf_op jit(solution)/shard_map/reduce_scatter | solution.py:344
  1466.9 709.0 %reduce-scatter.9.cloned.1.call-start = ((), (), s32[]{:S(2)}) async-start(), calls=%async_computation.18 | async-start | bytes 4718592 | tf_op jit(solution)/shard_map/reduce_scatter | solution.py:340
  1474.0 756.8 %reduce-scatter.13.cloned.1.call-start = ((), (), s32[]{:S(2)}) async-start(), calls=%async_computation.20 | async-start | bytes 4718592 | tf_op jit(solution)/shard_map/reduce_scatter | solution.py:342
  1482.3 803.5 %reduce-scatter.15.cloned.1.call-start = ((), (), s32[]{:S(2)}) async-start(), calls=%async_computation.21 | async-start | bytes 4718592 | tf_op jit(solution)/shard_map/reduce_scatter | solution.py:343
  1489.4 887.4 %reduce-scatter.19.cloned.1.call-start = ((), (), s32[]{:S(2)}) async-start(), calls=%async_computation.23 | async-start | bytes 12976128 | tf_op jit(solution)/shard_map/reduce_scatter | solution.py:345
  1501.5 966.5 %reduce-scatter.21.cloned.1.call-start = ((), (), s32[]{:S(2)}) async-start(), calls=%async_computation.24 | async-start | bytes 12976128 | tf_op jit(solution)/shard_map/reduce_scatter | solution.py:346
  1513.4 1045.5 %reduce-scatter.23.cloned.1.call-start = ((), (), s32[]{:S(2)}) async-start(), calls=%async_computation.25 | async-start | bytes 12976128 | tf_op jit(solution)/shard_map/reduce_scatter | solution.py:347
  2012.0 5.9 copy-start.26
  (11 other events, 18.6 us)
Sparse Core Ops, SparseCore 0:
  9.8 37.8 all-gather.10
  49.6 35.1 all-gather.14
  86.7 35.1 all-gather.12
  123.6 35.1 all-gather.16
  160.5 35.0 all-gather.18
  300.4 290.9 all-reduce.5
  593.2 64.6 all-gather.20
  659.7 65.6 all-gather.22
  727.3 65.5 all-gather.24
  828.7 290.8 all-reduce.7
  1450.5 561.4 all-reduce.9
  2015.8 50.0 reduce-scatter.10
  2069.8 51.0 reduce-scatter.16
  2124.7 51.1 reduce-scatter.8
  2179.7 51.1 reduce-scatter.12
  2234.6 51.1 reduce-scatter.14
  2289.7 87.1 reduce-scatter.18
  2380.8 87.1 reduce-scatter.20
  2472.1 86.8 reduce-scatter.22
where the time goes:
time: 2580 us; the launch traced here: 2570 us
  waiting for transfers between devices  1770 us (69%)
  matrix products  494 us (19%)
  local copies, waits for them, and re-layouts  124 us (5%)
  other arithmetic  114 us (4%)
  blocking collectives  43.8 us (2%)
    psum x1, waiting for transfers between devices, per_device(): feed = lax.psum(forward_mm(hidden, full_down), 'tp')  475 us
    psum x1, waiting for transfers between devices, per_device(): branch = lax.psum(forward_mm(gated, full_output), 'tp')  289 us
    dot_general x212, matrix products, einsum_high(): return jnp.einsum(formula, left_side, right_side, precision=HIGHEST)  281 us
    psum x1, waiting for transfers between devices, per_device(): lax.psum(through_transpose(grad_gate_low, back_gate) + through_transpose(...  274 us
    reduce_scatter x1, waiting for transfers between devices, per_device(): lax.psum_scatter(grad_w_up, ('fsdp', 'ctx'), scatter_dimension=0, tiled=T...  91.1 us
    reduce_scatter x1, waiting for transfers between devices, per_device(): lax.psum_scatter(grad_w_gate, ('fsdp', 'ctx'), scatter_dimension=0, tiled...  91.1 us
    reduce_scatter x1, waiting for transfers between devices, per_device(): lax.psum_scatter(grad_w_down, ('fsdp', 'ctx'), scatter_dimension=1, tiled...  90.9 us
    dot_general x8, matrix products, through_transpose(): lax.dot_general(left_side, right_side, (((1,), (1,)), ((), ())), preferre...  71.7 us
  transfers between devices with their start and end apart: 19, of which 17 were waited for; matrix products, arithmetic and copies ran while one was open for 14% of the time, Pallas kernels for 0%

commit v1 on v0

v1 whole, which is shorter than its diff:
```python
import functools

import jax
import jax.numpy as jnp
from jax import lax
from jax.experimental import pallas as pl
from jax.experimental.pallas import tpu as pltpu
from jax.sharding import PartitionSpec as P

HEAD_DIM = 128
EPSILON = 1e-05
F32 = jnp.float32
BF16 = jnp.bfloat16
BY_AXIS = pl.DeviceIdType.MESH
VMEM_BYTES = 62 * 1024 * 1024
ANY = pl.BlockSpec(memory_space=pl.ANY)
WHOLE = pl.BlockSpec(memory_space=pltpu.VMEM)


def dot(left, right, dims=((1,), (0,))):
    return lax.dot_general(left, right, (dims, ((), ())), preferred_element_type=F32)


NT = ((1,), (1,))
TN = ((0,), (0,))


def sigmoid(value):
    return 1.0 / (1.0 + jnp.exp(-value))


def slope(pre, sig):
    return sig * (1.0 + pre * (1.0 - sig))


def ones_times(ones, value):
    high = value.astype(BF16)
    rest = (value - high.astype(F32)).astype(BF16)
    return dot(ones, high) + dot(ones, rest)


def ring_place(index, size, folded):
    if folded:
        return index + (index // 2) * (1 - 2 * (index % 2))
    return index


class RingGather:
    def __init__(self, shards, outs, where, sems, size, folded):
        self.shards, self.outs, self.where, self.size = shards, outs, where, size
        self.ring_send, self.ring_recv, self.pair_send, self.pair_recv, self.local = sems
        self.place = ring_place(lax.axis_index("fsdp"), size, folded)
        self.folded = folded
        self.core = lax.axis_index("ctx") % 2
        self.pair = lax.axis_index("ctx") + 1 - 2 * self.core

    def device(self, place):
        return ring_place(lax.rem(place + 2 * self.size, self.size), self.size, self.folded)

    def peers(self):
        return [
            {"fsdp": self.device(self.place + 1)},
            {"fsdp": self.device(self.place - 1)},
            {"ctx": self.pair},
        ]

    def rows(self, i, core, way):
        quarter = self.shards[i].shape[0] // 4
        return pl.multiple_of((2 * core + way) * quarter, 16), quarter

    def in_shard(self, i, core, way):
        at, length = self.rows(i, core, way)
        return self.shards[i].at[pl.ds(at, length), :]

    def in_out(self, i, block, core, way):
        out, dim, column = self.where[i]
        at, length = self.rows(i, core, way)
        deep, wide = self.shards[i].shape
        if dim == 0:
            start = pl.multiple_of(block * deep + at, 16)
            return self.outs[out].at[pl.ds(start, length), pl.ds(column, wide)]
        start = pl.multiple_of(block * wide, 128)
        return self.outs[out].at[pl.ds(at, length), pl.ds(start, wide)]

    def own_block(self, i):
        out, dim, column = self.where[i]
        deep, wide = self.shards[i].shape
        block = self.device(self.place)
        if dim == 0:
            start = pl.multiple_of(block * deep, 16)
            return self.outs[out].at[pl.ds(start, deep), pl.ds(column, wide)]
        return self.outs[out].at[:, pl.ds(pl.multiple_of(block * wide, 128), wide)]

    def local_copy(self, i):
        return pltpu.make_async_copy(self.shards[i], self.own_block(i), self.local.at[i])

    def ring(self, i, way, step):
        sign = 1 - 2 * way
        block = self.device(self.place - sign * step)
        there = self.in_out(i, block, self.core, way)
        here = self.in_shard(i, self.core, way) if step == 0 else there
        at = (i * 2 + way) * (self.size - 1) + step
        return pltpu.make_async_remote_copy(
            src_ref=here,
            dst_ref=there,
            send_sem=self.ring_send.at[at],
            recv_sem=self.ring_recv.at[at],
            device_id={"fsdp": self.device(self.place + sign)},
            device_id_type=BY_AXIS,
        )

    def across(self, i, way, step, core):
        sign = 1 - 2 * way
        block = self.device(self.place - sign * (step + 1))
        piece = self.in_out(i, block, core, way)
        at = (i * 2 + way) * (self.size - 1) + step
        return pltpu.make_async_remote_copy(
            src_ref=piece,
            dst_ref=piece,
            send_sem=self.pair_send.at[at],
            recv_sem=self.pair_recv.at[at],
            device_id={"ctx": self.pair},
            device_id_type=BY_AXIS,
        )

    def each(self):
        return [(i, way) for i in range(len(self.shards)) for way in range(2)]

    def start(self):
        for i, way in self.each():
            self.ring(i, way, 0).start()
        for i in range(len(self.shards)):
            self.local_copy(i).start()

    def advance(self, step):
        for i, way in self.each():
            arrived = self.ring(i, way, step)
            arrived.wait_recv()
            if step + 1 < self.size - 1:
                self.ring(i, way, step + 1).start()
            self.across(i, way, step, self.core).start()

    def finish(self):
        for i, way in self.each():
            for step in range(self.size - 1):
                self.ring(i, way, step).wait_send()
                self.across(i, way, step, self.core).wait_send()
                self.across(i, way, step, 1 - self.core).wait_recv()
        for i in range(len(self.shards)):
            self.local_copy(i).wait()

    @staticmethod
    def scratch(count, size):
        copies = count * 2 * (size - 1)
        return [pltpu.SemaphoreType.DMA((copies,)) for _ in range(4)] + [
            pltpu.SemaphoreType.DMA((count,))
        ]


def meet(peers):
    barrier = pltpu.get_barrier_semaphore()
    total = 0
    for condition, peer in peers:
        if condition is None:
            pl.semaphore_signal(barrier, inc=1, device_id=peer, device_id_type=BY_AXIS)
            total = total + 1
        else:

            @pl.when(condition)
            def _():
                pl.semaphore_signal(barrier, inc=1, device_id=peer, device_id_type=BY_AXIS)

            total = total + condition.astype(jnp.int32)
    pl.semaphore_wait(barrier, total)


def gather_weights(shards, out_shapes, where, collective_id):
    size = lax.axis_size("fsdp")
    folded = size == 4
    count = len(shards)

    def kernel(*refs):
        ins, outs, sems = refs[:count], refs[count : count + len(out_shapes)], refs[-5:]
        job = RingGather(ins, outs, where, sems, size, folded)
        meet([(None, peer) for peer in job.peers()])
        job.start()
        for step in range(size - 1):
            job.advance(step)
        job.finish()

    return pl.pallas_call(
        kernel,
        out_shape=[jax.ShapeDtypeStruct(s, BF16) for s in out_shapes],
        in_specs=[WHOLE] * count,
        out_specs=[ANY] * len(out_shapes),
        scratch_shapes=RingGather.scratch(count, size),
        compiler_params=pltpu.CompilerParams(
            collective_id=collective_id, has_side_effects=True, vmem_limit_bytes=VMEM_BYTES
        ),
        name="gather_weights",
    )(*shards)


def line_sum(name, part, extras, extra_outs, epilogue, collective_id, chunk=32, gather=None):
    size = lax.axis_size("tp")
    rows, width = part.shape
    half = rows // 2
    chunk = min(chunk, half)
    count = half // chunk
    n_extra, n_extra_out = len(extras), len(extra_outs)
    if gather is None:
        shards, gathered, where = [], [], []
    else:
        shards, gathered, where = gather
    n_shards, n_gathered = len(shards), len(gathered)
    fsdp_size = lax.axis_size("fsdp")

    def kernel(*refs):
        refs = list(refs)

        def take(n):
            taken = refs[:n]
            del refs[:n]
            return taken

        (part_ref,) = take(1)
        extra_refs = take(n_extra)
        shard_refs = take(n_shards)
        (out_ref,) = take(1)
        extra_out_refs = take(n_extra_out)
        gathered_refs = take(n_gathered)
        came, gone, sum_send, sum_recv, back_send, back_recv = take(6)
        place = lax.axis_index("tp")
        first, last = place == 0, place == size - 1
        peers = [(jnp.logical_not(first), {"tp": place - 1}), (jnp.logical_not(last), {"tp": place + 1})]
        job = None
        if n_shards:
            job = RingGather(shard_refs, gathered_refs, where, take(5), fsdp_size, fsdp_size == 4)
            peers += [(None, peer) for peer in job.peers()]
        meet(peers)

        source = (first, last)
        owner = (last, first)
        ahead = (place + 1, place - 1)
        behind = (place - 1, place + 1)

        def at(way, k):
            start = k * chunk + (half if way == 0 else 0)
            return pl.ds(pl.multiple_of(start, chunk), chunk)

        def onward(way, k, from_part):
            source_ref = part_ref.at[at(way, k), :] if from_part else gone.at[way, k]
            return pltpu.make_async_remote_copy(
                src_ref=source_ref,
                dst_ref=came.at[way, k],
                send_sem=sum_send.at[way, k],
                recv_sem=sum_recv.at[way, k],
                device_id={"tp": ahead[way]},
                device_id_type=BY_AXIS,
            )

        def back(way, k):
            piece = out_ref.at[at(way, k), :]
            return pltpu.make_async_remote_copy(
                src_ref=piece,
                dst_ref=piece,
                send_sem=back_send.at[way, k],
                recv_sem=back_recv.at[way, k],
                device_id={"tp": behind[way]},
                device_id_type=BY_AXIS,
            )

        for way in range(2):

            @pl.when(source[way])
            def _():
                @pl.loop(0, count)
                def _(k):
                    onward(way, k, True).start()

        if job is not None:
            job.start()

        def add(k):
            for way in range(2):

                @pl.when(jnp.logical_not(source[way]))
                def _():
                    onward(way, k, False).wait_recv()
                    total = came[way, k].astype(F32) + part_ref[at(way, k), :].astype(F32)

                    @pl.when(owner[way])
                    def _():
                        start = pl.multiple_of(k * chunk, chunk)
                        out_ref[at(way, k), :] = epilogue(
                            extra_refs, extra_out_refs, at(way, k), pl.ds(start, chunk), total
                        )
                        back(way, k).start()

                    @pl.when(jnp.logical_not(owner[way]))
                    def _():
                        gone[way, k] = total.astype(BF16)
                        onward(way, k, False).start()

        def spread(k):
            for way in range(2):

                @pl.when(jnp.logical_not(owner[way]))
                def _():
                    back(way, k).wait_recv()

                    @pl.when(jnp.logical_not(source[way]))
                    def _():
                        back(way, k).start()

        steps = [add, spread]
        cuts = []
        if job is not None:
            cuts = [((2 * count - 2) * (i + 1)) // fsdp_size for i in range(fsdp_size - 1)]
        for number, step in enumerate(steps):
            low, high = number * count, (number + 1) * count
            edges = [low] + [c for c in cuts if low < c < high] + [high]
            for left, right in zip(edges[:-1], edges[1:]):
                if left in cuts:
                    job.advance(cuts.index(left))

                @pl.loop(left - low, right - low)
                def _(k):
                    step(k)

        if job is not None:
            job.finish()

        for way in range(2):

            @pl.when(jnp.logical_not(owner[way]))
            def _():
                @pl.loop(0, count)
                def _(k):
                    onward(way, k, False).wait_send()

            @pl.when(jnp.logical_not(source[way]))
            def _():
                @pl.loop(0, count)
                def _(k):
                    back(way, k).wait_send()

    scratch = [
        pltpu.VMEM((2, count, chunk, width), BF16),
        pltpu.VMEM((2, count, chunk, width), BF16),
    ] + [pltpu.SemaphoreType.DMA((2, count)) for _ in range(4)]
    if n_shards:
        scratch += RingGather.scratch(n_shards, fsdp_size)
    return pl.pallas_call(
        kernel,
        out_shape=[jax.ShapeDtypeStruct((rows, width), BF16)]
        + [jax.ShapeDtypeStruct(s, d) for s, d in extra_outs]
        + [jax.ShapeDtypeStruct(s, BF16) for s in gathered],
        in_specs=[WHOLE] * (1 + n_extra + n_shards),
        out_specs=[WHOLE] * (1 + n_extra_out) + [ANY] * n_gathered,
        scratch_shapes=scratch,
        compiler_params=pltpu.CompilerParams(
            collective_id=collective_id, has_side_effects=True, vmem_limit_bytes=VMEM_BYTES
        ),
        name=name,
    )(part, *extras, *shards)


def rms(value):
    return lax.rsqrt(jnp.mean(value * value, axis=-1, keepdims=True) + EPSILON)


def middle_rows(extra, extra_out, rows, own, total):
    x_ref, gain_ref = extra
    middle = x_ref[rows, :].astype(F32) + total
    extra_out[0][own, :] = middle
    return (middle * rms(middle) * gain_ref[...]).astype(BF16)


def norm_back(grad, value, gain):
    inverse = rms(value)
    scaled = value * inverse
    weighted = grad * gain
    back = inverse * (weighted - scaled * jnp.mean(weighted * scaled, axis=-1, keepdims=True))
    return back, jnp.sum(grad * scaled, axis=0, keepdims=True)


def grad_middle_rows(extra, extra_out, rows, own, total):
    middle_ref, grad_out_ref, gain_ref = extra
    back, gain_part = norm_back(total, middle_ref[own, :], gain_ref[...])
    grad_middle = grad_out_ref[rows, :].astype(F32) + back
    extra_out[0][own, :] = grad_middle
    add_rows(extra_out[1], own, gain_part)
    return grad_middle.astype(BF16)


def input_grad_rows(extra, extra_out, rows, own, total):
    x_ref, grad_middle_ref, gain_ref = extra
    back, gain_part = norm_back(total, x_ref[rows, :].astype(F32), gain_ref[...])
    add_rows(extra_out[0], own, gain_part)
    return (grad_middle_ref[own, :] + back).astype(BF16)


def add_rows(sum_ref, own, term):
    sum_ref[pl.ds(own.start // own.size, 1), :] = term


def lower_ones(length):
    at = lax.broadcasted_iota(jnp.int32, (length, length), 0)
    before = lax.broadcasted_iota(jnp.int32, (length, length), 1)
    return at >= before


def chunk_decay(forget, gap, live, lower):
    closing = sigmoid(-forget)
    opened = gap * closing
    remain = 1.0 - opened
    decay = jnp.where(live, jnp.log(remain), 0.0)
    keys = jnp.where(live, opened, 0.0)
    return closing, remain, keys, ones_times(lower, decay)


def rows_live(valid_ref, chunk_index, length):
    at = lax.broadcasted_iota(jnp.int32, (length, HEAD_DIM), 0) + chunk_index * length
    return at < valid_ref[0]


def span_end_kernel(heads, length, valid_ref, forget_ref, value_ref, gap_ref, end_ref):
    index = pl.program_id(0)

    @pl.when(index == 0)
    def _():
        end_ref[...] = jnp.zeros_like(end_ref)

    live = rows_live(valid_ref, index, length)
    lower = lower_ones(length).astype(BF16)
    for h in range(heads):
        cols = slice(h * HEAD_DIM, (h + 1) * HEAD_DIM)
        _, _, keys, cumulative = chunk_decay(forget_ref[:, cols], gap_ref[:, cols], live, lower)
        total = cumulative[length - 1 :, :]
        tail = (keys * jnp.exp(total - cumulative)).astype(BF16)
        end_ref[h] = jnp.exp(total) * end_ref[h] + dot(value_ref[:, cols].astype(BF16), tail, TN)


def mix_kernel(
    heads, length, valid_ref, query_ref, forget_ref, value_ref, gate_ref, gap_ref, gain_ref, start_ref,
    gated_ref, mixed_ref, states_ref, state_ref,
):
    index = pl.program_id(0)

    @pl.when(index == 0)
    def _():
        state_ref[...] = start_ref[...]

    live = rows_live(valid_ref, index, length)
    mask = lower_ones(length)
    lower = mask.astype(BF16)
    for h in range(heads):
        cols = slice(h * HEAD_DIM, (h + 1) * HEAD_DIM)
        _, _, keys, cumulative = chunk_decay(forget_ref[:, cols], gap_ref[:, cols], live, lower)
        pre = query_ref[:, cols]
        queries = (pre * sigmoid(pre) * jnp.exp(cumulative)).astype(BF16)
        shrunk = keys * jnp.exp(-cumulative)
        values = value_ref[:, cols].astype(BF16)
        state = state_ref[h]
        states_ref[0, h] = state
        scores = jnp.where(mask, dot(queries, shrunk.astype(BF16), NT), 0.0).astype(BF16)
        mixed = dot(scores, values) + dot(queries, state.astype(BF16), NT)
        mixed_ref[:, cols] = mixed
        growth = jnp.exp(cumulative[length - 1 :, :])
        state_ref[h] = growth * state + dot(values, (shrunk * growth).astype(BF16), TN)
        gate = gate_ref[:, cols]
        gated_ref[:, cols] = (mixed * rms(mixed) * gain_ref[...] * (gate * sigmoid(gate))).astype(BF16)


def span_begin_kernel(
    heads, length, valid_ref, grad_ref, mixed_ref, query_ref, forget_ref, gate_ref, gap_ref, gain_ref,
    grad_gate_ref, grad_mixed_ref, gain_part_ref, begin_ref,
):
    step = pl.program_id(0)
    index = pl.num_programs(0) - 1 - step

    @pl.when(step == 0)
    def _():
        begin_ref[...] = jnp.zeros_like(begin_ref)
        gain_part_ref[...] = jnp.zeros_like(gain_part_ref)

    live = rows_live(valid_ref, index, length)
    lower = lower_ones(length).astype(BF16)
    gain = gain_ref[...]
    for h in range(heads):
        cols = slice(h * HEAD_DIM, (h + 1) * HEAD_DIM)
        mixed = mixed_ref[:, cols]
        inverse = rms(mixed)
        scaled = mixed * inverse
        gate = gate_ref[:, cols]
        sig = sigmoid(gate)
        grad = grad_ref[:, cols].astype(F32)
        grad_gate_ref[:, cols] = (grad * scaled * gain * slope(gate, sig)).astype(BF16)
        grad_scaled = grad * (gate * sig)
        gain_part_ref[...] += jnp.sum(grad_scaled * scaled, axis=0, keepdims=True)
        weighted = grad_scaled * gain
        grad_mixed = inverse * (weighted - scaled * jnp.mean(weighted * scaled, axis=-1, keepdims=True))
        grad_mixed = grad_mixed.astype(BF16)
        grad_mixed_ref[:, cols] = grad_mixed
        _, _, _, cumulative = chunk_decay(forget_ref[:, cols], gap_ref[:, cols], live, lower)
        pre = query_ref[:, cols]
        queries = (pre * sigmoid(pre) * jnp.exp(cumulative)).astype(BF16)
        growth = jnp.exp(cumulative[length - 1 :, :])
        begin_ref[h] = growth * begin_ref[h] + dot(grad_mixed, queries, TN)


def mix_back_kernel(
    heads, length, valid_ref, grad_ref, query_ref, forget_ref, value_ref, gap_ref, states_ref, last_ref, end_ref,
    grad_query_ref, grad_forget_ref, grad_value_ref, gap_part_ref, flow_ref, after_ref,
):
    step = pl.program_id(0)
    index = pl.num_programs(0) - 1 - step

    @pl.when(step == 0)
    def _():
        flow_ref[...] = end_ref[...]
        after_ref[...] = last_ref[...]
        gap_part_ref[...] = jnp.zeros_like(gap_part_ref)

    live = rows_live(valid_ref, index, length)
    mask = lower_ones(length)
    lower = mask.astype(BF16)
    for h in range(heads):
        cols = slice(h * HEAD_DIM, (h + 1) * HEAD_DIM)
        gap = gap_ref[:, cols]
        closing, remain, keys, cumulative = chunk_decay(forget_ref[:, cols], gap, live, lower)
        pre = query_ref[:, cols]
        sig = sigmoid(pre)
        growth = jnp.exp(cumulative)
        shrink = jnp.exp(-cumulative)
        end_growth = growth[length - 1 :, :]
        queries = (pre * sig * growth).astype(BF16)
        shrunk_wide = keys * shrink
        shrunk = shrunk_wide.astype(BF16)
        tail = (shrunk_wide * end_growth).astype(BF16)
        values = value_ref[:, cols].astype(BF16)
        grad = grad_ref[:, cols]
        state = states_ref[0, h]
        flow = flow_ref[h]
        low_flow = flow.astype(BF16)
        scores = jnp.where(mask, dot(queries, shrunk, NT), 0.0).astype(BF16)
        grad_scores = jnp.where(mask, dot(grad, values, NT), 0.0).astype(BF16)
        to_queries = dot(grad, state.astype(BF16)) + dot(grad_scores, shrunk)
        to_keys = dot(grad_scores, queries, TN) + end_growth * dot(values, low_flow)
        grad_value_ref[:, cols] = (dot(scores, grad, TN) + dot(tail, low_flow, NT)).astype(BF16)
        grad_query_ref[:, cols] = (to_queries * growth * slope(pre, sig)).astype(BF16)
        terms = queries.astype(F32) * to_queries - shrunk.astype(F32) * to_keys
        high = terms.astype(BF16)
        rest = (terms - high.astype(F32)).astype(BF16)
        suffix = dot(lower, high, TN) + dot(lower, rest, TN)
        crossing = jnp.sum(flow * after_ref[h], axis=0, keepdims=True)
        pressure = jnp.where(live, to_keys * shrink - (suffix + crossing) / remain, 0.0)
        gap_part_ref[:, cols] += jnp.sum(closing * pressure, axis=0, keepdims=True)
        grad_forget_ref[:, cols] = (-closing * (1.0 - closing) * gap * pressure).astype(BF16)
        flow_ref[h] = end_growth * flow + dot(grad, queries, TN)
        after_ref[h] = state


def plain_call(kernel, name, grid, in_specs, out_specs, out_shape, scratch, flops, moved):
    return pl.pallas_call(
        kernel,
        grid_spec=pltpu.PrefetchScalarGridSpec(
            num_scalar_prefetch=1, grid=grid, in_specs=in_specs, out_specs=out_specs, scratch_shapes=scratch
        ),
        out_shape=out_shape,
        compiler_params=pltpu.CompilerParams(
            dimension_semantics=("arbitrary",), vmem_limit_bytes=VMEM_BYTES
        ),
        cost_estimate=pl.CostEstimate(flops=flops, bytes_accessed=moved, transcendentals=flops // 64),
        name=name,
    )


def combine(earlier, later):
    return (earlier[0] * later[0], later[0][:, None, :] * earlier[1] + later[1])


def from_earlier(state, decay, axis):
    size = lax.axis_size(axis)
    if size == 2:
        return lax.ppermute(state, axis, [(0, 1)])
    mine = lax.axis_index(axis)
    states, decays = lax.all_gather(state, axis), lax.all_gather(decay, axis)
    total = jnp.zeros_like(state)
    for k in range(size):
        new = decays[k][:, None, :] * total + states[k]
        total = jnp.where(k < mine, new, total)
    return total


def from_later(state, decay, axis):
    size = lax.axis_size(axis)
    if size == 2:
        return lax.ppermute(state, axis, [(1, 0)])
    mine = lax.axis_index(axis)
    states, decays = lax.all_gather(state, axis), lax.all_gather(decay, axis)
    total = jnp.zeros_like(state)
    for k in reversed(range(size)):
        new = decays[k][:, None, :] * total + states[k]
        total = jnp.where(k > mine, new, total)
    return total


def per_device(
    inputs, lengths, w_query, w_forget, w_input, w_outgate, w_output, w_gate, w_up, w_down,
    norm_gain, ffn_gain, head_gain, forget_gap, cotangent,
):
    groups, span, width = inputs.shape
    rows = groups * span
    fsdp, ctx, tp = lax.axis_size("fsdp"), lax.axis_size("ctx"), lax.axis_size("tp")
    local = forget_gap.shape[0]
    heads = local // HEAD_DIM
    ff = w_gate.shape[1]
    length = min(128, span)
    chunks = span // length
    place = lax.axis_index("tp")
    half = rows // 2

    valid = jnp.clip(lengths - lax.axis_index("ctx") * span, 0, span).astype(jnp.int32)
    keep = (jnp.arange(rows, dtype=jnp.int32) < valid[0])[:, None]
    x = inputs.reshape(rows, width)
    grad_low = jnp.where(keep, cotangent.reshape(rows, width), jnp.zeros((), BF16))
    gap = forget_gap.reshape(1, local)
    head_row = head_gain.reshape(1, HEAD_DIM)

    w_four, w_out = gather_weights(
        [w_query, w_forget, w_input, w_outgate, w_output],
        [(fsdp * w_query.shape[0], 4 * local), (local, width)],
        [(0, 0, 0), (0, 0, local), (0, 0, 2 * local), (0, 0, 3 * local), (1, 1, 0)],
        1,
    )

    wide = x.astype(F32)
    normed = (wide * rms(wide) * norm_gain).astype(BF16)
    pre = dot(normed, w_four)

    def column(j):
        return pl.BlockSpec((length, local), lambda i, *_: (i, j))

    def column_back(j):
        return pl.BlockSpec((length, local), lambda i, *_: (chunks - 1 - i, j))

    fixed = lambda shape: pl.BlockSpec(shape, lambda i, *_: (0,) * len(shape))
    state_shape = (heads, HEAD_DIM, HEAD_DIM)
    work = 2 * rows * local * HEAD_DIM
    moved = rows * local * 4

    local_end = plain_call(
        functools.partial(span_end_kernel, heads, length), "span_end", (chunks,),
        [column(1), column(2), fixed((1, local))], fixed(state_shape),
        jax.ShapeDtypeStruct(state_shape, F32), [], 3 * work, 2 * moved,
    )(valid, pre, pre, gap)
    span_decay = None
    if ctx > 2:
        keep_rows = keep.astype(F32)
        closing = jax.nn.sigmoid(-pre[:, local : 2 * local])
        logs = jnp.log(1.0 - gap * closing) * keep_rows
        span_decay = jnp.exp(jnp.sum(logs, axis=0)).reshape(heads, HEAD_DIM)
    start = from_earlier(local_end, span_decay, "ctx")
    gated, mixed, states = plain_call(
        functools.partial(mix_kernel, heads, length), "mix", (chunks,),
        [column(0), column(1), column(2), column(3), fixed((1, local)), fixed((1, HEAD_DIM)), fixed(state_shape)],
        [column(0), column(0), pl.BlockSpec((1,) + state_shape, lambda i, *_: (i, 0, 0, 0))],
        [
            jax.ShapeDtypeStruct((rows, local), BF16),
            jax.ShapeDtypeStruct((rows, local), F32),
            jax.ShapeDtypeStruct((chunks,) + state_shape, F32),
        ],
        [pltpu.VMEM(state_shape, F32)], 6 * work, 6 * moved,
    )(valid, pre, pre, pre, pre, gap, head_row, start)
    if ctx == 2:
        keep_rows = keep.astype(F32)
        closing = jax.nn.sigmoid(-pre[:, local : 2 * local])
        logs = jnp.log(1.0 - gap * closing) * keep_rows
        span_decay = jnp.exp(jnp.sum(logs, axis=0)).reshape(heads, HEAD_DIM)
    state_end = local_end + span_decay[:, None, :] * start

    branch = dot(gated, w_out).astype(BF16)
    normed_two, middle, w_both, w_back = line_sum(
        "sum_branch", branch, [x, ffn_gain.reshape(1, width)], [((half, width), F32)], middle_rows, 2,
        gather=(
            [w_gate, w_up, w_down],
            [(fsdp * w_gate.shape[0], 2 * ff), (ff, width)],
            [(0, 0, 0), (0, 0, ff), (1, 1, 0)],
        ),
    )

    both = dot(normed_two, w_both)
    gate_hidden, up_hidden = both[:, :ff], both[:, ff:]
    sig = jax.nn.sigmoid(gate_hidden)
    act = gate_hidden * sig
    hidden = (act * up_hidden).astype(BF16)
    mine = jnp.concatenate(
        [jnp.where(place == 0, middle, 0.0), jnp.where(place == tp - 1, middle, 0.0)], axis=0
    )
    feed = (dot(hidden, w_back) + mine).astype(BF16)
    result = lax.psum(feed, "tp").reshape(groups, span, width)

    grad_hidden = dot(grad_low, w_back, NT)
    grad_gate = (grad_hidden * up_hidden * slope(gate_hidden, sig)).astype(BF16)
    grad_up = (grad_hidden * act).astype(BF16)
    grad_both = jnp.concatenate([grad_gate, grad_up], axis=1)
    part_two = dot(grad_both, w_both, NT).astype(BF16)
    grad_branch, grad_middle, ffn_gain_part = line_sum(
        "sum_norm_two", part_two, [middle, grad_low, ffn_gain.reshape(1, width)],
        [((half, width), F32), ((half // min(32, half), width), F32)], grad_middle_rows, 3,
    )
    grad_w_down = dot(hidden, grad_low, TN).astype(BF16)
    grad_w_both = dot(normed_two, grad_both, TN).astype(BF16)

    grad_gated = dot(grad_branch, w_out, NT)
    grad_outgate, grad_mixed, head_part, local_begin = plain_call(
        functools.partial(span_begin_kernel, heads, length), "span_begin", (chunks,),
        [column_back(0), column_back(0), column_back(0), column_back(1), column_back(3), fixed((1, local)),
         fixed((1, HEAD_DIM))],
        [column_back(0), column_back(0), fixed((1, HEAD_DIM)), fixed(state_shape)],
        [
            jax.ShapeDtypeStruct((rows, local), BF16),
            jax.ShapeDtypeStruct((rows, local), BF16),
            jax.ShapeDtypeStruct((1, HEAD_DIM), F32),
            jax.ShapeDtypeStruct(state_shape, F32),
        ],
        [], 3 * work, 6 * moved,
    )(valid, grad_gated, mixed, pre, pre, pre, gap, head_row)
    grad_end = from_later(local_begin, span_decay, "ctx")
    grad_query, grad_forget, grad_value, gap_part = plain_call(
        functools.partial(mix_back_kernel, heads, length), "mix_back", (chunks,),
        [column_back(0), column_back(0), column_back(1), column_back(2), fixed((1, local)),
         pl.BlockSpec((1,) + state_shape, lambda i, *_: (chunks - 1 - i, 0, 0, 0)), fixed(state_shape),
         fixed(state_shape)],
        [column_back(0), column_back(0), column_back(0), fixed((1, local))],
        [jax.ShapeDtypeStruct((rows, local), BF16)] * 3 + [jax.ShapeDtypeStruct((1, local), F32)],
        [pltpu.VMEM(state_shape, F32), pltpu.VMEM(state_shape, F32)], 12 * work, 6 * moved,
    )(valid, grad_mixed, pre, pre, pre, gap, states, state_end, grad_end)

    grad_four = jnp.concatenate([grad_query, grad_forget, grad_value, grad_outgate], axis=1)
    part_one = dot(grad_four, w_four, NT).astype(BF16)
    input_grad, norm_gain_part = line_sum(
        "sum_norm_one", part_one, [x, grad_middle, norm_gain.reshape(1, width)],
        [((half // min(32, half), width), F32)], input_grad_rows, 4,
    )
    input_grad = input_grad.reshape(groups, span, width)
    grad_w_output = dot(gated, grad_branch, TN).astype(BF16)
    grad_w_four = dot(normed, grad_four, TN).astype(BF16)

    both_axes = ("fsdp", "ctx")

    def scatter(grad, dim):
        return lax.psum_scatter(grad, both_axes, scatter_dimension=dim, tiled=True).astype(F32)

    out_down = scatter(grad_w_down, 1)
    out_both = scatter(grad_w_both, 0)
    out_output = scatter(grad_w_output, 1)
    out_four = scatter(grad_w_four, 0)

    owner = jnp.logical_or(place == 0, place == tp - 1)
    sums = jnp.concatenate(
        [
            jnp.where(owner, jnp.sum(norm_gain_part, axis=0), 0.0),
            jnp.where(owner, jnp.sum(ffn_gain_part, axis=0), 0.0),
            head_part[0],
            lax.dynamic_update_slice(jnp.zeros((tp * local,), F32), gap_part[0], (place * local,)),
        ]
    )
    sums = lax.psum(sums, ("fsdp", "ctx", "tp"))
    grad_norm_gain, grad_ffn_gain = sums[:width], sums[width : 2 * width]
    grad_head_gain = sums[2 * width : 2 * width + HEAD_DIM]
    grad_gap = lax.dynamic_slice(sums, (2 * width + HEAD_DIM + place * local,), (local,))
    return (
        result,
        input_grad,
        out_four[:, :local],
        out_four[:, local : 2 * local],
        out_four[:, 2 * local : 3 * local],
        out_four[:, 3 * local :],
        out_output,
        out_both[:, :ff],
        out_both[:, ff:],
        out_down,
        grad_norm_gain,
        grad_ffn_gain,
        grad_head_gain,
        grad_gap,
    )


def solution(mesh):
    tokens = P("fsdp", "ctx", None)
    inward, outward = P("fsdp", "tp"), P("tp", "fsdp")
    grad_in, grad_back = P(("fsdp", "ctx"), "tp"), P("tp", ("fsdp", "ctx"))
    return jax.shard_map(
        per_device,
        mesh=mesh,
        in_specs=(tokens, P("fsdp")) + (inward,) * 4 + (outward, inward, inward, outward)
        + (P(), P(), P(), P("tp"), tokens),
        out_specs=(tokens, tokens) + (grad_in,) * 4 + (grad_back, grad_in, grad_in, grad_back)
        + (P(), P(), P(), P("tp")),
        check_vma=False,
    )
```

time: 2580 us -> 1300 us (0.50)
  waiting for transfers between devices: 1770 us -> 1.45 us
  Pallas kernels: 0 us -> 1030 us
  matrix products: 494 us -> 146 us
  local copies, waits for them, and re-layouts: 124 us -> 27.5 us
  other arithmetic: 114 us -> 19.4 us
    psum x3 -> x1, waiting for transfers between devices: 1040 us -> 0.01 us  [per_device(): result = lax.psum(feed, 'tp').reshape(groups, span, width)]
    pallas_call x0 -> x8, Pallas kernels: none -> 1030 us  [the longest x3 930 us: line_sum(): pl.pallas_call(kernel, out_shape=[jax.ShapeDtypeStruct((rows, width), BF1...]
    reduce_scatter x8 -> x4, waiting for transfers between devices: 498 us -> 0.01 us  [scatter(): lax.psum_scatter(grad, both_axes, scatter_dimension=dim, tiled=True)]
    dot_general x236 -> x12, matrix products: 494 us -> 146 us  [dot(): lax.dot_general(left, right, (dims, ((), ())), preferred_element_type=F32)]
    all_gather x8 -> x0, waiting for transfers between devices: 229 us -> none  [the longest x1 55.7 us: per_device(): lax.all_gather(w_down, 'fsdp', axis=1, tiled=True)]
    squeeze x32 -> x0, local copies, waits for them, and re-layouts: 29.4 us -> none  [per_device(): lax.scan(forward_block, zero_state, (to_blocks(query_tok), to_blocks(key_...]
  transfers between devices with their start and end apart: 19 -> 7, of which waited for: 17 -> 1; matrix products, arithmetic and copies ran while one was open for 14% -> 8% of each run, Pallas kernels for 0% -> 30%
where the time goes in v1:
time: 1300 us; the launch traced here: 1290 us
  Pallas kernels  1030 us (79%)
  matrix products  146 us (11%)
  blocking collectives  48.2 us (4%)
  local copies, waits for them, and re-layouts  27.5 us (2%)
  other arithmetic  19.4 us (1%)
  between operations  16.6 us (1%)
    pallas_call x3, Pallas kernels, line_sum(): pl.pallas_call(kernel, out_shape=[jax.ShapeDtypeStruct((rows, width), BF1...  930 us
    dot_general x12, matrix products, dot(): lax.dot_general(left, right, (dims, ((), ())), preferred_element_type=F32)  146 us
    pallas_call x1, Pallas kernels, gather_weights(): pl.pallas_call(kernel, out_shape=[jax.ShapeDtypeStruct(s, BF16) for s in...  51.5 us
    psum x1, blocking collectives, per_device(): sums = lax.psum(sums, ('fsdp', 'ctx', 'tp'))  48.2 us
  transfers between devices with their start and end apart: 7, of which 1 were waited for; matrix products, arithmetic and copies ran while one was open for 8% of the time, Pallas kernels for 30%

profile of v1, /device:TPU:0, one launch (start us, length us, event | category | flops | bytes accessed | tf_op | source)
XLA Modules:
  0.0 1294.0 jit_solution(16184868071069870508)
XLA Ops:
  8.1 3.1 fusion
  11.8 51.5 %gather_weights.1 = (bf16[2048,2048]{1,0:T(8,128)(2,1)}, bf16[512,2048]{1,0:T(8,128)(2,1)}) custom-call(bf16[512,512]{1,0:T(8,128)(2,1)} %refs_0_.1, bf16[512,512]{1,0:T(8,128)(2,1)} %refs_1_.1, bf16[512,512]{1,0:T(8,128)(2,1)} %refs_2_.1, bf16[512,512]{1,0:T(8,128)(2,1)} %refs_3_.2, bf16[512,512]{1,0:T(8,128)(2,1)} %refs_4_.2), custom_call_target="tpu_custom_call" | custom-call | tf_op jit(solution)/shard_map/gather_weights/pallas_call | solution.py:191
  63.3 14.6 %fusion.14.forget_ref.value_ref.query_ref.gate_ref = f32[1024,2048]{1,0:T(8,128)} fusion(bf16[2048,2048]{1,0:T(8,128)(2,1)} %get-tuple-element.36, f32[2048]{0:T(1024)S(1)} %copy-done.11, f32[1024]{0:T(1024)S(1)} %add_rsqrt_fusion, bf16[1,1024,2048]{2,1,0:T(8,128)(2,1)} %param.15), kind=kOutput, calls=%fused_computation.32 | convolution fusion | flops 8598323200 | bytes 20983808 | tf_op jit(solution)/shard_map/dot_general | solution.py:21
  77.9 9.6 span_end.1
  87.5 2.3 collective-permute-start
  89.8 4.6 bitcast_select_fusion.refs_2_
  94.4 0.7 copy-done.4
  95.1 12.4 mix.1
  107.5 6.3 convolution_convert_fusion.5.refs_0_
  113.8 286.2 %sum_branch.1 = (bf16[1024,2048]{1,0:T(8,128)(2,1)}, f32[512,2048]{1,0:T(8,128)}, bf16[2048,2816]{1,0:T(8,128)(2,1)}, bf16[1408,2048]{1,0:T(8,128)(2,1)}) custom-call(bf16[1024,2048]{1,0:T(8,128)(2,1)} %convolution_convert_fusion.5.refs_0_, bf16[1024,2048]{1,0:T(8,128)(2,1)} %bitcast.45, f32[1,2048]{1,0:T(1,128)} %bitcast.48, bf16[512,1408]{1,0:T(8,128)(2,1)} %refs_3_.3, ...), custom_call_target="tpu_custom_call" | custom-call | tf_op jit(solution)/shard_map/sum_branch/pallas_call | solution.py:354
  400.0 18.8 %fusion.24 = f32[1024,2816]{1,0:T(8,128)} fusion(bf16[1024,2048]{1,0:T(8,128)(2,1)} %get-tuple-element.39, bf16[2048,2816]{1,0:T(8,128)(2,1)} %get-tuple-element.40), kind=kOutput, calls=%fused_computation.52 | convolution fusion | flops 11811160064 | bytes 27262976 | tf_op jit(solution)/shard_map/dot_general | solution.py:21
  418.9 13.5 %multiply_convert_fusion.1 = (bf16[1024,1408]{1,0:T(8,128)(2,1)}, bf16[1024,1408]{1,0:T(8,128)(2,1)}, bf16[1024,1408]{1,0:T(8,128)(2,1)}) fusion(f32[1024,2816]{1,0:T(8,128)} %fusion.24, bf16[1024,2048]{1,0:T(8,128)(2,1)S(1)} %copy-done.1, bf16[1408,2048]{1,0:T(8,128)(2,1)S(1)} %copy-done.14), kind=kOutput, calls=%fused_computation.12 | convolution fusion | flops 5927206912 | bytes 30146560 | tf_op jit(solution)/shard_map/dot_general | solution.py:21
  432.4 18.0 %convolution_convert_fusion.3.refs_0_ = bf16[1024,2048]{1,0:T(8,128)(2,1)} fusion(bf16[2048,2816]{1,0:T(8,128)(2,1)} %get-tuple-element.40, bf16[1024,1408]{1,0:T(8,128)(2,1)} %get-tuple-element.59, bf16[1024,1408]{1,0:T(8,128)(2,1)} %get-tuple-element.58), kind=kOutput, calls=%fused_computation.18 | convolution fusion | flops 11824791552 | bytes 21495808 | tf_op jit(solution)/shard_map/dot_general | solution.py:21
  450.3 278.5 %sum_norm_two.1 = (bf16[1024,2048]{1,0:T(8,128)(2,1)}, f32[512,2048]{1,0:T(8,128)}, f32[16,2048]{1,0:T(8,128)}) custom-call(bf16[1024,2048]{1,0:T(8,128)(2,1)} %convolution_convert_fusion.3.refs_0_, f32[512,2048]{1,0:T(8,128)} %get-tuple-element.42.refs_1_, bf16[1024,2048]{1,0:T(8,128)(2,1)} %bitcast_select_fusion.refs_2_, f32[1,2048]{1,0:T(1,128)} %bitcast.49), custom_call_target="tpu_custom_call" | custom-call | tf_op jit(solution)/shard_map/sum_norm_two/pallas_call | solution.py:354
  728.9 6.0 convolution_convert_fusion.6
  734.9 10.4 convolution_convert_fusion.1
  745.4 0.6 copy-done.10
  746.0 2.6 fusion.12
  748.6 6.7 fusion.25.grad_ref
  755.3 11.0 span_begin.1
  766.3 1.5 collective-permute-start.1
  767.8 0.7 multiply_add_fusion.last_ref
  768.6 1.4 collective-permute-done.1.end_ref
  769.9 0.7 copy-done.16
  770.6 17.0 %mix_back.1 = (bf16[1024,512]{1,0:T(8,128)(2,1)}, bf16[1024,512]{1,0:T(8,128)(2,1)}, bf16[1024,512]{1,0:T(8,128)(2,1)}, f32[1,512]{1,0:T(1,128)}) custom-call(s32[1]{0:T(128)} %min.6.valid_ref, bf16[1024,512]{1,0:T(8,128)(2,1)} %get-tuple-element.45.grad_ref, f32[1024,2048]{1,0:T(8,128)} %fusion.14.forget_ref.value_ref.query_ref.gate_ref, ...), custom_call_target="tpu_custom_call" | custom-call | flops 1610612736 | bytes 12582912 | tf_op jit(solution)/shard_map/mix_back/pallas_call | solution.py:732
  787.7 1.5 constant_dynamic-update-slice_fusion.3
  789.2 2.7 constant_dynamic-update-slice_fusion.2
  792.3 2.0 copy-done.8
  794.3 11.8 convolution_convert_fusion.2
  806.2 1.9 copy-done.18
  808.0 17.4 %convolution_convert_fusion = bf16[2048,2816]{1,0:T(8,128)(2,1)} fusion(bf16[1024,2048]{1,0:T(8,128)(2,1)} %get-tuple-element.39, bf16[1024,1408]{1,0:T(8,128)(2,1)} %get-tuple-element.59, bf16[1024,1408]{1,0:T(8,128)(2,1)S(1)} %copy-done.18), kind=kOutput, calls=%fused_computation | convolution fusion | flops 11828461568 | bytes 21495808 | tf_op jit(solution)/shard_map/dot_general | solution.py:21
  825.9 3.4 broadcast_select_fusion.1
  829.5 1.1 copy-done.17
  830.6 8.2 fusion.5
  838.8 0.9 copy-done.9
  839.7 14.0 %convolution_convert_fusion.4.refs_0_ = bf16[1024,2048]{1,0:T(8,128)(2,1)} fusion(bf16[1024,2048]{1,0:T(8,128)(2,1)} %copy-done.8, bf16[2048,2048]{1,0:T(8,128)(2,1)} %get-tuple-element.36), kind=kOutput, calls=%fused_computation.19 | convolution fusion | flops 8592031744 | bytes 16777216 | tf_op jit(solution)/shard_map/dot_general | solution.py:21
  853.7 364.8 %sum_norm_one.1 = (bf16[1024,2048]{1,0:T(8,128)(2,1)}, f32[16,2048]{1,0:T(8,128)}) custom-call(bf16[1024,2048]{1,0:T(8,128)(2,1)} %convolution_convert_fusion.4.refs_0_, bf16[1024,2048]{1,0:T(8,128)(2,1)} %bitcast.46, f32[512,2048]{1,0:T(8,128)} %get-tuple-element.52.refs_2_, f32[1,2048]{1,0:T(1,128)} %bitcast.54), custom_call_target="tpu_custom_call" | custom-call | tf_op jit(solution)/shard_map/sum_norm_one/pallas_call | solution.py:354
  1218.5 0.9 reduce_sum.38
  1219.7 48.2 %psum.15 = f32[6272]{0:T(1024)S(1)} all-reduce(f32[6272]{0:T(1024)S(1)} %pad_maximum_fusion.3), channel_id=1, replica_groups=mesh['fsdp'=4,'ctx'=2,'tp'=4] {'fsdp','ctx','tp'}, use_global_device_ids=true, to_apply=%region_9.10 | all-reduce | flops 6272 | bytes 50176 | tf_op jit(solution)/shard_map/psum | solution.py:771
  1267.9 0.5 slice.59
  1268.4 0.7 dynamic_slice.3
  1269.1 0.6 fusion.23
  1269.7 1.8 convert_element_type.72
  1271.5 2.3 convert_element_type.76
  1273.8 2.6 fusion.22
  1276.4 3.1 fusion.21
  1279.5 4.9 copy.36
  1284.4 2.0 copy.37
  (63 shorter events, 1.5 us)
Async XLA Ops:
  8.0 55.3 %copy-start.11 = (f32[2048]{0:T(1024)S(1)}, f32[2048]{0:T(1024)}, u32[]{:S(2)}) copy-start(f32[2048]{0:T(1024)} %param.25) | copy-start | bytes 24580
  8.0 1261.7 %reduce-scatter.7.cloned.1.call-start = ((), (), s32[]{:S(2)}) async-start(), calls=%async_computation.6 | async-start | bytes 2359296 | tf_op jit(solution)/shard_map/reduce_scatter | solution.py:755
  87.5 6.9 collective-permute-start
  94.4 0.7 copy-start.4
  400.0 18.8 %copy-start.1 = (bf16[1024,2048]{1,0:T(8,128)(2,1)S(1)}, bf16[1024,2048]{1,0:T(8,128)(2,1)}, u32[]{:S(2)}) copy-start(bf16[1024,2048]{1,0:T(8,128)(2,1)} %bitcast_select_fusion.refs_2_) | copy-start | bytes 12582916
  400.0 18.8 %copy-start.14 = (bf16[1408,2048]{1,0:T(8,128)(2,1)S(1)}, bf16[1408,2048]{1,0:T(8,128)(2,1)}, u32[]{:S(2)}) copy-start(bf16[1408,2048]{1,0:T(8,128)(2,1)} %get-tuple-element.41) | copy-start | bytes 17301508
  450.3 278.5 %copy-start.15 = (bf16[1024,512]{1,0:T(8,128)(2,1)S(1)}, bf16[1024,512]{1,0:T(8,128)(2,1)}, u32[]{:S(2)}) copy-start(bf16[1024,512]{1,0:T(8,128)(2,1)} %get-tuple-element.37) | copy-start | bytes 3145732
  734.9 536.6 %reduce-scatter.11.cloned.1.call-start = ((), (), s32[]{:S(2)}) async-start(), calls=%async_computation.8 | async-start | bytes 6488064 | tf_op jit(solution)/shard_map/reduce_scatter | solution.py:755
  745.4 0.7 copy-start.10
  745.4 528.4 %reduce-scatter.5.cloned.1.call-start = ((), (), s32[]{:S(2)}) async-start(), calls=%async_computation.5 | async-start | bytes 9437184 | tf_op jit(solution)/shard_map/reduce_scatter | solution.py:755
  755.3 12.5 copy-start.3
  755.3 12.5 copy-start.5
  766.3 3.6 collective-permute-start.1
  769.9 0.7 copy-start.16
  787.6 4.3 copy-start.7
  787.7 4.4 copy-start.6
  787.7 6.6 copy-start
  792.3 2.0 copy-start.8
  806.1 2.0 copy-start.18
  806.1 470.3 %reduce-scatter.9.cloned.1.call-start = ((), (), s32[]{:S(2)}) async-start(), calls=%async_computation.7 | async-start | bytes 12976128 | tf_op jit(solution)/shard_map/reduce_scatter | solution.py:755
  825.5 3.7 slice-start
  825.5 454.0 %all-reduce.2.cloned.1.call-start = ((), (), s32[]{:S(2)}) async-start(), calls=%async_computation.4 | async-start | bytes 8388608 | tf_op jit(solution)/shard_map/psum | solution.py:703
  825.8 3.7 slice-start.1
  825.8 4.8 copy-start.17
  838.8 0.9 copy-start.9
  853.7 365.7 %copy-start.12 = (f32[1,512]{1,0:T(1,128)S(1)}, f32[1,512]{1,0:T(1,128)}, u32[]{:S(2)}) copy-start(f32[1,512]{1,0:T(1,128)} %get-tuple-element.57) | copy-start | bytes 6148
  853.7 366.0 %copy-start.13 = (f32[1,128]{1,0:T(1,128)S(1)}, f32[1,128]{1,0:T(1,128)}, u32[]{:S(2)}) copy-start(f32[1,128]{1,0:T(1,128)} %get-tuple-element.56) | copy-start | bytes 1540
  1279.5 4.9 copy-start.2
Sparse Core Ops, SparseCore 0:
  735.0 43.6 reduce-scatter.6
  782.1 58.8 reduce-scatter.10
  844.5 71.5 reduce-scatter.4
  919.4 87.1 reduce-scatter.8
Sparse Core Ops, SparseCore 1:
  838.9 224.3 all-reduce.1

commit v2 on v1

--- a/solution.py
+++ b/solution.py
@@ -157,6 +157,132 @@
         ]
 
 
+class RingScatter:
+    def __init__(self, grads, outs, dims, scratch, sems, size, folded):
+        self.grads, self.outs, self.dims, self.size, self.folded = grads, outs, dims, size, folded
+        count = len(grads)
+        self.own, self.came, self.passed = scratch[:count], scratch[count : 2 * count], scratch[2 * count :]
+        self.pair_send, self.pair_recv, self.local, self.ring_send, self.ring_recv = sems
+        self.place = ring_place(lax.axis_index("fsdp"), size, folded)
+        self.core = lax.axis_index("ctx")
+
+    device = RingGather.device
+
+    def peers(self):
+        return [
+            {"fsdp": self.device(self.place + 1)},
+            {"fsdp": self.device(self.place - 1)},
+            {"ctx": 1 - self.core},
+        ]
+
+    def block(self, i, offset, core):
+        index = self.device(self.place + offset) * 2 + core
+        extent = self.outs[i].shape[self.dims[i]]
+        start = pl.multiple_of(index * extent, extent)
+        if self.dims[i] == 0:
+            return self.grads[i].at[pl.ds(start, extent), :]
+        return self.grads[i].at[:, pl.ds(start, extent)]
+
+    def local_copy(self, i, offset):
+        return pltpu.make_async_copy(
+            self.block(i, offset, self.core), self.own[i].at[offset], self.local.at[i * self.size + offset]
+        )
+
+    def across(self, i, offset):
+        at = i * self.size + offset
+        return pltpu.make_async_remote_copy(
+            src_ref=self.block(i, offset, 1 - self.core),
+            dst_ref=self.came[i].at[offset],
+            send_sem=self.pair_send.at[at],
+            recv_sem=self.pair_recv.at[at],
+            device_id={"ctx": 1 - self.core},
+            device_id_type=BY_AXIS,
+        )
+
+    def offset(self, way, step):
+        return (-(step + 1) if way == 0 else step + 1) % self.size
+
+    def ring(self, i, way, step):
+        half = self.outs[i].shape[0] // 2
+        at = (i * 2 + way) * (self.size - 1) + step
+        return pltpu.make_async_remote_copy(
+            src_ref=self.came[i].at[self.offset(way, step), pl.ds(way * half, half), :],
+            dst_ref=self.passed[i].at[way, step],
+            send_sem=self.ring_send.at[at],
+            recv_sem=self.ring_recv.at[at],
+            device_id={"fsdp": self.device(self.place + 1 - 2 * way)},
+            device_id_type=BY_AXIS,
+        )
+
+    def order(self):
+        used = []
+        for step in range(self.size):
+            for way in range(2):
+                if self.offset(way, step) not in used:
+                    used.append(self.offset(way, step))
+        return used
+
+    def start(self):
+        for offset in self.order():
+            for i in range(len(self.grads)):
+                self.across(i, offset).start()
+                self.local_copy(i, offset).start()
+
+    def advance(self, step):
+        before = {self.offset(way, s) for s in range(step) for way in range(2)}
+        fresh = {self.offset(way, step) for way in range(2)} - before
+        for i in range(len(self.grads)):
+            for offset in sorted(fresh):
+                self.across(i, offset).wait_recv()
+                self.local_copy(i, offset).wait()
+            for way in range(2):
+                if step > 0:
+                    self.ring(i, way, step - 1).wait_recv()
+                self.add(i, way, step)
+                if step < self.size - 1:
+                    self.ring(i, way, step).start()
+
+    def add(self, i, way, step):
+        half = self.outs[i].shape[0] // 2
+        offset = self.offset(way, step)
+        own, came, passed, out = self.own[i], self.came[i], self.passed[i], self.outs[i]
+
+        @pl.loop(0, half // 16)
+        def _(r):
+            rows = pl.ds(pl.multiple_of(way * half + r * 16, 16), 16)
+            total = own[offset, rows, :].astype(F32) + came[offset, rows, :].astype(F32)
+            if step > 0:
+                total += passed[way, step - 1, pl.ds(pl.multiple_of(r * 16, 16), 16), :].astype(F32)
+            if step < self.size - 1:
+                came[offset, rows, :] = total.astype(BF16)
+            else:
+                out[rows, :] = total
+
+    def finish(self):
+        for i in range(len(self.grads)):
+            for offset in range(self.size):
+                self.across(i, offset).wait_send()
+            for way in range(2):
+                for step in range(self.size - 1):
+                    self.ring(i, way, step).wait_send()
+
+    @staticmethod
+    def out_shape(grad, dim, size):
+        deep, wide = grad.shape
+        return (deep // (2 * size), wide) if dim == 0 else (deep, wide // (2 * size))
+
+    @staticmethod
+    def buffers(shapes, size):
+        full = [pltpu.VMEM((size,) + s, BF16) for s in shapes]
+        return full + full + [pltpu.VMEM((2, size - 1, s[0] // 2, s[1]), BF16) for s in shapes]
+
+    @staticmethod
+    def scratch(count, size):
+        return [pltpu.SemaphoreType.DMA((count * size,)) for _ in range(3)] + [
+            pltpu.SemaphoreType.DMA((count * 2 * (size - 1),)) for _ in range(2)
+        ]
+
+
 def meet(peers):
     barrier = pltpu.get_barrier_semaphore()
     total = 0
@@ -201,7 +327,7 @@
     )(*shards)
 
 
-def line_sum(name, part, extras, extra_outs, epilogue, collective_id, chunk=32, gather=None):
+def line_sum(name, part, extras, extra_outs, epilogue, collective_id, chunk=32, skew=2, gather=None, scatter=None):
     size = lax.axis_size("tp")
     rows, width = part.shape
     half = rows // 2
@@ -213,7 +339,10 @@
     else:
         shards, gathered, where = gather
     n_shards, n_gathered = len(shards), len(gathered)
+    grads, dims = scatter or ([], [])
+    n_grads = len(grads)
     fsdp_size = lax.axis_size("fsdp")
+    scattered = [RingScatter.out_shape(g, d, fsdp_size) for g, d in zip(grads, dims)]
 
     def kernel(*refs):
         refs = list(refs)
@@ -226,9 +355,11 @@
         (part_ref,) = take(1)
         extra_refs = take(n_extra)
         shard_refs = take(n_shards)
+        grad_refs = take(n_grads)
         (out_ref,) = take(1)
         extra_out_refs = take(n_extra_out)
         gathered_refs = take(n_gathered)
+        scattered_refs = take(n_grads)
         came, gone, sum_send, sum_recv, back_send, back_recv = take(6)
         place = lax.axis_index("tp")
         first, last = place == 0, place == size - 1
@@ -236,6 +367,12 @@
         job = None
         if n_shards:
             job = RingGather(shard_refs, gathered_refs, where, take(5), fsdp_size, fsdp_size == 4)
+            peers += [(None, peer) for peer in job.peers()]
+        if n_grads:
+            buffers = take(3 * n_grads)
+            job = RingScatter(
+                grad_refs, scattered_refs, dims, buffers, take(5), fsdp_size, fsdp_size == 4
+            )
             peers += [(None, peer) for peer in job.peers()]
         meet(peers)
 
@@ -281,52 +418,62 @@
         if job is not None:
             job.start()
 
-        def add(k):
+        away = (place - 1, size - 2 - place)
+
+        def each_way(step, lead, act):
             for way in range(2):
+                k = step - skew * lead[way]
+
+                @pl.when(jnp.logical_and(k >= 0, k < count))
+                def _():
+                    act(way, k)
+
+        def add(way, k):
+            @pl.when(jnp.logical_not(source[way]))
+            def _():
+                onward(way, k, False).wait_recv()
+                total = came[way, k].astype(F32) + part_ref[at(way, k), :].astype(F32)
+
+                @pl.when(owner[way])
+                def _():
+                    start = pl.multiple_of(k * chunk, chunk)
+                    out_ref[at(way, k), :] = epilogue(
+                        extra_refs, extra_out_refs, at(way, k), pl.ds(start, chunk), total
+                    )
+                    back(way, k).start()
+
+                @pl.when(jnp.logical_not(owner[way]))
+                def _():
+                    gone[way, k] = total.astype(BF16)
+                    onward(way, k, False).start()
+
+        def spread(way, k):
+            @pl.when(jnp.logical_not(owner[way]))
+            def _():
+                back(way, k).wait_recv()
 
                 @pl.when(jnp.logical_not(source[way]))
                 def _():
-                    onward(way, k, False).wait_recv()
-                    total = came[way, k].astype(F32) + part_ref[at(way, k), :].astype(F32)
-
-                    @pl.when(owner[way])
-                    def _():
-                        start = pl.multiple_of(k * chunk, chunk)
-                        out_ref[at(way, k), :] = epilogue(
-                            extra_refs, extra_out_refs, at(way, k), pl.ds(start, chunk), total
-                        )
-                        back(way, k).start()
-
-                    @pl.when(jnp.logical_not(owner[way]))
-                    def _():
-                        gone[way, k] = total.astype(BF16)
-                        onward(way, k, False).start()
-
-        def spread(k):
-            for way in range(2):
-
-                @pl.when(jnp.logical_not(owner[way]))
-                def _():
-                    back(way, k).wait_recv()
-
-                    @pl.when(jnp.logical_not(source[way]))
-                    def _():
-                        back(way, k).start()
-
-        steps = [add, spread]
+                    back(way, k).start()
+
+        steps = count + skew * (size - 2)
+        phases = [(add, away), (spread, (away[1], away[0]))]
         cuts = []
-        if job is not None:
-            cuts = [((2 * count - 2) * (i + 1)) // fsdp_size for i in range(fsdp_size - 1)]
-        for number, step in enumerate(steps):
-            low, high = number * count, (number + 1) * count
+        if n_shards:
+            cuts = [((2 * steps - 2) * (i + 1)) // fsdp_size for i in range(fsdp_size - 1)]
+        if n_grads:
+            first_cut, last_cut = (2 * steps) // 5, 2 * steps - 2
+            cuts = [first_cut + ((last_cut - first_cut) * i) // (fsdp_size - 1) for i in range(fsdp_size)]
+        for number, (act, lead) in enumerate(phases):
+            low, high = number * steps, (number + 1) * steps
             edges = [low] + [c for c in cuts if low < c < high] + [high]
             for left, right in zip(edges[:-1], edges[1:]):
                 if left in cuts:
                     job.advance(cuts.index(left))
 
                 @pl.loop(left - low, right - low)
-                def _(k):
-                    step(k)
+                def _(step):
+                    each_way(step, lead, act)
 
         if job is not None:
             job.finish()
@@ -351,19 +498,77 @@
     ] + [pltpu.SemaphoreType.DMA((2, count)) for _ in range(4)]
     if n_shards:
         scratch += RingGather.scratch(n_shards, fsdp_size)
+    if n_grads:
+        scratch += RingScatter.buffers(scattered, fsdp_size) + RingScatter.scratch(n_grads, fsdp_size)
     return pl.pallas_call(
         kernel,
         out_shape=[jax.ShapeDtypeStruct((rows, width), BF16)]
         + [jax.ShapeDtypeStruct(s, d) for s, d in extra_outs]
-        + [jax.ShapeDtypeStruct(s, BF16) for s in gathered],
-        in_specs=[WHOLE] * (1 + n_extra + n_shards),
-        out_specs=[WHOLE] * (1 + n_extra_out) + [ANY] * n_gathered,
+        + [jax.ShapeDtypeStruct(s, BF16) for s in gathered]
+        + [jax.ShapeDtypeStruct(s, F32) for s in scattered],
+        in_specs=[WHOLE] * (1 + n_extra + n_shards) + [ANY] * n_grads,
+        out_specs=[WHOLE] * (1 + n_extra_out) + [ANY] * n_gathered + [WHOLE] * n_grads,
         scratch_shapes=scratch,
         compiler_params=pltpu.CompilerParams(
             collective_id=collective_id, has_side_effects=True, vmem_limit_bytes=VMEM_BYTES
         ),
         name=name,
-    )(part, *extras, *shards)
+    )(part, *extras, *shards, *grads)
+
+
+def small_sum(vector, collective_id):
+    length = vector.shape[0]
+    rows = -(-length // 1024) * 8
+    block = jnp.pad(vector, (0, rows * 128 - length)).reshape(rows, 128)
+    axes = [(axis, lax.axis_size(axis)) for axis in ("ctx", "fsdp", "tp")]
+
+    def kernel(in_ref, out_ref, *scratch):
+        slots, sends, recvs = scratch[:3], scratch[3:6], scratch[6:9]
+        meet(
+            [
+                (None, {axis: lax.rem(lax.axis_index(axis) + step, size)})
+                for axis, size in axes
+                for step in range(1, size)
+            ]
+        )
+        total = in_ref[...]
+        for number, (axis, size) in enumerate(axes):
+            mine = lax.axis_index(axis)
+            slot = slots[number]
+            slot[mine] = total
+            copies = [
+                pltpu.make_async_remote_copy(
+                    src_ref=slot.at[mine],
+                    dst_ref=slot.at[mine],
+                    send_sem=sends[number].at[step - 1],
+                    recv_sem=recvs[number].at[step - 1],
+                    device_id={axis: lax.rem(mine + step, size)},
+                    device_id_type=BY_AXIS,
+                )
+                for step in range(1, size)
+            ]
+            for copy in copies:
+                copy.start()
+            for copy in copies:
+                copy.wait_recv()
+            total = slot[0]
+            for k in range(1, size):
+                total = total + slot[k]
+            for copy in copies:
+                copy.wait_send()
+        out_ref[...] = total
+
+    summed = pl.pallas_call(
+        kernel,
+        out_shape=jax.ShapeDtypeStruct((rows, 128), F32),
+        in_specs=[WHOLE],
+        out_specs=WHOLE,
+        scratch_shapes=[pltpu.VMEM((size, rows, 128), F32) for _, size in axes]
+        + [pltpu.SemaphoreType.DMA((size - 1,)) for _, size in axes] * 2,
+        compiler_params=pltpu.CompilerParams(collective_id=collective_id, has_side_effects=True),
+        name="small_sum",
+    )(block)
+    return summed.reshape(-1)[:length]
 
 
 def rms(value):
@@ -707,12 +912,23 @@
     grad_up = (grad_hidden * act).astype(BF16)
     grad_both = jnp.concatenate([grad_gate, grad_up], axis=1)
     part_two = dot(grad_both, w_both, NT).astype(BF16)
-    grad_branch, grad_middle, ffn_gain_part = line_sum(
-        "sum_norm_two", part_two, [middle, grad_low, ffn_gain.reshape(1, width)],
-        [((half, width), F32), ((half // min(32, half), width), F32)], grad_middle_rows, 3,
-    )
     grad_w_down = dot(hidden, grad_low, TN).astype(BF16)
     grad_w_both = dot(normed_two, grad_both, TN).astype(BF16)
+    both_axes = ("fsdp", "ctx")
+
+    def scattered(grads, dims):
+        if ctx == 2:
+            return (grads, dims), None
+        return None, [
+            lax.psum_scatter(g, both_axes, scatter_dimension=d, tiled=True).astype(F32) for g, d in zip(grads, dims)
+        ]
+
+    job, sums_ffn = scattered([grad_w_both, grad_w_down], [0, 1])
+    grad_branch, grad_middle, ffn_gain_part, *more = line_sum(
+        "sum_norm_two", part_two, [middle, grad_low, ffn_gain.reshape(1, width)],
+        [((half, width), F32), ((half // min(32, half), width), F32)], grad_middle_rows, 3, scatter=job,
+    )
+    out_both, out_down = sums_ffn or more
 
     grad_gated = dot(grad_branch, w_out, NT)
     grad_outgate, grad_mixed, head_part, local_begin = plain_call(
@@ -741,23 +957,15 @@
 
     grad_four = jnp.concatenate([grad_query, grad_forget, grad_value, grad_outgate], axis=1)
     part_one = dot(grad_four, w_four, NT).astype(BF16)
-    input_grad, norm_gain_part = line_sum(
-        "sum_norm_one", part_one, [x, grad_middle, norm_gain.reshape(1, width)],
-        [((half // min(32, half), width), F32)], input_grad_rows, 4,
-    )
-    input_grad = input_grad.reshape(groups, span, width)
     grad_w_output = dot(gated, grad_branch, TN).astype(BF16)
     grad_w_four = dot(normed, grad_four, TN).astype(BF16)
-
-    both_axes = ("fsdp", "ctx")
-
-    def scatter(grad, dim):
-        return lax.psum_scatter(grad, both_axes, scatter_dimension=dim, tiled=True).astype(F32)
-
-    out_down = scatter(grad_w_down, 1)
-    out_both = scatter(grad_w_both, 0)
-    out_output = scatter(grad_w_output, 1)
-    out_four = scatter(grad_w_four, 0)
+    job, sums_mix = scattered([grad_w_four, grad_w_output], [0, 1])
+    input_grad, norm_gain_part, *more = line_sum(
+        "sum_norm_one", part_one, [x, grad_middle, norm_gain.reshape(1, width)],
+        [((half // min(32, half), width), F32)], input_grad_rows, 4, scatter=job,
+    )
+    out_four, out_output = sums_mix or more
+    input_grad = input_grad.reshape(groups, span, width)
 
     owner = jnp.logical_or(place == 0, place == tp - 1)
     sums = jnp.concatenate(
@@ -768,7 +976,7 @@
             lax.dynamic_update_slice(jnp.zeros((tp * local,), F32), gap_part[0], (place * local,)),
         ]
     )
-    sums = lax.psum(sums, ("fsdp", "ctx", "tp"))
+    sums = small_sum(sums, 5)
     grad_norm_gain, grad_ffn_gain = sums[:width], sums[width : 2 * width]
     grad_head_gain = sums[2 * width : 2 * width + HEAD_DIM]
     grad_gap = lax.dynamic_slice(sums, (2 * width + HEAD_DIM + place * local,), (local,))

time: 1300 us -> 764 us (0.59)
  Pallas kernels: 1030 us -> 546 us
  blocking collectives: 48.2 us -> 0 us
    pallas_call x3, Pallas kernels: 930 us -> 433 us  [line_sum(): pl.pallas_call(kernel, out_shape=[jax.ShapeDtypeStruct((rows, width), BF1...]
    psum x1 -> x0, blocking collectives: 48.2 us -> none  [per_device(): sums = lax.psum(sums, ('fsdp', 'ctx', 'tp'))]
  transfers between devices with their start and end apart: 7 -> 3, of which waited for: 1 -> 0; matrix products, arithmetic and copies ran while one was open for 8% -> 9% of each run, Pallas kernels for 30% -> 30%
where the time goes in v2:
time: 764 us; the launch traced here: 755 us
  Pallas kernels  546 us (71%)
  matrix products  147 us (19%)
  local copies, waits for them, and re-layouts  25.9 us (3%)
  other arithmetic  16.8 us (2%)
  between operations  15.4 us (2%)
    pallas_call x3, Pallas kernels, line_sum(): pl.pallas_call(kernel, out_shape=[jax.ShapeDtypeStruct((rows, width), BF1...  433 us
    dot_general x12, matrix products, dot(): lax.dot_general(left, right, (dims, ((), ())), preferred_element_type=F32)  147 us
    pallas_call x1, Pallas kernels, gather_weights(): pl.pallas_call(kernel, out_shape=[jax.ShapeDtypeStruct(s, BF16) for s in...  51.5 us
    pallas_call x1, Pallas kernels, per_device(): plain_call(functools.partial(mix_back_kernel, heads, length), 'mix_back',...  17 us
  transfers between devices with their start and end apart: 3, of which 0 were waited for; matrix products, arithmetic and copies ran while one was open for 9% of the time, Pallas kernels for 30%

profile of v2, /device:TPU:0, one launch (start us, length us, event | category | flops | bytes accessed | tf_op | source)
XLA Modules:
  0.0 755.1 jit_solution(13349779038798660681)
XLA Ops:
  7.2 3.1 fusion
  11.0 51.5 %gather_weights.1 = (bf16[2048,2048]{1,0:T(8,128)(2,1)}, bf16[512,2048]{1,0:T(8,128)(2,1)}) custom-call(bf16[512,512]{1,0:T(8,128)(2,1)} %refs_0_.1, bf16[512,512]{1,0:T(8,128)(2,1)} %refs_1_.1, bf16[512,512]{1,0:T(8,128)(2,1)} %refs_2_.1, bf16[512,512]{1,0:T(8,128)(2,1)} %refs_3_.2, bf16[512,512]{1,0:T(8,128)(2,1)} %refs_4_.2), custom_call_target="tpu_custom_call" | custom-call | tf_op jit(solution)/shard_map/gather_weights/pallas_call | solution.py:317
  62.5 14.5 %fusion.14.forget_ref.value_ref.query_ref.gate_ref = f32[1024,2048]{1,0:T(8,128)} fusion(bf16[2048,2048]{1,0:T(8,128)(2,1)} %get-tuple-element.40, f32[2048]{0:T(1024)S(1)} %copy-done.14, f32[1024]{0:T(1024)S(1)} %add_rsqrt_fusion, bf16[1,1024,2048]{2,1,0:T(8,128)(2,1)} %param.15), kind=kOutput, calls=%fused_computation.32 | convolution fusion | flops 8598323200 | bytes 20983808 | tf_op jit(solution)/shard_map/dot_general | solution.py:21
  77.0 9.7 %span_end.1 = f32[4,128,128]{2,1,0:T(8,128)} custom-call(s32[1]{0:T(128)} %min.6.valid_ref, f32[1024,2048]{1,0:T(8,128)} %fusion.14.forget_ref.value_ref.query_ref.gate_ref, f32[1024,2048]{1,0:T(8,128)} %fusion.14.forget_ref.value_ref.query_ref.gate_ref, f32[1,512]{1,0:T(1,128)} %bitcast.58), custom_call_target="tpu_custom_call" | custom-call | flops 402653184 | bytes 4194304 | tf_op jit(solution)/shard_map/span_end/pallas_call | solution.py:859
  86.6 2.3 collective-permute-start
  89.0 4.5 bitcast_select_fusion.refs_2_
  93.4 2.4 fusion.12
  95.9 0.6 exponential_bitcast_fusion
  96.5 0.7 copy-done.7
  97.2 12.4 %mix.1 = (bf16[1024,512]{1,0:T(8,128)(2,1)}, f32[1024,512]{1,0:T(8,128)}, f32[8,4,128,128]{3,2,1,0:T(8,128)}) custom-call(s32[1]{0:T(128)} %min.6.valid_ref, f32[1024,2048]{1,0:T(8,128)} %fusion.14.forget_ref.value_ref.query_ref.gate_ref, f32[1024,2048]{1,0:T(8,128)} %fusion.14.forget_ref.value_ref.query_ref.gate_ref, ...), custom_call_target="tpu_custom_call" | custom-call | flops 805306368 | bytes 12582912 | tf_op jit(solution)/shard_map/mix/pallas_call | solution.py:871
  109.6 6.3 convolution_convert_fusion.5.refs_0_
  115.9 115.8 %sum_branch.1 = (bf16[1024,2048]{1,0:T(8,128)(2,1)}, f32[512,2048]{1,0:T(8,128)}, bf16[2048,2816]{1,0:T(8,128)(2,1)}, bf16[1408,2048]{1,0:T(8,128)(2,1)}) custom-call(bf16[1024,2048]{1,0:T(8,128)(2,1)} %convolution_convert_fusion.5.refs_0_, bf16[1024,2048]{1,0:T(8,128)(2,1)} %bitcast.55, f32[1,2048]{1,0:T(1,128)} %bitcast.62, bf16[512,1408]{1,0:T(8,128)(2,1)} %refs_3_.3, ...), custom_call_target="tpu_custom_call" | custom-call | tf_op jit(solution)/shard_map/sum_branch/pallas_call | solution.py:503
  231.7 18.8 %fusion.24 = f32[1024,2816]{1,0:T(8,128)} fusion(bf16[1024,2048]{1,0:T(8,128)(2,1)} %get-tuple-element.43, bf16[2048,2816]{1,0:T(8,128)(2,1)} %get-tuple-element.44), kind=kOutput, calls=%fused_computation.59 | convolution fusion | flops 11811160064 | bytes 27262976 | tf_op jit(solution)/shard_map/dot_general | solution.py:21
  250.5 13.5 %multiply_convert_fusion.1 = (bf16[1024,1408]{1,0:T(8,128)(2,1)}, bf16[1024,1408]{1,0:T(8,128)(2,1)}, bf16[1024,1408]{1,0:T(8,128)(2,1)}) fusion(f32[1024,2816]{1,0:T(8,128)} %fusion.24, bf16[1024,2048]{1,0:T(8,128)(2,1)S(1)} %copy-done.2, bf16[1408,2048]{1,0:T(8,128)(2,1)S(1)} %copy-done.21), kind=kOutput, calls=%fused_computation.12 | convolution fusion | flops 5927206912 | bytes 30146560 | tf_op jit(solution)/shard_map/dot_general | solution.py:21
  264.0 19.0 %convolution_convert_fusion.refs_4_ = bf16[2048,2816]{1,0:T(8,128)(2,1)} fusion(bf16[1024,2048]{1,0:T(8,128)(2,1)} %get-tuple-element.43, bf16[1024,1408]{1,0:T(8,128)(2,1)} %get-tuple-element.67, bf16[1024,1408]{1,0:T(8,128)(2,1)} %get-tuple-element.66), kind=kOutput, calls=%fused_computation | convolution fusion | flops 11828461568 | bytes 21495808 | tf_op jit(solution)/shard_map/dot_general | solution.py:21
  283.0 17.3 %convolution_convert_fusion.3.refs_0_ = bf16[1024,2048]{1,0:T(8,128)(2,1)} fusion(bf16[2048,2816]{1,0:T(8,128)(2,1)} %get-tuple-element.44, bf16[1024,1408]{1,0:T(8,128)(2,1)} %get-tuple-element.67, bf16[1024,1408]{1,0:T(8,128)(2,1)S(1)} %copy-done.25), kind=kOutput, calls=%fused_computation.18 | convolution fusion | flops 11824791552 | bytes 21495808 | tf_op jit(solution)/shard_map/dot_general | solution.py:21
  300.3 8.2 %convolution_convert_fusion.2.refs_5_ = bf16[1408,2048]{1,0:T(8,128)(2,1)} fusion(bf16[1024,1408]{1,0:T(8,128)(2,1)S(1)} %copy-done.24, bf16[1024,2048]{1,0:T(8,128)(2,1)S(1)} %copy-done.2), kind=kOutput, calls=%fused_computation.9 | convolution fusion | flops 5908463616 | bytes 12845056 | tf_op jit(solution)/shard_map/dot_general | solution.py:21
  308.6 4.4 broadcast_select_fusion.1
  313.0 117.1 %sum_norm_two.1 = (bf16[1024,2048]{1,0:T(8,128)(2,1)}, f32[512,2048]{1,0:T(8,128)}, f32[16,2048]{1,0:T(8,128)}, f32[256,2816]{1,0:T(8,128)}, f32[1408,256]{1,0:T(8,128)}) custom-call(bf16[1024,2048]{1,0:T(8,128)(2,1)} %convolution_convert_fusion.3.refs_0_, f32[512,2048]{1,0:T(8,128)} %get-tuple-element.46.refs_1_, ...), custom_call_target="tpu_custom_call" | custom-call | tf_op jit(solution)/shard_map/sum_norm_two/pallas_call | solution.py:503
  430.1 6.6 fusion.25.grad_ref
  436.7 10.6 %span_begin.1 = (bf16[1024,512]{1,0:T(8,128)(2,1)}, bf16[1024,512]{1,0:T(8,128)(2,1)}, f32[1,128]{1,0:T(1,128)}, f32[4,128,128]{2,1,0:T(8,128)}) custom-call(s32[1]{0:T(128)} %min.6.valid_ref, f32[1024,512]{1,0:T(8,128)} %fusion.25.grad_ref, f32[1024,512]{1,0:T(8,128)} %get-tuple-element.48.mixed_ref, ...), custom_call_target="tpu_custom_call" | custom-call | flops 402653184 | bytes 12582912 | tf_op jit(solution)/shard_map/span_begin/pallas_call | solution.py:934
  447.4 1.6 collective-permute-start.1
  448.9 3.6 fusion.22
  452.5 11.8 %fusion.5 = bf16[1,1024,2048]{2,1,0:T(8,128)(2,1)} fusion(f32[512,2048]{1,0:T(8,128)} %get-tuple-element.70, f32[512,2048]{1,0:T(8,128)S(1)} %copy-done.3, bf16[1024,1408]{1,0:T(8,128)(2,1)} %get-tuple-element.68, bf16[1408,2048]{1,0:T(8,128)(2,1)} %get-tuple-element.45), kind=kOutput, calls=%fused_computation.16 | convolution fusion | flops 5911871488 | bytes 21233664 | tf_op jit(solution)/shard_map/dot_general | solution.py:21
  464.3 5.9 convolution_convert_fusion.6.refs_5_
  470.3 0.9 copy-done.12
  471.3 0.7 multiply_add_fusion.last_ref
  472.1 0.7 copy-done.23
  472.8 17.0 %mix_back.1 = (bf16[1024,512]{1,0:T(8,128)(2,1)}, bf16[1024,512]{1,0:T(8,128)(2,1)}, bf16[1024,512]{1,0:T(8,128)(2,1)}, f32[1,512]{1,0:T(1,128)}) custom-call(s32[1]{0:T(128)} %min.6.valid_ref, bf16[1024,512]{1,0:T(8,128)(2,1)} %get-tuple-element.49.grad_ref, f32[1024,2048]{1,0:T(8,128)} %fusion.14.forget_ref.value_ref.query_ref.gate_ref, ...), custom_call_target="tpu_custom_call" | custom-call | flops 1610612736 | bytes 12582912 | tf_op jit(solution)/shard_map/mix_back/pallas_call | solution.py:948
  489.8 1.5 constant_dynamic-update-slice_fusion.3
  491.3 1.4 constant_dynamic-update-slice_fusion.2
  492.9 0.1 constant_dynamic-update-slice_fusion
  493.1 12.7 %convolution_convert_fusion.4.refs_0_ = bf16[1024,2048]{1,0:T(8,128)(2,1)} fusion(bf16[1024,2048]{1,0:T(8,128)(2,1)S(1)} %constant_dynamic-update-slice_fusion, bf16[2048,2048]{1,0:T(8,128)(2,1)} %get-tuple-element.40), kind=kOutput, calls=%fused_computation.19 | convolution fusion | flops 8592031744 | bytes 16777216 | tf_op jit(solution)/shard_map/dot_general | solution.py:21
  505.8 11.9 %convolution_convert_fusion.1.refs_4_ = bf16[2048,2048]{1,0:T(8,128)(2,1)} fusion(bf16[1024,2048]{1,0:T(8,128)(2,1)S(1)} %constant_dynamic-update-slice_fusion, f32[2048]{0:T(1024)S(1)} %copy-done.15, f32[1024]{0:T(1024)S(1)} %copy-done.18, bf16[1,1024,2048]{2,1,0:T(8,128)(2,1)S(1)} %copy-done), kind=kOutput, calls=%fused_computation.8 | convolution fusion | flops 8602517504 | bytes 16789504 | tf_op jit(solution)/shard_map/dot_general | solution.py:21
  517.7 199.7 %sum_norm_one.1 = (bf16[1024,2048]{1,0:T(8,128)(2,1)}, f32[16,2048]{1,0:T(8,128)}, f32[256,2048]{1,0:T(8,128)}, f32[512,256]{1,0:T(8,128)}) custom-call(bf16[1024,2048]{1,0:T(8,128)(2,1)} %convolution_convert_fusion.4.refs_0_, bf16[1024,2048]{1,0:T(8,128)(2,1)} %bitcast.56, f32[512,2048]{1,0:T(8,128)} %get-tuple-element.56.refs_2_, f32[1,2048]{1,0:T(1,128)} %bitcast.64, ...), custom_call_target="tpu_custom_call" | custom-call | tf_op jit(solution)/shard_map/sum_norm_one/pallas_call | solution.py:503
  717.5 0.9 reduce_sum.38
  718.4 0.3 dynamic_update_slice.3
  718.7 0.6 fusion.16.in_ref
  719.3 12.7 %small_sum.1 = f32[56,128]{1,0:T(8,128)} custom-call(f32[56,128]{1,0:T(8,128)} %fusion.16.in_ref), custom_call_target="tpu_custom_call" | custom-call | tf_op jit(solution)/shard_map/small_sum/pallas_call | solution.py:561
  732.0 0.8 slice_bitcast_fusion
  732.8 0.7 dynamic_slice.3
  733.4 1.2 slice_bitcast_fusion.3
  734.6 1.3 slice_bitcast_fusion.1
  735.9 2.9 fusion.23
  738.8 4.9 copy.38
  743.7 2.1 copy.39
  745.8 0.8 copy.40
  746.7 1.1 copy.41
  (61 shorter events, 0.6 us)
Async XLA Ops:
  7.2 55.3 %copy-start.14 = (f32[2048]{0:T(1024)S(1)}, f32[2048]{0:T(1024)}, u32[]{:S(2)}) copy-start(f32[2048]{0:T(1024)} %param.25) | copy-start | bytes 24580
  7.2 731.6 %all-reduce.3.cloned.1.call-start = ((), (), s32[]{:S(2)}) async-start(), calls=%async_computation | async-start | bytes 8388608 | tf_op jit(solution)/shard_map/psum | solution.py:908
  10.3 66.7 %copy-start.17 = (f32[1024]{0:T(1024)}, f32[1024]{0:T(1024)S(1)}, u32[]{:S(2)}) copy-start(f32[1024]{0:T(1024)S(1)} %add_rsqrt_fusion) | copy-start | bytes 12292
  86.6 9.9 %collective-permute-start = (f32[4,128,128]{2,1,0:T(8,128)}, f32[4,128,128]{2,1,0:T(8,128)S(1)}, u32[]{:S(2)}, u32[]{:S(2)}) collective-permute-start(f32[4,128,128]{2,1,0:T(8,128)} %span_end.1), channel_id=1, source_target_pairs={{0,4},{1,5},{2,6},{3,7},{8,12},{9,13},{10,14},{11,15},{16,20},{17,... | collective-permute-start | bytes 786440 | tf_op jit(solution)/shard_map/ppermute | solution.py:792
  89.0 4.5 copy-start.13
  96.5 0.7 copy-start.7
  231.7 18.8 %copy-start.2 = (bf16[1024,2048]{1,0:T(8,128)(2,1)S(1)}, bf16[1024,2048]{1,0:T(8,128)(2,1)}, u32[]{:S(2)}) copy-start(bf16[1024,2048]{1,0:T(8,128)(2,1)} %bitcast_select_fusion.refs_2_) | copy-start | bytes 12582916
  231.7 18.8 %copy-start.21 = (bf16[1408,2048]{1,0:T(8,128)(2,1)S(1)}, bf16[1408,2048]{1,0:T(8,128)(2,1)}, u32[]{:S(2)}) copy-start(bf16[1408,2048]{1,0:T(8,128)(2,1)} %get-tuple-element.45) | copy-start | bytes 17301508
  264.0 19.0 %copy-start.25 = (bf16[1024,1408]{1,0:T(8,128)(2,1)S(1)}, bf16[1024,1408]{1,0:T(8,128)(2,1)}, u32[]{:S(2)}) copy-start(bf16[1024,1408]{1,0:T(8,128)(2,1)} %get-tuple-element.66) | copy-start | bytes 8650756
  283.0 17.3 %copy-start.24 = (bf16[1024,1408]{1,0:T(8,128)(2,1)S(1)}, bf16[1024,1408]{1,0:T(8,128)(2,1)}, u32[]{:S(2)}) copy-start(bf16[1024,1408]{1,0:T(8,128)(2,1)} %get-tuple-element.68) | copy-start | bytes 8650756
  300.3 8.2 %copy-start.1 = (f32[512,2048]{1,0:T(8,128)S(1)}, f32[512,2048]{1,0:T(8,128)}, u32[]{:S(2)}) copy-start(f32[512,2048]{1,0:T(8,128)} %get-tuple-element.46.refs_1_) | copy-start | bytes 12582916
  447.4 5.1 copy-start.3
  447.4 24.7 %collective-permute-start.1 = (f32[4,128,128]{2,1,0:T(8,128)}, f32[4,128,128]{2,1,0:T(8,128)S(1)}, u32[]{:S(2)}, u32[]{:S(2)}) collective-permute-start(f32[4,128,128]{2,1,0:T(8,128)} %get-tuple-element.51), channel_id=1, source_target_pairs={{4,0},{5,1},{6,2},{7,3},{12,8},{13,9},{14,10},{15,11},{20,16},{21,... | collective-permute-start | bytes 786440 | tf_op jit(solution)/shard_map/ppermute | solution.py:805
  452.5 11.8 %copy-start.22 = (bf16[1024,512]{1,0:T(8,128)(2,1)S(1)}, bf16[1024,512]{1,0:T(8,128)(2,1)}, u32[]{:S(2)}) copy-start(bf16[1024,512]{1,0:T(8,128)(2,1)} %get-tuple-element.41) | copy-start | bytes 3145732
  470.2 0.9 copy-start.12
  470.2 1.0 copy-start.6
  470.2 1.1 copy-start.8
  470.2 1.1 copy-start.16
  472.1 0.7 copy-start.23
  489.8 3.0 copy-start.10
  489.8 3.1 copy-start.9
  493.1 12.8 %copy-start = (bf16[1,1024,2048]{2,1,0:T(8,128)(2,1)S(1)}, bf16[1,1024,2048]{2,1,0:T(8,128)(2,1)}, u32[]{:S(2)}) copy-start(bf16[1,1024,2048]{2,1,0:T(8,128)(2,1)} %param.15) | copy-start | bytes 12582916
  493.1 12.8 %copy-start.15 = (f32[2048]{0:T(1024)S(1)}, f32[2048]{0:T(1024)}, u32[]{:S(2)}) copy-start(f32[2048]{0:T(1024)} %param.25) | copy-start | bytes 24580
  493.1 12.8 %copy-start.18 = (f32[1024]{0:T(1024)S(1)}, f32[1024]{0:T(1024)}, u32[]{:S(2)}) copy-start(f32[1024]{0:T(1024)} %copy-done.17) | copy-start | bytes 12292
  517.7 200.7 %copy-start.19 = (f32[1,512]{1,0:T(1,128)S(1)}, f32[1,512]{1,0:T(1,128)}, u32[]{:S(2)}) copy-start(f32[1,512]{1,0:T(1,128)} %get-tuple-element.65) | copy-start | bytes 6148
  517.7 201.0 %copy-start.20 = (f32[1,128]{1,0:T(1,128)S(1)}, f32[1,128]{1,0:T(1,128)}, u32[]{:S(2)}) copy-start(f32[1,128]{1,0:T(1,128)} %get-tuple-element.64) | copy-start | bytes 1540
  738.8 4.9 copy-start.4
  743.7 2.1 copy-start.11
  743.7 3.0 copy-start.5
Sparse Core Ops, SparseCore 0:
  470.4 230.0 all-reduce.2

commit v3 on v2

--- a/solution.py
+++ b/solution.py
@@ -12,7 +12,7 @@
 F32 = jnp.float32
 BF16 = jnp.bfloat16
 BY_AXIS = pl.DeviceIdType.MESH
-VMEM_BYTES = 62 * 1024 * 1024
+VMEM_BYTES = 67043328
 ANY = pl.BlockSpec(memory_space=pl.ANY)
 WHOLE = pl.BlockSpec(memory_space=pltpu.VMEM)
 
@@ -21,6 +21,7 @@
     return lax.dot_general(left, right, (dims, ((), ())), preferred_element_type=F32)
 
 
+NN = ((1,), (0,))
 NT = ((1,), (1,))
 TN = ((0,), (0,))
 
@@ -66,7 +67,7 @@
 
     def rows(self, i, core, way):
         quarter = self.shards[i].shape[0] // 4
-        return pl.multiple_of((2 * core + way) * quarter, 16), quarter
+        return pl.multiple_of((2 * way + core) * quarter, 16), quarter
 
     def in_shard(self, i, core, way):
         at, length = self.rows(i, core, way)
@@ -140,14 +141,21 @@
                 self.ring(i, way, step + 1).start()
             self.across(i, way, step, self.core).start()
 
-    def finish(self):
+    def wait_across(self, arrays, step):
+        for i in arrays:
+            for way in range(2):
+                self.across(i, way, step, 1 - self.core).wait_recv()
+
+    def finish(self, waited=()):
         for i, way in self.each():
             for step in range(self.size - 1):
                 self.ring(i, way, step).wait_send()
                 self.across(i, way, step, self.core).wait_send()
-                self.across(i, way, step, 1 - self.core).wait_recv()
+                if i not in waited:
+                    self.across(i, way, step, 1 - self.core).wait_recv()
         for i in range(len(self.shards)):
-            self.local_copy(i).wait()
+            if i not in waited:
+                self.local_copy(i).wait()
 
     @staticmethod
     def scratch(count, size):
@@ -190,8 +198,9 @@
 
     def across(self, i, offset):
         at = i * self.size + offset
+        give = self.own[i].at[0, offset] if self.grads[i] is None else self.block(i, offset, 1 - self.core)
         return pltpu.make_async_remote_copy(
-            src_ref=self.block(i, offset, 1 - self.core),
+            src_ref=give,
             dst_ref=self.came[i].at[offset],
             send_sem=self.pair_send.at[at],
             recv_sem=self.pair_recv.at[at],
@@ -234,7 +243,8 @@
         for i in range(len(self.grads)):
             for offset in sorted(fresh):
                 self.across(i, offset).wait_recv()
-                self.local_copy(i, offset).wait()
+                if self.grads[i] is not None:
+                    self.local_copy(i, offset).wait()
             for way in range(2):
                 if step > 0:
                     self.ring(i, way, step - 1).wait_recv()
@@ -250,7 +260,8 @@
         @pl.loop(0, half // 16)
         def _(r):
             rows = pl.ds(pl.multiple_of(way * half + r * 16, 16), 16)
-            total = own[offset, rows, :].astype(F32) + came[offset, rows, :].astype(F32)
+            kept = own[offset, rows, :] if self.grads[i] is not None else own[1, offset, rows, :]
+            total = kept.astype(F32) + came[offset, rows, :].astype(F32)
             if step > 0:
                 total += passed[way, step - 1, pl.ds(pl.multiple_of(r * 16, 16), 16), :].astype(F32)
             if step < self.size - 1:
@@ -300,49 +311,372 @@
     pl.semaphore_wait(barrier, total)
 
 
-def gather_weights(shards, out_shapes, where, collective_id):
+def project(x, cotangent, gain, valid, shards, w_out_shard, collective_id):
     size = lax.axis_size("fsdp")
-    folded = size == 4
+    rows, width = x.shape
+    deep, local = shards[0].shape
     count = len(shards)
-
-    def kernel(*refs):
-        ins, outs, sems = refs[:count], refs[count : count + len(out_shapes)], refs[-5:]
-        job = RingGather(ins, outs, where, sems, size, folded)
+    total = count * local
+    half = deep // 2
+    tile = min(512, total)
+    step_rows = min(64, rows)
+    copies = 1 + 2 * (size - 1)
+
+    def kernel(
+        valid_ref, gain_ref, x_ref, cot_ref, *refs
+    ):
+        shard_refs, refs = refs[: count + 1], refs[count + 1 :]
+        pre_ref, normed_ref, grad_ref, four_ref, out_ref = refs[:5]
+        x_here, grad_here, normed, acc, four, in_sem, save_sem, four_sem, pre_sem = refs[5:14]
+        where = [(0, 0, i * local) for i in range(count)] + [(1, 1, 0)]
+        job = RingGather(shard_refs, [four, out_ref], where, refs[14:], size, size == 4)
+        loads = [
+            pltpu.make_async_copy(x_ref, x_here, in_sem.at[0]),
+            pltpu.make_async_copy(cot_ref, grad_here, in_sem.at[1]),
+        ]
+        for load in loads:
+            load.start()
         meet([(None, peer) for peer in job.peers()])
         job.start()
+        loads[0].wait()
+
+        @pl.loop(0, rows // step_rows)
+        def _(r):
+            at = pl.ds(pl.multiple_of(r * step_rows, step_rows), step_rows)
+            wide = x_here[at, :].astype(F32)
+            normed[at, :] = (wide * rms(wide) * gain_ref[...]).astype(BF16)
+
+        saves = [
+            pltpu.make_async_copy(normed, normed_ref, save_sem.at[0]),
+            pltpu.make_async_copy(grad_here, grad_ref, save_sem.at[1]),
+        ]
+        saves[0].start()
+
+        def save_four(start, length, number):
+            at = pl.ds(start, length)
+            return pltpu.make_async_copy(four.at[at, :], four_ref.at[at, :], four_sem.at[number])
+
+        def save_pre(n):
+            at = pl.ds(pl.multiple_of(n * tile, tile), tile)
+            return pltpu.make_async_copy(acc.at[:, at], pre_ref.at[:, at], pre_sem.at[n])
+
+        def multiply(start, length, first, last):
+            @pl.loop(0, total // tile)
+            def _(n):
+                cols = pl.ds(pl.multiple_of(n * tile, tile), tile)
+                deep_at = pl.ds(start, length)
+                term = dot(normed[:, deep_at], four[deep_at, cols])
+                acc[:, cols] = term if first else acc[:, cols] + term
+                if last:
+                    save_pre(n).start()
+
+        for i in range(count):
+            job.local_copy(i).wait()
+        own = pl.multiple_of(job.device(job.place) * deep, deep)
+        save_four(own, deep, 0).start()
+        multiply(own, deep, True, False)
+        loads[1].wait()
+
+        @pl.loop(0, rows // step_rows)
+        def _(r):
+            at = pl.ds(pl.multiple_of(r * step_rows, step_rows), step_rows)
+            row = lax.broadcasted_iota(jnp.int32, (step_rows, width), 0) + r * step_rows
+            wide = grad_here[at, :].astype(F32)
+            grad_here[at, :] = jnp.where(row < valid_ref[0], wide, 0.0).astype(BF16)
+
+        saves[1].start()
         for step in range(size - 1):
             job.advance(step)
-        job.finish()
+            job.wait_across(range(count), step)
+            for way in range(2):
+                block = job.device(job.place - (1 - 2 * way) * (step + 1))
+                start = pl.multiple_of(block * deep + way * half, half)
+                save_four(start, half, 1 + 2 * step + way).start()
+                multiply(start, half, False, step == size - 2 and way == 1)
+        job.finish(range(count))
+        for save in saves:
+            save.wait()
+        save_four(own, deep, 0).wait()
+        for step in range(size - 1):
+            for way in range(2):
+                save_four(0, half, 1 + 2 * step + way).wait()
+        for n in range(total // tile):
+            save_pre(n).wait()
 
     return pl.pallas_call(
         kernel,
-        out_shape=[jax.ShapeDtypeStruct(s, BF16) for s in out_shapes],
-        in_specs=[WHOLE] * count,
-        out_specs=[ANY] * len(out_shapes),
-        scratch_shapes=RingGather.scratch(count, size),
+        out_shape=[
+            jax.ShapeDtypeStruct((rows, total), F32),
+            jax.ShapeDtypeStruct((rows, width), BF16),
+            jax.ShapeDtypeStruct((rows, width), BF16),
+            jax.ShapeDtypeStruct((width, total), BF16),
+            jax.ShapeDtypeStruct((w_out_shard.shape[0], width), BF16),
+        ],
+        in_specs=[pl.BlockSpec(memory_space=pltpu.SMEM), WHOLE, ANY, ANY] + [WHOLE] * (count + 1),
+        out_specs=[ANY] * 5,
+        scratch_shapes=[
+            pltpu.VMEM((rows, width), BF16),
+            pltpu.VMEM((rows, width), BF16),
+            pltpu.VMEM((rows, width), BF16),
+            pltpu.VMEM((rows, total), F32),
+            pltpu.VMEM((width, total), BF16),
+            pltpu.SemaphoreType.DMA((2,)),
+            pltpu.SemaphoreType.DMA((2,)),
+            pltpu.SemaphoreType.DMA((copies,)),
+            pltpu.SemaphoreType.DMA((total // tile,)),
+        ]
+        + RingGather.scratch(count + 1, size),
         compiler_params=pltpu.CompilerParams(
             collective_id=collective_id, has_side_effects=True, vmem_limit_bytes=VMEM_BYTES
         ),
-        name="gather_weights",
-    )(*shards)
-
-
-def line_sum(name, part, extras, extra_outs, epilogue, collective_id, chunk=32, skew=2, gather=None, scatter=None):
+        name="project",
+    )(valid, gain, x, cotangent, *shards, w_out_shard)
+
+
+class GatherJob:
+    def __init__(self, shards, out_shapes, where):
+        self.size = lax.axis_size("fsdp")
+        self.inputs, self.in_specs = shards, [WHOLE] * len(shards)
+        self.out_shape = [jax.ShapeDtypeStruct(s, BF16) for s in out_shapes]
+        self.out_specs = [ANY] * len(out_shapes)
+        self.scratch = RingGather.scratch(len(shards), self.size)
+        self.where = where
+
+    def bind(self, ins, outs, scratch):
+        self.job = RingGather(ins, outs, self.where, scratch, self.size, self.size == 4)
+
+    def peers(self):
+        return self.job.peers()
+
+    def tasks(self):
+        return []
+
+    def cuts(self, steps):
+        return [((2 * steps - 2) * (i + 1)) // self.size for i in range(self.size - 1)]
+
+    def start(self):
+        self.job.start()
+
+    def advance(self, number):
+        self.job.advance(number)
+
+    def finish(self):
+        self.job.finish()
+
+
+class ScatterJob(GatherJob):
+    def __init__(self, grads, dims):
+        self.size = lax.axis_size("fsdp")
+        self.dims = dims
+        shapes = [RingScatter.out_shape(g, d, self.size) for g, d in zip(grads, dims)]
+        self.inputs, self.in_specs = grads, [ANY] * len(grads)
+        self.out_shape = [jax.ShapeDtypeStruct(s, F32) for s in shapes]
+        self.out_specs = [WHOLE] * len(grads)
+        self.scratch = RingScatter.buffers(shapes, self.size) + RingScatter.scratch(len(grads), self.size)
+
+    def bind(self, ins, outs, scratch):
+        self.job = RingScatter(
+            ins, outs, self.dims, scratch[:-5], scratch[-5:], self.size, self.size == 4
+        )
+
+    def cuts(self, steps):
+        first, last = (2 * steps) // 5, 2 * steps - 2
+        return [first + ((last - first) * i) // (self.size - 1) for i in range(self.size)]
+
+
+class ProductJob:
+    def __init__(self, left_at, right_at, dims, shape, tile):
+        self.left_at, self.right_at, self.dims, self.shape, self.tile = left_at, right_at, dims, shape, tile
+        self.inputs, self.in_specs = [], []
+        self.out_shape, self.out_specs = [jax.ShapeDtypeStruct(shape, BF16)], [ANY]
+        self.scratch = [pltpu.VMEM((2, tile, shape[1]), BF16), pltpu.SemaphoreType.DMA((2,))]
+
+    def bind(self, ins, outs, scratch):
+        (self.out,) = outs
+        self.stage, self.sem = scratch
+
+    def peers(self):
+        return []
+
+    def cuts(self, steps):
+        return []
+
+    def start(self):
+        pass
+
+    def tasks(self):
+        return [(self.shape[0] // self.tile, self.act, (self.left_at, self.right_at))]
+
+    def copy(self, i):
+        where = pl.ds(pl.multiple_of(i * self.tile, self.tile), self.tile)
+        return pltpu.make_async_copy(self.stage.at[i % 2], self.out.at[where, :], self.sem.at[i % 2])
+
+    def act(self, i):
+        @pl.when(i >= 2)
+        def _():
+            self.copy(i - 2).wait()
+
+        where = pl.ds(pl.multiple_of(i * self.tile, self.tile), self.tile)
+        product_tile(self.operands[self.left_at], self.operands[self.right_at], self.dims, where, self.stage.at[i % 2])
+        self.copy(i).start()
+
+    def finish(self):
+        tiles = self.shape[0] // self.tile
+        for i in range(max(0, tiles - 2), tiles):
+            self.copy(i).wait()
+
+
+def product_tile(left, right, dims, where, out):
+    rows = left[:, where].T if dims == TN else left[where, :]
+    width = out.shape[-1]
+    for start in range(0, width, 512):
+        cols = slice(start, min(start + 512, width))
+        if dims == NT:
+            out[:, cols] = dot(rows, right[cols, :], NT).astype(out.dtype)
+        else:
+            out[:, cols] = dot(rows, right[:, cols]).astype(out.dtype)
+
+
+class ProductScatterJob(ScatterJob):
+    def __init__(self, pairs, shapes, dims):
+        self.size = lax.axis_size("fsdp")
+        self.pairs, self.dims = pairs, dims
+        shapes = [RingScatter.out_shape(jax.ShapeDtypeStruct(s, BF16), d, self.size) for s, d in zip(shapes, dims)]
+        self.inputs, self.in_specs = [], []
+        self.out_shape = [jax.ShapeDtypeStruct(s, F32) for s in shapes]
+        self.out_specs = [WHOLE] * len(shapes)
+        self.scratch = [pltpu.VMEM((2, self.size) + s, BF16) for s in shapes]
+        self.scratch += [pltpu.VMEM((self.size,) + s, BF16) for s in shapes]
+        self.scratch += [pltpu.VMEM((2, self.size - 1, s[0] // 2, s[1]), BF16) for s in shapes]
+        self.scratch += RingScatter.scratch(len(shapes), self.size)
+
+    def bind(self, ins, outs, scratch):
+        self.job = RingScatter(
+            [None] * len(outs), outs, self.dims, scratch[:-5], scratch[-5:], self.size, self.size == 4
+        )
+
+    def cuts(self, steps):
+        first, last = min(self.ready_at + 2, 2 * steps - 8), 2 * steps - 3
+        return [first + ((last - first) * i) // (self.size - 1) for i in range(self.size)]
+
+    def start(self):
+        pass
+
+    def tasks(self):
+        made = []
+        for i in sorted(range(len(self.pairs)), key=lambda i: -self.dims[i]):
+            tiles = 2 * self.size if self.dims[i] == 0 else self.size
+            made.append((tiles, functools.partial(self.act, i), self.pairs[i]))
+        return made
+
+    def act(self, i, t):
+        job = self.job
+        left, right = (self.operands[p] for p in self.pairs[i])
+        if self.dims[i] == 0:
+            offset, mine = lax.rem(t // 2 + 1, self.size), t % 2
+            core = mine * job.core + (1 - mine) * (1 - job.core)
+            extent = job.outs[i].shape[0]
+            index = job.device(job.place + offset) * 2 + core
+            where = pl.ds(pl.multiple_of(index * extent, extent), extent)
+            product_tile(left, right, TN, where, job.own[i].at[mine, offset])
+
+            @pl.when(mine == 0)
+            def _():
+                job.across(i, offset).start()
+        else:
+            offset = lax.rem(t + 1, self.size)
+            extent = job.outs[i].shape[1]
+            start = pl.multiple_of(job.device(job.place + offset) * 2 * extent, 2 * extent)
+            tile = dot(left[...].T, right[:, pl.ds(start, 2 * extent)]).astype(BF16)
+            for core in range(2):
+                mine = 1 - core + (2 * core - 1) * job.core
+                job.own[i][mine, offset] = tile[:, core * extent : (core + 1) * extent]
+            job.across(i, offset).start()
+
+
+class VectorJob:
+    def __init__(self, others):
+        self.axes = [(axis, lax.axis_size(axis)) for axis in ("ctx", "fsdp", "tp")]
+        self.inputs, self.in_specs = [others], [WHOLE]
+        self.out_shape, self.out_specs = [jax.ShapeDtypeStruct(others.shape, F32)], [WHOLE]
+        self.scratch = [pltpu.VMEM((size,) + others.shape, F32) for _, size in self.axes] + [
+            pltpu.SemaphoreType.DMA((size - 1,)) for _, size in self.axes
+        ] * 2
+
+    def bind(self, ins, outs, scratch):
+        self.others, self.out = ins[0], outs[0]
+        self.slots, self.sends, self.recvs = scratch[:3], scratch[3:6], scratch[6:]
+
+    def peers(self):
+        return [
+            {axis: lax.rem(lax.axis_index(axis) + step, size)} for axis, size in self.axes for step in range(1, size)
+        ]
+
+    def cuts(self, steps):
+        return [steps + (steps * (i + 1)) // 6 for i in range(len(self.axes) + 1)]
+
+    def tasks(self):
+        return []
+
+    def start(self):
+        pass
+
+    def copies(self, number):
+        axis, size = self.axes[number]
+        mine = lax.axis_index(axis)
+        return [
+            pltpu.make_async_remote_copy(
+                src_ref=self.slots[number].at[mine],
+                dst_ref=self.slots[number].at[mine],
+                send_sem=self.sends[number].at[step - 1],
+                recv_sem=self.recvs[number].at[step - 1],
+                device_id={axis: lax.rem(mine + step, size)},
+                device_id_type=BY_AXIS,
+            )
+            for step in range(1, size)
+        ]
+
+    def advance(self, number):
+        if number == 0:
+            total = self.others[...] + self.extra()
+        else:
+            for copy in self.copies(number - 1):
+                copy.wait_recv()
+            slot = self.slots[number - 1]
+            total = slot[0]
+            for k in range(1, self.axes[number - 1][1]):
+                total = total + slot[k]
+        if number == len(self.axes):
+            self.out[...] = total
+            return
+        self.slots[number][lax.axis_index(self.axes[number][0])] = total
+        for copy in self.copies(number):
+            copy.start()
+
+    def finish(self):
+        for number in range(len(self.axes)):
+            for copy in self.copies(number):
+                copy.wait_send()
+
+
+def line_sum(
+    name, part, halves, gain, n_out, epilogue, collective_id, jobs=(), operands=(), chunk=32, skew=2
+):
     size = lax.axis_size("tp")
-    rows, width = part.shape
+    product = isinstance(part, tuple)
+    if product:
+        left_at, right_at, part_dims = part
+        rows = operands[left_at].shape[0]
+        width = operands[right_at].shape[1 - part_dims[1][0]]
+    else:
+        rows, width = part.shape
     half = rows // 2
     chunk = min(chunk, half)
     count = half // chunk
-    n_extra, n_extra_out = len(extras), len(extra_outs)
-    if gather is None:
-        shards, gathered, where = [], [], []
-    else:
-        shards, gathered, where = gather
-    n_shards, n_gathered = len(shards), len(gathered)
-    grads, dims = scatter or ([], [])
-    n_grads = len(grads)
-    fsdp_size = lax.axis_size("fsdp")
-    scattered = [RingScatter.out_shape(g, d, fsdp_size) for g, d in zip(grads, dims)]
+    group = min(128, half)
+    groups = half // group
+    per_group = group // chunk
+    vector = [job for job in jobs if isinstance(job, VectorJob)]
 
     def kernel(*refs):
         refs = list(refs)
@@ -352,43 +686,76 @@
             del refs[:n]
             return taken
 
-        (part_ref,) = take(1)
-        extra_refs = take(n_extra)
-        shard_refs = take(n_shards)
-        grad_refs = take(n_grads)
+        part_refs, (gain_ref,) = take(0 if product else 1), take(1)
+        half_refs = take(len(halves))
+        operand_refs = take(len(operands))
+        job_ins = [take(len(job.inputs)) for job in jobs]
         (out_ref,) = take(1)
-        extra_out_refs = take(n_extra_out)
-        gathered_refs = take(n_gathered)
-        scattered_refs = take(n_grads)
-        came, gone, sum_send, sum_recv, back_send, back_recv = take(6)
+        own_refs = take(n_out)
+        (gain_part_ref,) = take(1)
+        job_outs = [take(len(job.out_shape)) for job in jobs]
+        part_here, came, sum_send, sum_recv, back_send, back_recv, operand_sem, half_sem, own_sem, part_sem = take(10)
+        half_here = take(len(halves))
+        operand_here = take(len(operands))
+        own_here = take(n_out)
+        job_scratch = [take(len(job.scratch)) for job in jobs]
         place = lax.axis_index("tp")
         first, last = place == 0, place == size - 1
-        peers = [(jnp.logical_not(first), {"tp": place - 1}), (jnp.logical_not(last), {"tp": place + 1})]
-        job = None
-        if n_shards:
-            job = RingGather(shard_refs, gathered_refs, where, take(5), fsdp_size, fsdp_size == 4)
-            peers += [(None, peer) for peer in job.peers()]
-        if n_grads:
-            buffers = take(3 * n_grads)
-            job = RingScatter(
-                grad_refs, scattered_refs, dims, buffers, take(5), fsdp_size, fsdp_size == 4
-            )
-            peers += [(None, peer) for peer in job.peers()]
-        meet(peers)
-
         source = (first, last)
         owner = (last, first)
         ahead = (place + 1, place - 1)
         behind = (place - 1, place + 1)
+        base = (half, 0)
+
+        loaded = set()
+
+        def operand_copy(i):
+            return pltpu.make_async_copy(operand_refs[i], operand_here[i], operand_sem.at[i])
+
+        def need(places):
+            for i in places:
+                if i not in loaded:
+                    operand_copy(i).wait()
+                    loaded.add(i)
+
+        def half_copy(way, i):
+            start = base[way] if half_refs[i].shape[0] == rows else 0
+            return pltpu.make_async_copy(half_refs[i].at[pl.ds(start, half), :], half_here[i], half_sem.at[i])
+
+        def part_copy(way, g):
+            where = pl.ds(pl.multiple_of(base[way] + g * group, group), group)
+            return pltpu.make_async_copy(part_refs[0].at[where, :], part_here.at[where, :], part_sem.at[way, g])
+
+        if not product:
+            for g in range(groups):
+                for way in range(2):
+
+                    @pl.when(jnp.logical_not(source[way]))
+                    def _():
+                        part_copy(way, g).start()
+
+        for i in range(len(operands)):
+            operand_copy(i).start()
+
+        for way in range(2):
+
+            @pl.when(owner[way])
+            def _():
+                for i in range(len(halves)):
+                    half_copy(way, i).start()
+
+        for ins, outs, scratch, job in zip(job_ins, job_outs, job_scratch, jobs):
+            job.operands = operand_here
+            job.bind(ins, outs, scratch)
+        peers = [(jnp.logical_not(first), {"tp": place - 1}), (jnp.logical_not(last), {"tp": place + 1})]
+        meet(peers + [(None, peer) for job in jobs for peer in job.peers()])
 
         def at(way, k):
-            start = k * chunk + (half if way == 0 else 0)
-            return pl.ds(pl.multiple_of(start, chunk), chunk)
+            return pl.ds(pl.multiple_of(k * chunk + base[way], chunk), chunk)
 
         def onward(way, k, from_part):
-            source_ref = part_ref.at[at(way, k), :] if from_part else gone.at[way, k]
             return pltpu.make_async_remote_copy(
-                src_ref=source_ref,
+                src_ref=(part_here if product else part_refs[0]).at[at(way, k), :] if from_part else came.at[way, k],
                 dst_ref=came.at[way, k],
                 send_sem=sum_send.at[way, k],
                 recv_sem=sum_recv.at[way, k],
@@ -407,16 +774,48 @@
                 device_id_type=BY_AXIS,
             )
 
-        for way in range(2):
-
-            @pl.when(source[way])
-            def _():
-                @pl.loop(0, count)
-                def _(k):
-                    onward(way, k, True).start()
-
-        if job is not None:
+        def own_copy(k):
+            where = pl.ds(pl.multiple_of(k * chunk, chunk), chunk)
+            return pltpu.make_async_copy(own_here[0].at[where, :], own_refs[0].at[where, :], own_sem.at[k])
+
+        def part_rows(j):
+            way, g = j % 2, j // 2
+            where = pl.ds(pl.multiple_of((1 - way) * half + g * group, group), group)
+            left = operand_here[left_at][where, :]
+            for start in range(0, width, 512):
+                cols = slice(start, min(start + 512, width))
+                right = operand_here[right_at]
+                right = right[:, cols] if part_dims == NN else right[cols, :]
+                part_here[where, cols] = dot(left, right, part_dims).astype(BF16)
+            for w in range(2):
+
+                @pl.when(jnp.logical_and(source[w], way == w))
+                def _():
+                    @pl.loop(0, per_group)
+                    def _(k):
+                        onward(w, g * per_group + k, True).start()
+
+        tasks, at_step = [], 0
+        if product:
+            need((left_at, right_at))
+
+            @pl.loop(0, 2)
+            def _(j):
+                part_rows(j)
+
+            tasks, at_step = [(0, 2 * groups - 2, lambda i: part_rows(i + 2), ())], 2 * groups - 2
+        else:
+            for way in range(2):
+
+                @pl.when(source[way])
+                def _():
+                    @pl.loop(0, count)
+                    def _(k):
+                        onward(way, k, True).start()
+
+        for job in jobs:
             job.start()
+        gain_part_ref[...] = jnp.zeros_like(gain_part_ref)
 
         away = (place - 1, size - 2 - place)
 
@@ -431,20 +830,33 @@
         def add(way, k):
             @pl.when(jnp.logical_not(source[way]))
             def _():
+                if not product:
+
+                    @pl.when(k % per_group == 0)
+                    def _():
+                        part_copy(way, k // per_group).wait()
+
                 onward(way, k, False).wait_recv()
-                total = came[way, k].astype(F32) + part_ref[at(way, k), :].astype(F32)
+                total = came[way, k].astype(F32) + part_here[at(way, k), :].astype(F32)
 
                 @pl.when(owner[way])
                 def _():
-                    start = pl.multiple_of(k * chunk, chunk)
+                    @pl.when(k == 0)
+                    def _():
+                        for i in range(len(halves)):
+                            half_copy(way, i).wait()
+
+                    own = pl.ds(pl.multiple_of(k * chunk, chunk), chunk)
                     out_ref[at(way, k), :] = epilogue(
-                        extra_refs, extra_out_refs, at(way, k), pl.ds(start, chunk), total
+                        half_here, gain_ref[...], own_here[0] if n_out else None, gain_part_ref, own, total
                     )
                     back(way, k).start()
+                    if n_out:
+                        own_copy(k).start()
 
                 @pl.when(jnp.logical_not(owner[way]))
                 def _():
-                    gone[way, k] = total.astype(BF16)
+                    came[way, k] = total.astype(BF16)
                     onward(way, k, False).start()
 
         def spread(way, k):
@@ -457,25 +869,46 @@
                     back(way, k).start()
 
         steps = count + skew * (size - 2)
-        phases = [(add, away), (spread, (away[1], away[0]))]
-        cuts = []
-        if n_shards:
-            cuts = [((2 * steps - 2) * (i + 1)) // fsdp_size for i in range(fsdp_size - 1)]
-        if n_grads:
-            first_cut, last_cut = (2 * steps) // 5, 2 * steps - 2
-            cuts = [first_cut + ((last_cut - first_cut) * i) // (fsdp_size - 1) for i in range(fsdp_size)]
-        for number, (act, lead) in enumerate(phases):
+        for job in vector:
+            job.extra = lambda: jnp.where(
+                lax.broadcasted_iota(jnp.int32, (8, width), 0) == 0, gain_part_ref[...], 0.0
+            )
+        for job in jobs:
+            for tiles, act, needs in job.tasks():
+                tasks.append((at_step, tiles, act, needs))
+                at_step += tiles
+            job.ready_at = at_step
+        acts = sorted((cut, n, i) for n, job in enumerate(jobs) for i, cut in enumerate(job.cuts(steps)))
+        bounds = {t[0] for t in tasks} | {t[0] + t[1] for t in tasks}
+        for number, (act, lead) in enumerate([(add, away), (spread, (away[1], away[0]))]):
             low, high = number * steps, (number + 1) * steps
-            edges = [low] + [c for c in cuts if low < c < high] + [high]
+            here = [a for a in acts if low <= a[0] < high]
+            edges = sorted({low, high} | {a[0] for a in here} | {e for e in bounds if low < e < high})
             for left, right in zip(edges[:-1], edges[1:]):
-                if left in cuts:
-                    job.advance(cuts.index(left))
+                for cut, n, i in here:
+                    if cut == left:
+                        jobs[n].advance(i)
+                active = [t for t in tasks if t[0] <= left and right <= t[0] + t[1]]
+                for t in active:
+                    need(t[3])
 
                 @pl.loop(left - low, right - low)
                 def _(step):
                     each_way(step, lead, act)
-
-        if job is not None:
+                    for t in active:
+                        t[2](step + low - t[0])
+
+        for first_step, tiles, act, needs in tasks:
+            done = min(max(2 * steps - first_step, 0), tiles)
+            if done < tiles:
+                need(needs)
+
+                @pl.loop(done, tiles)
+                def _(i):
+                    act(i)
+
+        need(range(len(operands)))
+        for job in jobs:
             job.finish()
 
         for way in range(2):
@@ -492,122 +925,74 @@
                 def _(k):
                     back(way, k).wait_send()
 
+            if n_out:
+
+                @pl.when(owner[way])
+                def _():
+                    @pl.loop(0, count)
+                    def _(k):
+                        own_copy(k).wait()
+
     scratch = [
+        pltpu.VMEM((rows, width), BF16),
         pltpu.VMEM((2, count, chunk, width), BF16),
-        pltpu.VMEM((2, count, chunk, width), BF16),
-    ] + [pltpu.SemaphoreType.DMA((2, count)) for _ in range(4)]
-    if n_shards:
-        scratch += RingGather.scratch(n_shards, fsdp_size)
-    if n_grads:
-        scratch += RingScatter.buffers(scattered, fsdp_size) + RingScatter.scratch(n_grads, fsdp_size)
+        *[pltpu.SemaphoreType.DMA((2, count)) for _ in range(4)],
+        pltpu.SemaphoreType.DMA((max(1, len(operands)),)),
+        pltpu.SemaphoreType.DMA((max(1, len(halves)),)),
+        pltpu.SemaphoreType.DMA((count,)),
+        pltpu.SemaphoreType.DMA((2, groups)),
+        *[pltpu.VMEM((half, width), h.dtype) for h in halves],
+        *[pltpu.VMEM(o.shape, o.dtype) for o in operands],
+        *[pltpu.VMEM((half, width), F32)] * n_out,
+    ]
     return pl.pallas_call(
         kernel,
         out_shape=[jax.ShapeDtypeStruct((rows, width), BF16)]
-        + [jax.ShapeDtypeStruct(s, d) for s, d in extra_outs]
-        + [jax.ShapeDtypeStruct(s, BF16) for s in gathered]
-        + [jax.ShapeDtypeStruct(s, F32) for s in scattered],
-        in_specs=[WHOLE] * (1 + n_extra + n_shards) + [ANY] * n_grads,
-        out_specs=[WHOLE] * (1 + n_extra_out) + [ANY] * n_gathered + [WHOLE] * n_grads,
-        scratch_shapes=scratch,
+        + [jax.ShapeDtypeStruct((half, width), F32)] * n_out
+        + [jax.ShapeDtypeStruct((8, width), F32)]
+        + [shape for job in jobs for shape in job.out_shape],
+        in_specs=[ANY] * (not product) + [WHOLE] + [ANY] * (len(halves) + len(operands)) + [spec for job in jobs for spec in job.in_specs],
+        out_specs=[WHOLE] + [ANY] * n_out + [WHOLE] + [spec for job in jobs for spec in job.out_specs],
+        scratch_shapes=scratch + [shape for job in jobs for shape in job.scratch],
         compiler_params=pltpu.CompilerParams(
             collective_id=collective_id, has_side_effects=True, vmem_limit_bytes=VMEM_BYTES
         ),
         name=name,
-    )(part, *extras, *shards, *grads)
-
-
-def small_sum(vector, collective_id):
-    length = vector.shape[0]
-    rows = -(-length // 1024) * 8
-    block = jnp.pad(vector, (0, rows * 128 - length)).reshape(rows, 128)
-    axes = [(axis, lax.axis_size(axis)) for axis in ("ctx", "fsdp", "tp")]
-
-    def kernel(in_ref, out_ref, *scratch):
-        slots, sends, recvs = scratch[:3], scratch[3:6], scratch[6:9]
-        meet(
-            [
-                (None, {axis: lax.rem(lax.axis_index(axis) + step, size)})
-                for axis, size in axes
-                for step in range(1, size)
-            ]
-        )
-        total = in_ref[...]
-        for number, (axis, size) in enumerate(axes):
-            mine = lax.axis_index(axis)
-            slot = slots[number]
-            slot[mine] = total
-            copies = [
-                pltpu.make_async_remote_copy(
-                    src_ref=slot.at[mine],
-                    dst_ref=slot.at[mine],
-                    send_sem=sends[number].at[step - 1],
-                    recv_sem=recvs[number].at[step - 1],
-                    device_id={axis: lax.rem(mine + step, size)},
-                    device_id_type=BY_AXIS,
-                )
-                for step in range(1, size)
-            ]
-            for copy in copies:
-                copy.start()
-            for copy in copies:
-                copy.wait_recv()
-            total = slot[0]
-            for k in range(1, size):
-                total = total + slot[k]
-            for copy in copies:
-                copy.wait_send()
-        out_ref[...] = total
-
-    summed = pl.pallas_call(
-        kernel,
-        out_shape=jax.ShapeDtypeStruct((rows, 128), F32),
-        in_specs=[WHOLE],
-        out_specs=WHOLE,
-        scratch_shapes=[pltpu.VMEM((size, rows, 128), F32) for _, size in axes]
-        + [pltpu.SemaphoreType.DMA((size - 1,)) for _, size in axes] * 2,
-        compiler_params=pltpu.CompilerParams(collective_id=collective_id, has_side_effects=True),
-        name="small_sum",
-    )(block)
-    return summed.reshape(-1)[:length]
+    )(*([] if product else [part]), gain, *halves, *operands, *[array for job in jobs for array in job.inputs])
 
 
 def rms(value):
     return lax.rsqrt(jnp.mean(value * value, axis=-1, keepdims=True) + EPSILON)
 
 
-def middle_rows(extra, extra_out, rows, own, total):
-    x_ref, gain_ref = extra
-    middle = x_ref[rows, :].astype(F32) + total
-    extra_out[0][own, :] = middle
-    return (middle * rms(middle) * gain_ref[...]).astype(BF16)
-
-
-def norm_back(grad, value, gain):
+def middle_rows(halves, gain, own_ref, gain_part_ref, own, total):
+    middle = halves[0][own, :].astype(F32) + total
+    own_ref[own, :] = middle
+    return (middle * rms(middle) * gain).astype(BF16)
+
+
+def output_rows(halves, gain, own_ref, gain_part_ref, own, total):
+    return (halves[0][own, :] + total).astype(BF16)
+
+
+def norm_back(grad, value, gain, gain_part_ref):
     inverse = rms(value)
     scaled = value * inverse
     weighted = grad * gain
-    back = inverse * (weighted - scaled * jnp.mean(weighted * scaled, axis=-1, keepdims=True))
-    return back, jnp.sum(grad * scaled, axis=0, keepdims=True)
-
-
-def grad_middle_rows(extra, extra_out, rows, own, total):
-    middle_ref, grad_out_ref, gain_ref = extra
-    back, gain_part = norm_back(total, middle_ref[own, :], gain_ref[...])
-    grad_middle = grad_out_ref[rows, :].astype(F32) + back
-    extra_out[0][own, :] = grad_middle
-    add_rows(extra_out[1], own, gain_part)
+    gain_part_ref[0:1, :] += jnp.sum(grad * scaled, axis=0, keepdims=True)
+    return inverse * (weighted - scaled * jnp.mean(weighted * scaled, axis=-1, keepdims=True))
+
+
+def grad_middle_rows(halves, gain, own_ref, gain_part_ref, own, total):
+    back = norm_back(total, halves[0][own, :], gain, gain_part_ref)
+    grad_middle = halves[1][own, :].astype(F32) + back
+    own_ref[own, :] = grad_middle
     return grad_middle.astype(BF16)
 
 
-def input_grad_rows(extra, extra_out, rows, own, total):
-    x_ref, grad_middle_ref, gain_ref = extra
-    back, gain_part = norm_back(total, x_ref[rows, :].astype(F32), gain_ref[...])
-    add_rows(extra_out[0], own, gain_part)
-    return (grad_middle_ref[own, :] + back).astype(BF16)
-
-
-def add_rows(sum_ref, own, term):
-    sum_ref[pl.ds(own.start // own.size, 1), :] = term
+def input_grad_rows(halves, gain, own_ref, gain_part_ref, own, total):
+    back = norm_back(total, halves[0][own, :].astype(F32), gain, gain_part_ref)
+    return (halves[1][own, :] + back).astype(BF16)
 
 
 def lower_ones(length):
@@ -649,7 +1034,7 @@
 
 def mix_kernel(
     heads, length, valid_ref, query_ref, forget_ref, value_ref, gate_ref, gap_ref, gain_ref, start_ref,
-    gated_ref, mixed_ref, states_ref, state_ref,
+    gated_ref, mixed_ref, states_ref, end_ref, state_ref,
 ):
     index = pl.program_id(0)
 
@@ -676,6 +1061,10 @@
         state_ref[h] = growth * state + dot(values, (shrunk * growth).astype(BF16), TN)
         gate = gate_ref[:, cols]
         gated_ref[:, cols] = (mixed * rms(mixed) * gain_ref[...] * (gate * sigmoid(gate))).astype(BF16)
+
+    @pl.when(index == pl.num_programs(0) - 1)
+    def _():
+        end_ref[...] = state_ref[...]
 
 
 def span_begin_kernel(
@@ -828,22 +1217,14 @@
     half = rows // 2
 
     valid = jnp.clip(lengths - lax.axis_index("ctx") * span, 0, span).astype(jnp.int32)
-    keep = (jnp.arange(rows, dtype=jnp.int32) < valid[0])[:, None]
     x = inputs.reshape(rows, width)
-    grad_low = jnp.where(keep, cotangent.reshape(rows, width), jnp.zeros((), BF16))
     gap = forget_gap.reshape(1, local)
     head_row = head_gain.reshape(1, HEAD_DIM)
-
-    w_four, w_out = gather_weights(
-        [w_query, w_forget, w_input, w_outgate, w_output],
-        [(fsdp * w_query.shape[0], 4 * local), (local, width)],
-        [(0, 0, 0), (0, 0, local), (0, 0, 2 * local), (0, 0, 3 * local), (1, 1, 0)],
-        1,
+    norm_row, ffn_row = norm_gain.reshape(1, width), ffn_gain.reshape(1, width)
+
+    pre, normed, grad_low, w_four, w_out = project(
+        x, cotangent.reshape(rows, width), norm_row, valid, [w_query, w_forget, w_input, w_outgate], w_output, 1
     )
-
-    wide = x.astype(F32)
-    normed = (wide * rms(wide) * norm_gain).astype(BF16)
-    pre = dot(normed, w_four)
 
     def column(j):
         return pl.BlockSpec((length, local), lambda i, *_: (i, j))
@@ -863,37 +1244,34 @@
     )(valid, pre, pre, gap)
     span_decay = None
     if ctx > 2:
-        keep_rows = keep.astype(F32)
+        keep = (jnp.arange(rows, dtype=jnp.int32) < valid[0])[:, None]
         closing = jax.nn.sigmoid(-pre[:, local : 2 * local])
-        logs = jnp.log(1.0 - gap * closing) * keep_rows
+        logs = jnp.where(keep, jnp.log(1.0 - gap * closing), 0.0)
         span_decay = jnp.exp(jnp.sum(logs, axis=0)).reshape(heads, HEAD_DIM)
     start = from_earlier(local_end, span_decay, "ctx")
-    gated, mixed, states = plain_call(
+    gated, mixed, states, state_end = plain_call(
         functools.partial(mix_kernel, heads, length), "mix", (chunks,),
         [column(0), column(1), column(2), column(3), fixed((1, local)), fixed((1, HEAD_DIM)), fixed(state_shape)],
-        [column(0), column(0), pl.BlockSpec((1,) + state_shape, lambda i, *_: (i, 0, 0, 0))],
+        [column(0), column(0), pl.BlockSpec((1,) + state_shape, lambda i, *_: (i, 0, 0, 0)), fixed(state_shape)],
         [
             jax.ShapeDtypeStruct((rows, local), BF16),
             jax.ShapeDtypeStruct((rows, local), F32),
             jax.ShapeDtypeStruct((chunks,) + state_shape, F32),
+            jax.ShapeDtypeStruct(state_shape, F32),
         ],
         [pltpu.VMEM(state_shape, F32)], 6 * work, 6 * moved,
     )(valid, pre, pre, pre, pre, gap, head_row, start)
-    if ctx == 2:
-        keep_rows = keep.astype(F32)
-        closing = jax.nn.sigmoid(-pre[:, local : 2 * local])
-        logs = jnp.log(1.0 - gap * closing) * keep_rows
-        span_decay = jnp.exp(jnp.sum(logs, axis=0)).reshape(heads, HEAD_DIM)
-    state_end = local_end + span_decay[:, None, :] * start
-
-    branch = dot(gated, w_out).astype(BF16)
-    normed_two, middle, w_both, w_back = line_sum(
-        "sum_branch", branch, [x, ffn_gain.reshape(1, width)], [((half, width), F32)], middle_rows, 2,
-        gather=(
-            [w_gate, w_up, w_down],
-            [(fsdp * w_gate.shape[0], 2 * ff), (ff, width)],
-            [(0, 0, 0), (0, 0, ff), (1, 1, 0)],
-        ),
+
+    normed_two, middle, _, w_both, w_back = line_sum(
+        "sum_branch", (0, 1, NN), [x], ffn_row, 1, middle_rows, 2,
+        [
+            GatherJob(
+                [w_gate, w_up, w_down],
+                [(fsdp * w_gate.shape[0], 2 * ff), (ff, width)],
+                [(0, 0, 0), (0, 0, ff), (1, 1, 0)],
+            )
+        ],
+        [gated, w_out],
     )
 
     both = dot(normed_two, w_both)
@@ -901,35 +1279,35 @@
     sig = jax.nn.sigmoid(gate_hidden)
     act = gate_hidden * sig
     hidden = (act * up_hidden).astype(BF16)
-    mine = jnp.concatenate(
-        [jnp.where(place == 0, middle, 0.0), jnp.where(place == tp - 1, middle, 0.0)], axis=0
-    )
-    feed = (dot(hidden, w_back) + mine).astype(BF16)
-    result = lax.psum(feed, "tp").reshape(groups, span, width)
 
     grad_hidden = dot(grad_low, w_back, NT)
     grad_gate = (grad_hidden * up_hidden * slope(gate_hidden, sig)).astype(BF16)
     grad_up = (grad_hidden * act).astype(BF16)
     grad_both = jnp.concatenate([grad_gate, grad_up], axis=1)
-    part_two = dot(grad_both, w_both, NT).astype(BF16)
-    grad_w_down = dot(hidden, grad_low, TN).astype(BF16)
-    grad_w_both = dot(normed_two, grad_both, TN).astype(BF16)
+    result, _, part_two, grad_w_down, grad_w_both = line_sum(
+        "sum_feed", (0, 1, NN), [middle], ffn_row, 0, output_rows, 5,
+        [
+            ProductJob(2, 3, NT, (rows, width), min(128, rows)),
+            ProductJob(0, 4, TN, (ff, width), 128),
+            ProductJob(5, 2, TN, (width, 2 * ff), 256),
+        ],
+        [hidden, w_back, grad_both, w_both, grad_low, normed_two],
+    )
+    result = result.reshape(groups, span, width)
     both_axes = ("fsdp", "ctx")
 
     def scattered(grads, dims):
         if ctx == 2:
-            return (grads, dims), None
-        return None, [
+            return [ScatterJob(grads, dims)], None
+        return [], [
             lax.psum_scatter(g, both_axes, scatter_dimension=d, tiled=True).astype(F32) for g, d in zip(grads, dims)
         ]
 
     job, sums_ffn = scattered([grad_w_both, grad_w_down], [0, 1])
     grad_branch, grad_middle, ffn_gain_part, *more = line_sum(
-        "sum_norm_two", part_two, [middle, grad_low, ffn_gain.reshape(1, width)],
-        [((half, width), F32), ((half // min(32, half), width), F32)], grad_middle_rows, 3, scatter=job,
+        "sum_norm_two", part_two, [middle, grad_low], ffn_row, 1, grad_middle_rows, 3, job
     )
     out_both, out_down = sums_ffn or more
-
     grad_gated = dot(grad_branch, w_out, NT)
     grad_outgate, grad_mixed, head_part, local_begin = plain_call(
         functools.partial(span_begin_kernel, heads, length), "span_begin", (chunks,),
@@ -956,30 +1334,26 @@
     )(valid, grad_mixed, pre, pre, pre, gap, states, state_end, grad_end)
 
     grad_four = jnp.concatenate([grad_query, grad_forget, grad_value, grad_outgate], axis=1)
-    part_one = dot(grad_four, w_four, NT).astype(BF16)
-    grad_w_output = dot(gated, grad_branch, TN).astype(BF16)
-    grad_w_four = dot(normed, grad_four, TN).astype(BF16)
-    job, sums_mix = scattered([grad_w_four, grad_w_output], [0, 1])
-    input_grad, norm_gain_part, *more = line_sum(
-        "sum_norm_one", part_one, [x, grad_middle, norm_gain.reshape(1, width)],
-        [((half // min(32, half), width), F32)], input_grad_rows, 4, scatter=job,
+    owner = jnp.logical_or(place == 0, place == tp - 1)
+    gap_row = lax.dynamic_update_slice(jnp.zeros((tp * local,), F32), gap_part[0], (place * local,))
+    small = jnp.zeros((8, width), F32)
+    small = small.at[1].set(jnp.where(owner, ffn_gain_part[0], 0.0))
+    small = small.at[2, :HEAD_DIM].set(head_part[0]).at[3, : tp * local].set(gap_row)
+    jobs, operands, sums_mix = [VectorJob(small)], [grad_four, w_four], None
+    if ctx == 2:
+        shapes = [(width, 4 * local), (local, width)]
+        jobs.append(ProductScatterJob([(2, 0), (3, 4)], shapes, [0, 1]))
+        operands += [normed, gated, grad_branch]
+    else:
+        grads = [dot(normed, grad_four, TN).astype(BF16), dot(gated, grad_branch, TN).astype(BF16)]
+        _, sums_mix = scattered(grads, [0, 1])
+    input_grad, _, sums, *more = line_sum(
+        "sum_norm_one", (0, 1, NT), [x, grad_middle], norm_row, 0, input_grad_rows, 4, jobs, operands
     )
     out_four, out_output = sums_mix or more
     input_grad = input_grad.reshape(groups, span, width)
-
-    owner = jnp.logical_or(place == 0, place == tp - 1)
-    sums = jnp.concatenate(
-        [
-            jnp.where(owner, jnp.sum(norm_gain_part, axis=0), 0.0),
-            jnp.where(owner, jnp.sum(ffn_gain_part, axis=0), 0.0),
-            head_part[0],
-            lax.dynamic_update_slice(jnp.zeros((tp * local,), F32), gap_part[0], (place * local,)),
-        ]
-    )
-    sums = small_sum(sums, 5)
-    grad_norm_gain, grad_ffn_gain = sums[:width], sums[width : 2 * width]
-    grad_head_gain = sums[2 * width : 2 * width + HEAD_DIM]
-    grad_gap = lax.dynamic_slice(sums, (2 * width + HEAD_DIM + place * local,), (local,))
+    grad_norm_gain, grad_ffn_gain, grad_head_gain = sums[0], sums[1], sums[2, :HEAD_DIM]
+    grad_gap = lax.dynamic_slice(sums[3], (place * local,), (local,))
     return (
         result,
         input_grad,

time: 764 us -> 678 us (0.89)
  matrix products: 147 us -> 38.9 us
  Pallas kernels: 546 us -> 594 us
  between operations: 15.4 us -> 1.68 us
    dot_general x12 -> x3, matrix products: 147 us -> 38.9 us  [dot(): lax.dot_general(left, right, (dims, ((), ())), preferred_element_type=F32)]
    pallas_call x3 -> x4, Pallas kernels: 433 us -> 488 us  [line_sum(): pl.pallas_call(kernel, out_shape=[jax.ShapeDtypeStruct((rows, width), BF1...]
    concatenate x0 -> x2, other arithmetic: none -> 9.35 us  [the longest x1 5.55 us: per_device(): grad_both = jnp.concatenate([grad_gate, grad_up], axis=1)]
    pallas_call x2 -> x1, Pallas kernels: 64.1 us -> 55.7 us  [project(): pl.pallas_call(kernel, out_shape=[jax.ShapeDtypeStruct((rows, total), F32...]
    select_n x3 -> x1, other arithmetic: 8.93 us -> 0.85 us  [per_device(): small = small.at[1].set(jnp.where(owner, ffn_gain_part[0], 0.0))]
  transfers between devices with their start and end apart: 3 -> 2, of which waited for: 0 -> 1; matrix products, arithmetic and copies ran while one was open for 9% -> 1% of each run, Pallas kernels for 30% -> 0%
where the time goes in v3:
time: 678 us; the launch traced here: 671 us
  Pallas kernels  594 us (88%)
  matrix products  38.9 us (6%)
  local copies, waits for them, and re-layouts  21.8 us (3%)
  other arithmetic  10.2 us (2%)
    pallas_call x4, Pallas kernels, line_sum(): pl.pallas_call(kernel, out_shape=[jax.ShapeDtypeStruct((rows, width), BF1...  488 us
    pallas_call x1, Pallas kernels, project(): pl.pallas_call(kernel, out_shape=[jax.ShapeDtypeStruct((rows, total), F32...  55.7 us
    dot_general x3, matrix products, dot(): lax.dot_general(left, right, (dims, ((), ())), preferred_element_type=F32)  38.9 us
    pallas_call x1, Pallas kernels, per_device(): plain_call(functools.partial(mix_back_kernel, heads, length), 'mix_back',...  17 us
  transfers between devices with their start and end apart: 2, of which 1 were waited for; matrix products, arithmetic and copies ran while one was open for 1% of the time, Pallas kernels for 0%

profile of v3, /device:TPU:0, one launch (start us, length us, event | category | flops | bytes accessed | tf_op | source)
XLA Modules:
  0.0 671.2 jit_solution(1716657613405145795)
XLA Ops:
  1.3 55.7 %project.1 = (f32[1024,2048]{1,0:T(8,128)}, bf16[1024,2048]{1,0:T(8,128)(2,1)}, bf16[1024,2048]{1,0:T(8,128)(2,1)}, bf16[2048,2048]{1,0:T(8,128)(2,1)}, bf16[512,2048]{1,0:T(8,128)(2,1)}) custom-call(s32[1]{0:T(128)S(6)} %min.6.valid_ref, f32[1,2048]{1,0:T(1,128)} %bitcast.29, bf16[1024,2048]{1,0:T(8,128)(2,1)} %bitcast.20, bf16[1024,2048]{1,0:T(8,128)(2,1)} %bitcast.23, ...), custom_call_target="tpu_custom_call" | custom-call | tf_op jit(solution)/shard_map/project/pallas_call | solution.py:406
  57.1 9.7 %span_end.1 = f32[4,128,128]{2,1,0:T(8,128)} custom-call(s32[1]{0:T(128)S(6)} %min.6.valid_ref, f32[1024,2048]{1,0:T(8,128)} %get-tuple-element.84.forget_ref.value_ref.query_ref.gate_ref, f32[1024,2048]{1,0:T(8,128)} %get-tuple-element.84.forget_ref.value_ref.query_ref.gate_ref, f32[1,512]{1,0:T(1,128)} %bitcast.31), custom_call_target="tpu_custom_call" | custom-call | flops 402653184 | bytes 4194304 | tf_op jit(solution)/shard_map/span_end/pallas_call | solution.py:1240
  66.7 2.4 collective-permute-start
  69.1 0.8 collective-permute-done.start_ref
  69.9 12.9 %mix.1 = (bf16[1024,512]{1,0:T(8,128)(2,1)}, f32[1024,512]{1,0:T(8,128)}, f32[8,4,128,128]{3,2,1,0:T(8,128)}, f32[4,128,128]{2,1,0:T(8,128)}) custom-call(s32[1]{0:T(128)S(6)} %min.6.valid_ref, f32[1024,2048]{1,0:T(8,128)} %get-tuple-element.84.forget_ref.value_ref.query_ref.gate_ref, f32[1024,2048]{1,0:T(8,128)} %get-tuple-element.84.forget_ref.value_ref.query_ref.gate_ref, ...), custom_call_target="tpu_custom_call" | custom-call | flops 805306368 | bytes 12582912 | tf_op jit(solution)/shard_map/mix/pallas_call | solution.py:1252
  82.8 121.5 %sum_branch.1 = (bf16[1024,2048]{1,0:T(8,128)(2,1)}, f32[512,2048]{1,0:T(8,128)}, f32[8,2048]{1,0:T(8,128)}, bf16[2048,2816]{1,0:T(8,128)(2,1)}, bf16[1408,2048]{1,0:T(8,128)(2,1)}) custom-call(f32[1,2048]{1,0:T(1,128)} %bitcast.26, bf16[1024,2048]{1,0:T(8,128)(2,1)} %bitcast.21, bf16[1024,512]{1,0:T(8,128)(2,1)} %get-tuple-element.85.refs_2_.refs_6_, ...), custom_call_target="tpu_custom_call" | custom-call | tf_op jit(solution)/shard_map/sum_branch/pallas_call | solution.py:948
  204.3 0.0 copy-start
  204.3 0.0 copy-start.1
  204.3 18.8 %fusion.4 = f32[1024,2816]{1,0:T(8,128)} fusion(bf16[1024,2048]{1,0:T(8,128)(2,1)} %get-tuple-element.88.refs_7_, bf16[2048,2816]{1,0:T(8,128)(2,1)} %get-tuple-element.89.refs_5_), kind=kOutput, calls=%fused_computation.14 | convolution fusion | flops 11811160064 | bytes 27262976 | tf_op jit(solution)/shard_map/dot_general | solution.py:21
  223.1 0.0 copy-done
  223.1 0.0 copy-done.1
  223.1 13.5 %multiply_convert_fusion.1 = (bf16[1024,1408]{1,0:T(8,128)(2,1)}, bf16[1024,1408]{1,0:T(8,128)(2,1)}, bf16[1024,1408]{1,0:T(8,128)(2,1)}) fusion(f32[1024,2816]{1,0:T(8,128)} %fusion.4, bf16[1024,2048]{1,0:T(8,128)(2,1)S(1)} %copy-done, bf16[1408,2048]{1,0:T(8,128)(2,1)S(1)} %copy-done.1), kind=kOutput, calls=%fused_computation.2 | convolution fusion | flops 5927206912 | bytes 30146560 | tf_op jit(solution)/shard_map/dot_general | solution.py:21
  236.6 5.6 pad_maximum_fusion.refs_4_
  242.2 119.2 %sum_feed.1 = (bf16[1024,2048]{1,0:T(8,128)(2,1)}, f32[8,2048]{1,0:T(8,128)}, bf16[1024,2048]{1,0:T(8,128)(2,1)}, bf16[1408,2048]{1,0:T(8,128)(2,1)}, bf16[2048,2816]{1,0:T(8,128)(2,1)}) custom-call(f32[1,2048]{1,0:T(1,128)} %bitcast.27, f32[512,2048]{1,0:T(8,128)} %get-tuple-element.87.refs_1_.refs_2_, bf16[1024,1408]{1,0:T(8,128)(2,1)} %get-tuple-element.120.refs_2_, ...), custom_call_target="tpu_custom_call" | custom-call | tf_op jit(solution)/shard_map/sum_feed/pallas_call | solution.py:948
  361.4 113.4 %sum_norm_two.1 = (bf16[1024,2048]{1,0:T(8,128)(2,1)}, f32[512,2048]{1,0:T(8,128)}, f32[8,2048]{1,0:T(8,128)}, f32[256,2816]{1,0:T(8,128)}, f32[1408,256]{1,0:T(8,128)}) custom-call(bf16[1024,2048]{1,0:T(8,128)(2,1)} %get-tuple-element.93.refs_0_, f32[1,2048]{1,0:T(1,128)} %bitcast.28, f32[512,2048]{1,0:T(8,128)} %get-tuple-element.87.refs_1_.refs_2_, ...), custom_call_target="tpu_custom_call" | custom-call | tf_op jit(solution)/shard_map/sum_norm_two/pallas_call | solution.py:948
  474.7 6.6 fusion.5.grad_ref
  481.3 10.6 %span_begin.1 = (bf16[1024,512]{1,0:T(8,128)(2,1)}, bf16[1024,512]{1,0:T(8,128)(2,1)}, f32[1,128]{1,0:T(1,128)}, f32[4,128,128]{2,1,0:T(8,128)}) custom-call(s32[1]{0:T(128)S(6)} %min.6.valid_ref, f32[1024,512]{1,0:T(8,128)} %fusion.5.grad_ref, f32[1024,512]{1,0:T(8,128)} %get-tuple-element.98.mixed_ref, ...), custom_call_target="tpu_custom_call" | custom-call | flops 402653184 | bytes 12582912 | tf_op jit(solution)/shard_map/span_begin/pallas_call | solution.py:1312
  491.9 0.0 copy-start.6
  492.0 1.3 collective-permute-start.1
  493.3 3.6 fusion.1
  496.8 0.8 broadcast_select_fusion
  497.7 0.6 scatter.10
  498.3 0.0 copy-done.6
  498.3 1.3 scatter.11
  499.6 0.0 collective-permute-done.1.end_ref
  499.6 17.0 %mix_back.1 = (bf16[1024,512]{1,0:T(8,128)(2,1)}, bf16[1024,512]{1,0:T(8,128)(2,1)}, bf16[1024,512]{1,0:T(8,128)(2,1)}, f32[1,512]{1,0:T(1,128)}) custom-call(s32[1]{0:T(128)S(6)} %min.6.valid_ref, bf16[1024,512]{1,0:T(8,128)(2,1)} %get-tuple-element.99.grad_ref, f32[1024,2048]{1,0:T(8,128)} %get-tuple-element.84.forget_ref.value_ref.query_ref.gate_ref, ...), custom_call_target="tpu_custom_call" | custom-call | flops 1610612736 | bytes 12582912 | tf_op jit(solution)/shard_map/mix_back/pallas_call | solution.py:1326
  516.7 0.7 constant_dynamic-update-slice_fusion
  517.4 1.5 scatter.14.refs_8_
  518.9 3.8 pad_maximum_fusion.1.refs_3_
  522.7 134.2 %sum_norm_one.1 = (bf16[1024,2048]{1,0:T(8,128)(2,1)}, f32[8,2048]{1,0:T(8,128)}, f32[8,2048]{1,0:T(8,128)}, f32[256,2048]{1,0:T(8,128)}, f32[512,256]{1,0:T(8,128)}) custom-call(f32[1,2048]{1,0:T(1,128)} %bitcast.30, bf16[1024,2048]{1,0:T(8,128)(2,1)} %bitcast.22, f32[512,2048]{1,0:T(8,128)} %get-tuple-element.96.refs_2_, ...), custom_call_target="tpu_custom_call" | custom-call | tf_op jit(solution)/shard_map/sum_norm_one/pallas_call | solution.py:948
  656.9 0.0 copy-start.2
  656.9 1.7 fusion.3
  658.5 1.2 slice_bitcast_fusion
  659.7 2.9 fusion.2
  662.6 0.6 constant_dynamic-slice_fusion
  663.2 0.0 copy-done.2
  663.2 0.0 copy-start.3
  663.2 2.1 copy.37
  665.3 1.6 copy-done.3
  666.9 0.0 copy-start.5
  666.9 0.0 copy-start.4
  666.9 2.1 copy.38
  669.0 0.0 copy-done.5
  669.0 0.8 copy.39
  669.8 0.1 copy-done.4
  669.8 1.1 copy.40
  (1 shorter events, 0.0 us)
Async XLA Ops:
  66.7 3.1 collective-permute-start
  204.3 18.8 %copy-start = (bf16[1024,2048]{1,0:T(8,128)(2,1)S(1)}, bf16[1024,2048]{1,0:T(8,128)(2,1)}, u32[]{:S(2)}) copy-start(bf16[1024,2048]{1,0:T(8,128)(2,1)} %get-tuple-element.91.refs_6_.refs_3_) | copy-start | bytes 12582916
  204.3 18.8 %copy-start.1 = (bf16[1408,2048]{1,0:T(8,128)(2,1)S(1)}, bf16[1408,2048]{1,0:T(8,128)(2,1)}, u32[]{:S(2)}) copy-start(bf16[1408,2048]{1,0:T(8,128)(2,1)} %get-tuple-element.90.refs_3_) | copy-start | bytes 17301508
  491.9 6.4 copy-start.6
  492.0 7.7 %collective-permute-start.1 = (f32[4,128,128]{2,1,0:T(8,128)}, f32[4,128,128]{2,1,0:T(8,128)}, u32[]{:S(2)}, u32[]{:S(2)}) collective-permute-start(f32[4,128,128]{2,1,0:T(8,128)} %get-tuple-element.102), channel_id=1, source_target_pairs={{4,0},{5,1},{6,2},{7,3},{12,8},{13,9},{14,10},{15,11},{20,16},{21,... | collective-permute-start | bytes 786440 | tf_op jit(solution)/shard_map/ppermute | solution.py:1194
  656.9 6.3 copy-start.2
  663.2 3.7 copy-start.3
  666.9 2.1 copy-start.5
  666.9 3.0 copy-start.4

commit v4 on v3

--- a/solution.py
+++ b/solution.py
@@ -320,6 +320,7 @@
     half = deep // 2
     tile = min(512, total)
     step_rows = min(64, rows)
+    row_tile = min(512, rows)
     copies = 1 + 2 * (size - 1)
 
     def kernel(
@@ -365,8 +366,13 @@
             def _(n):
                 cols = pl.ds(pl.multiple_of(n * tile, tile), tile)
                 deep_at = pl.ds(start, length)
-                term = dot(normed[:, deep_at], four[deep_at, cols])
-                acc[:, cols] = term if first else acc[:, cols] + term
+
+                @pl.loop(0, rows // row_tile)
+                def _(r):
+                    at = pl.ds(pl.multiple_of(r * row_tile, row_tile), row_tile)
+                    term = dot(normed[at, deep_at], four[deep_at, cols])
+                    acc[at, cols] = term if first else acc[at, cols] + term
+
                 if last:
                     save_pre(n).start()
 
@@ -528,13 +534,25 @@
 
 def product_tile(left, right, dims, where, out):
     rows = left[:, where].T if dims == TN else left[where, :]
-    width = out.shape[-1]
-    for start in range(0, width, 512):
-        cols = slice(start, min(start + 512, width))
+
+    def act(cols):
         if dims == NT:
             out[:, cols] = dot(rows, right[cols, :], NT).astype(out.dtype)
         else:
             out[:, cols] = dot(rows, right[:, cols]).astype(out.dtype)
+
+    by_columns(out.shape[-1], act)
+
+
+def by_columns(width, act):
+    step = min(512, width)
+
+    @pl.loop(0, width // step)
+    def _(n):
+        act(pl.ds(pl.multiple_of(n * step, step), step))
+
+    if width % step:
+        act(pl.ds(width - width % step, width % step))
 
 
 class ProductScatterJob(ScatterJob):
@@ -594,17 +612,197 @@
             job.across(i, offset).start()
 
 
+class MixBackJob:
+    def __init__(self, valid, grad_branch, w_out, mixed, pre, states, gap, gain, state_end):
+        self.rows, self.width = grad_branch.shape
+        self.local = w_out.shape[0]
+        self.chunks, self.heads = states.shape[:2]
+        self.length = self.rows // self.chunks
+        self.inputs = [valid, grad_branch, w_out, mixed, pre, states, gap, gain, state_end]
+        self.in_specs = [pl.BlockSpec(memory_space=pltpu.SMEM)] + [ANY] * 5 + [WHOLE] * 3
+        self.out_shape = [jax.ShapeDtypeStruct((self.rows, self.local), BF16)] * 4 + [
+            jax.ShapeDtypeStruct((1, self.local), F32),
+            jax.ShapeDtypeStruct((1, HEAD_DIM), F32),
+        ]
+        self.out_specs = [ANY] * 4 + [WHOLE] * 2
+        state = states.shape[1:]
+        self.scratch = [
+            pltpu.VMEM(w_out.shape, BF16),
+            pltpu.VMEM((2, self.length, self.width), BF16),
+            pltpu.VMEM((2, self.length, self.local), F32),
+            pltpu.VMEM((2, self.length, 4 * self.local), F32),
+            pltpu.VMEM((2,) + state, F32),
+            pltpu.VMEM((self.length, self.local), F32),
+            pltpu.VMEM((self.rows, self.local), BF16),
+            *[pltpu.VMEM(state, F32)] * 4,
+            pltpu.VMEM((2, 4, self.length, self.local), BF16),
+            pltpu.SemaphoreType.DMA((2, 4)),
+            pltpu.SemaphoreType.DMA((2, 4)),
+            pltpu.SemaphoreType.DMA((3,)),
+        ]
+
+    def bind(self, ins, outs, scratch):
+        self.valid, self.grad_branch, self.w_out, self.mixed, self.pre, self.states, self.gap, self.gain, self.last = ins
+        self.outs, (self.gap_part, self.gain_part) = outs[:4], outs[4:]
+        self.w_here, self.grad_here, self.mixed_here, self.pre_here, self.states_here = scratch[:5]
+        self.gated, self.grad_mixed, self.begin, self.came, self.flow, self.after = scratch[5:11]
+        self.stage, self.in_sem, self.out_sem, self.sem = scratch[11:]
+        self.core = lax.axis_index("ctx")
+
+    def peers(self):
+        return [{"ctx": 1 - self.core}]
+
+    def cuts(self, steps):
+        return []
+
+    def w_copy(self):
+        return pltpu.make_async_copy(self.w_out, self.w_here, self.sem.at[0])
+
+    def across(self):
+        return pltpu.make_async_remote_copy(
+            src_ref=self.begin,
+            dst_ref=self.came,
+            send_sem=self.sem.at[1],
+            recv_sem=self.sem.at[2],
+            device_id={"ctx": 1 - self.core},
+            device_id_type=BY_AXIS,
+        )
+
+    def where(self, i):
+        return pl.ds(pl.multiple_of((self.chunks - 1 - i) * self.length, self.length), self.length)
+
+    def loads(self, phase, i):
+        slot = i % 2
+        copies = [pltpu.make_async_copy(self.pre.at[self.where(i), :], self.pre_here.at[slot], self.in_sem.at[slot, 0])]
+        if phase == 0:
+            whole = (self.grad_branch, self.grad_here, 1), (self.mixed, self.mixed_here, 2)
+            for source, here, n in whole:
+                copies.append(
+                    pltpu.make_async_copy(source.at[self.where(i), :], here.at[slot], self.in_sem.at[slot, n])
+                )
+        else:
+            copies.append(
+                pltpu.make_async_copy(
+                    self.states.at[self.chunks - 1 - i], self.states_here.at[slot], self.in_sem.at[slot, 3]
+                )
+            )
+        return copies
+
+    def begin_loads(self, phase, i):
+        for copy in self.loads(phase, i):
+            copy.start()
+
+    def end_loads(self, phase, i):
+        for copy in self.loads(phase, i):
+            copy.wait()
+
+    def save(self, k, i):
+        slot = i % 2
+        return pltpu.make_async_copy(
+            self.stage.at[slot, k], self.outs[k].at[self.where(i), :], self.out_sem.at[slot, k]
+        )
+
+    def start(self):
+        self.w_copy().start()
+        for i in range(2):
+            self.begin_loads(0, i)
+
+    def tasks(self):
+        return [(self.chunks, self.act_begin, ()), (1, lambda i: None, ()), (2 * self.chunks, self.act_back, ())]
+
+    def column(self, slot, k, start=0, wide=None):
+        return self.pre_here.at[slot, :, pl.ds(k * self.local + start, wide or self.local)]
+
+    def act_begin(self, i):
+        slot = i % 2
+
+        @pl.when(i == 0)
+        def _():
+            self.w_copy().wait()
+
+        self.end_loads(0, i)
+
+        @pl.when(i >= 2)
+        def _():
+            self.save(3, i - 2).wait()
+
+        self.gated[...] = dot(self.grad_here[slot], self.w_here[...], NT)
+        span_begin_chunk(
+            self.heads, self.length, i, self.chunks, self.valid, self.gated, self.mixed_here.at[slot],
+            self.column(slot, 0), self.column(slot, 1), self.column(slot, 3), self.gap, self.gain,
+            self.stage.at[slot, 3], self.grad_mixed.at[self.where(i), :], self.gain_part, self.begin,
+        )
+        self.save(3, i).start()
+
+        @pl.when(i + 2 < self.chunks)
+        def _():
+            self.begin_loads(0, i + 2)
+
+        @pl.when(i + 2 >= self.chunks)
+        def _():
+            self.begin_loads(1, i + 2 - self.chunks)
+
+        @pl.when(i == self.chunks - 1)
+        def _():
+            self.across().start()
+
+    def act_back(self, t):
+        i, part = t // 2, t % 2
+        slot = i % 2
+
+        @pl.when(t == 0)
+        def _():
+            self.across().wait_recv()
+            self.came[...] = jnp.where(self.core == 0, self.came[...], 0.0)
+
+        @pl.when(part == 0)
+        def _():
+            self.end_loads(1, i)
+
+            @pl.when(i >= 2)
+            def _():
+                for k in range(3):
+                    self.save(k, i - 2).wait()
+
+        heads, wide = self.heads // 2, self.local // 2
+        start = pl.multiple_of(part * wide, HEAD_DIM)
+        cols, some = pl.ds(start, wide), pl.ds(part * heads, heads)
+        mix_back_chunk(
+            heads, self.length, i, self.chunks, self.valid, self.grad_mixed.at[self.where(i), cols],
+            *[self.column(slot, k, start, wide) for k in range(3)], self.gap.at[:, cols],
+            self.states_here.at[pl.ds(slot, 1), some], self.last.at[some], self.came.at[some],
+            *[self.stage.at[slot, k, :, cols] for k in range(3)],
+            self.gap_part.at[:, cols], self.flow.at[some], self.after.at[some],
+        )
+
+        @pl.when(part == 1)
+        def _():
+            for k in range(3):
+                self.save(k, i).start()
+
+            @pl.when(i + 2 < self.chunks)
+            def _():
+                self.begin_loads(1, i + 2)
+
+    def finish(self):
+        for i in range(self.chunks - 2, self.chunks):
+            for k in range(4):
+                self.save(k, i).wait()
+        self.across().wait_send()
+
+
 class VectorJob:
-    def __init__(self, others):
+    def __init__(self, full, short, split):
         self.axes = [(axis, lax.axis_size(axis)) for axis in ("ctx", "fsdp", "tp")]
-        self.inputs, self.in_specs = [others], [WHOLE]
-        self.out_shape, self.out_specs = [jax.ShapeDtypeStruct(others.shape, F32)], [WHOLE]
-        self.scratch = [pltpu.VMEM((size,) + others.shape, F32) for _, size in self.axes] + [
+        self.inputs, self.in_specs = [full, short, split], [WHOLE] * 3
+        self.out_shape, self.out_specs = [jax.ShapeDtypeStruct(full.shape, F32)], [WHOLE]
+        self.scratch = [pltpu.VMEM((size,) + full.shape, F32) for _, size in self.axes] + [
             pltpu.SemaphoreType.DMA((size - 1,)) for _, size in self.axes
         ] * 2
 
     def bind(self, ins, outs, scratch):
-        self.others, self.out = ins[0], outs[0]
+        self.full, self.short, self.split = ins
+        (self.out,) = outs
         self.slots, self.sends, self.recvs = scratch[:3], scratch[3:6], scratch[6:]
 
     def peers(self):
@@ -638,7 +836,12 @@
 
     def advance(self, number):
         if number == 0:
-            total = self.others[...] + self.extra()
+            mine = lax.axis_index(self.axes[0][0])
+            slot, local = self.slots[0], self.split.shape[1]
+            slot[mine] = self.extra()
+            slot[mine, 1:2, :] = self.full[0:1, :]
+            slot[mine, 2:3, : self.short.shape[1]] = self.short[...]
+            slot[mine, 3:4, pl.ds(pl.multiple_of(lax.axis_index("tp") * local, local), local)] = self.split[...]
         else:
             for copy in self.copies(number - 1):
                 copy.wait_recv()
@@ -649,7 +852,8 @@
         if number == len(self.axes):
             self.out[...] = total
             return
-        self.slots[number][lax.axis_index(self.axes[number][0])] = total
+        if number > 0:
+            self.slots[number][lax.axis_index(self.axes[number][0])] = total
         for copy in self.copies(number):
             copy.start()
 
@@ -664,10 +868,13 @@
 ):
     size = lax.axis_size("tp")
     product = isinstance(part, tuple)
+    operands = [o if isinstance(o, tuple) else (o,) for o in operands]
+    operand_shapes = [(o[0].shape[0], sum(p.shape[1] for p in o)) for o in operands]
+    pieces = [p for o in operands for p in o]
     if product:
         left_at, right_at, part_dims = part
-        rows = operands[left_at].shape[0]
-        width = operands[right_at].shape[1 - part_dims[1][0]]
+        rows = operand_shapes[left_at][0]
+        width = operand_shapes[right_at][1 - part_dims[1][0]]
     else:
         rows, width = part.shape
     half = rows // 2
@@ -688,7 +895,7 @@
 
         part_refs, (gain_ref,) = take(0 if product else 1), take(1)
         half_refs = take(len(halves))
-        operand_refs = take(len(operands))
+        operand_refs = take(len(pieces))
         job_ins = [take(len(job.inputs)) for job in jobs]
         (out_ref,) = take(1)
         own_refs = take(n_out)
@@ -709,13 +916,18 @@
 
         loaded = set()
 
-        def operand_copy(i):
-            return pltpu.make_async_copy(operand_refs[i], operand_here[i], operand_sem.at[i])
+        def operand_copies(i):
+            first, column = sum(len(o) for o in operands[:i]), 0
+            for n, piece in enumerate(operands[i], first):
+                where = operand_here[i].at[:, pl.ds(column, piece.shape[1])]
+                yield pltpu.make_async_copy(operand_refs[n], where, operand_sem.at[n])
+                column += piece.shape[1]
 
         def need(places):
             for i in places:
                 if i not in loaded:
-                    operand_copy(i).wait()
+                    for copy in operand_copies(i):
+                        copy.wait()
                     loaded.add(i)
 
         def half_copy(way, i):
@@ -734,16 +946,13 @@
                     def _():
                         part_copy(way, g).start()
 
-        for i in range(len(operands)):
-            operand_copy(i).start()
-
-        for way in range(2):
-
-            @pl.when(owner[way])
-            def _():
-                for i in range(len(halves)):
-                    half_copy(way, i).start()
-
+        def load(places):
+            for i in places:
+                for copy in operand_copies(i):
+                    copy.start()
+
+        early = (left_at, right_at) if product else ()
+        load(early)
         for ins, outs, scratch, job in zip(job_ins, job_outs, job_scratch, jobs):
             job.operands = operand_here
             job.bind(ins, outs, scratch)
@@ -779,7 +988,7 @@
             return pltpu.make_async_copy(own_here[0].at[where, :], own_refs[0].at[where, :], own_sem.at[k])
 
         def part_rows(j):
-            way, g = j % 2, j // 2
+            way, g = lax.rem(j + jnp.where(place < size // 2, 0, 1), 2), j // 2
             where = pl.ds(pl.multiple_of((1 - way) * half + g * group, group), group)
             left = operand_here[left_at][where, :]
             for start in range(0, width, 512):
@@ -796,14 +1005,17 @@
                         onward(w, g * per_group + k, True).start()
 
         tasks, at_step = [], 0
+        need(early)
+        load([i for i in range(len(operands)) if i not in early])
+        for way in range(2):
+
+            @pl.when(owner[way])
+            def _():
+                for i in range(len(halves)):
+                    half_copy(way, i).start()
+
         if product:
-            need((left_at, right_at))
-
-            @pl.loop(0, 2)
-            def _(j):
-                part_rows(j)
-
-            tasks, at_step = [(0, 2 * groups - 2, lambda i: part_rows(i + 2), ())], 2 * groups - 2
+            tasks, at_step = [(-2, 2 * groups, part_rows, ())], 2 * groups - 2
         else:
             for way in range(2):
 
@@ -881,7 +1093,8 @@
         acts = sorted((cut, n, i) for n, job in enumerate(jobs) for i, cut in enumerate(job.cuts(steps)))
         bounds = {t[0] for t in tasks} | {t[0] + t[1] for t in tasks}
         for number, (act, lead) in enumerate([(add, away), (spread, (away[1], away[0]))]):
-            low, high = number * steps, (number + 1) * steps
+            base_step, high = number * steps, (number + 1) * steps
+            low = min([base_step] + [t[0] for t in tasks if number == 0])
             here = [a for a in acts if low <= a[0] < high]
             edges = sorted({low, high} | {a[0] for a in here} | {e for e in bounds if low < e < high})
             for left, right in zip(edges[:-1], edges[1:]):
@@ -892,11 +1105,11 @@
                 for t in active:
                     need(t[3])
 
-                @pl.loop(left - low, right - low)
+                @pl.loop(left - base_step, right - base_step)
                 def _(step):
                     each_way(step, lead, act)
                     for t in active:
-                        t[2](step + low - t[0])
+                        t[2](step + base_step - t[0])
 
         for first_step, tiles, act, needs in tasks:
             done = min(max(2 * steps - first_step, 0), tiles)
@@ -937,12 +1150,12 @@
         pltpu.VMEM((rows, width), BF16),
         pltpu.VMEM((2, count, chunk, width), BF16),
         *[pltpu.SemaphoreType.DMA((2, count)) for _ in range(4)],
-        pltpu.SemaphoreType.DMA((max(1, len(operands)),)),
+        pltpu.SemaphoreType.DMA((max(1, len(pieces)),)),
         pltpu.SemaphoreType.DMA((max(1, len(halves)),)),
         pltpu.SemaphoreType.DMA((count,)),
         pltpu.SemaphoreType.DMA((2, groups)),
         *[pltpu.VMEM((half, width), h.dtype) for h in halves],
-        *[pltpu.VMEM(o.shape, o.dtype) for o in operands],
+        *[pltpu.VMEM(shape, o[0].dtype) for shape, o in zip(operand_shapes, operands)],
         *[pltpu.VMEM((half, width), F32)] * n_out,
     ]
     return pl.pallas_call(
@@ -951,14 +1164,14 @@
         + [jax.ShapeDtypeStruct((half, width), F32)] * n_out
         + [jax.ShapeDtypeStruct((8, width), F32)]
         + [shape for job in jobs for shape in job.out_shape],
-        in_specs=[ANY] * (not product) + [WHOLE] + [ANY] * (len(halves) + len(operands)) + [spec for job in jobs for spec in job.in_specs],
+        in_specs=[ANY] * (not product) + [WHOLE] + [ANY] * (len(halves) + len(pieces)) + [spec for job in jobs for spec in job.in_specs],
         out_specs=[WHOLE] + [ANY] * n_out + [WHOLE] + [spec for job in jobs for spec in job.out_specs],
         scratch_shapes=scratch + [shape for job in jobs for shape in job.scratch],
         compiler_params=pltpu.CompilerParams(
             collective_id=collective_id, has_side_effects=True, vmem_limit_bytes=VMEM_BYTES
         ),
         name=name,
-    )(*([] if product else [part]), gain, *halves, *operands, *[array for job in jobs for array in job.inputs])
+    )(*([] if product else [part]), gain, *halves, *pieces, *[array for job in jobs for array in job.inputs])
 
 
 def rms(value):
@@ -1067,12 +1280,15 @@
         end_ref[...] = state_ref[...]
 
 
-def span_begin_kernel(
-    heads, length, valid_ref, grad_ref, mixed_ref, query_ref, forget_ref, gate_ref, gap_ref, gain_ref,
+def span_begin_kernel(heads, length, *refs):
+    span_begin_chunk(heads, length, pl.program_id(0), pl.num_programs(0), *refs)
+
+
+def span_begin_chunk(
+    heads, length, step, steps, valid_ref, grad_ref, mixed_ref, query_ref, forget_ref, gate_ref, gap_ref, gain_ref,
     grad_gate_ref, grad_mixed_ref, gain_part_ref, begin_ref,
 ):
-    step = pl.program_id(0)
-    index = pl.num_programs(0) - 1 - step
+    index = steps - 1 - step
 
     @pl.when(step == 0)
     def _():
@@ -1104,12 +1320,15 @@
         begin_ref[h] = growth * begin_ref[h] + dot(grad_mixed, queries, TN)
 
 
-def mix_back_kernel(
-    heads, length, valid_ref, grad_ref, query_ref, forget_ref, value_ref, gap_ref, states_ref, last_ref, end_ref,
-    grad_query_ref, grad_forget_ref, grad_value_ref, gap_part_ref, flow_ref, after_ref,
+def mix_back_kernel(heads, length, *refs):
+    mix_back_chunk(heads, length, pl.program_id(0), pl.num_programs(0), *refs)
+
+
+def mix_back_chunk(
+    heads, length, step, steps, valid_ref, grad_ref, query_ref, forget_ref, value_ref, gap_ref, states_ref, last_ref,
+    end_ref, grad_query_ref, grad_forget_ref, grad_value_ref, gap_part_ref, flow_ref, after_ref,
 ):
-    step = pl.program_id(0)
-    index = pl.num_programs(0) - 1 - step
+    index = steps - 1 - step
 
     @pl.when(step == 0)
     def _():
@@ -1214,7 +1433,6 @@
     length = min(128, span)
     chunks = span // length
     place = lax.axis_index("tp")
-    half = rows // 2
 
     valid = jnp.clip(lengths - lax.axis_index("ctx") * span, 0, span).astype(jnp.int32)
     x = inputs.reshape(rows, width)
@@ -1283,17 +1501,6 @@
     grad_hidden = dot(grad_low, w_back, NT)
     grad_gate = (grad_hidden * up_hidden * slope(gate_hidden, sig)).astype(BF16)
     grad_up = (grad_hidden * act).astype(BF16)
-    grad_both = jnp.concatenate([grad_gate, grad_up], axis=1)
-    result, _, part_two, grad_w_down, grad_w_both = line_sum(
-        "sum_feed", (0, 1, NN), [middle], ffn_row, 0, output_rows, 5,
-        [
-            ProductJob(2, 3, NT, (rows, width), min(128, rows)),
-            ProductJob(0, 4, TN, (ff, width), 128),
-            ProductJob(5, 2, TN, (width, 2 * ff), 256),
-        ],
-        [hidden, w_back, grad_both, w_both, grad_low, normed_two],
-    )
-    result = result.reshape(groups, span, width)
     both_axes = ("fsdp", "ctx")
 
     def scattered(grads, dims):
@@ -1303,49 +1510,56 @@
             lax.psum_scatter(g, both_axes, scatter_dimension=d, tiled=True).astype(F32) for g, d in zip(grads, dims)
         ]
 
-    job, sums_ffn = scattered([grad_w_both, grad_w_down], [0, 1])
-    grad_branch, grad_middle, ffn_gain_part, *more = line_sum(
-        "sum_norm_two", part_two, [middle, grad_low], ffn_row, 1, grad_middle_rows, 3, job
+    grad_branch, grad_middle, ffn_gain_part, grad_w_down, grad_w_both = line_sum(
+        "sum_norm_two", (0, 1, NT), [middle, grad_low], ffn_row, 1, grad_middle_rows, 3,
+        [ProductJob(2, 3, TN, (ff, width), 128), ProductJob(4, 0, TN, (width, 2 * ff), 128)],
+        [(grad_gate, grad_up), w_both, hidden, grad_low, normed_two],
     )
-    out_both, out_down = sums_ffn or more
-    grad_gated = dot(grad_branch, w_out, NT)
-    grad_outgate, grad_mixed, head_part, local_begin = plain_call(
-        functools.partial(span_begin_kernel, heads, length), "span_begin", (chunks,),
-        [column_back(0), column_back(0), column_back(0), column_back(1), column_back(3), fixed((1, local)),
-         fixed((1, HEAD_DIM))],
-        [column_back(0), column_back(0), fixed((1, HEAD_DIM)), fixed(state_shape)],
-        [
-            jax.ShapeDtypeStruct((rows, local), BF16),
-            jax.ShapeDtypeStruct((rows, local), BF16),
-            jax.ShapeDtypeStruct((1, HEAD_DIM), F32),
-            jax.ShapeDtypeStruct(state_shape, F32),
-        ],
-        [], 3 * work, 6 * moved,
-    )(valid, grad_gated, mixed, pre, pre, pre, gap, head_row)
-    grad_end = from_later(local_begin, span_decay, "ctx")
-    grad_query, grad_forget, grad_value, gap_part = plain_call(
-        functools.partial(mix_back_kernel, heads, length), "mix_back", (chunks,),
-        [column_back(0), column_back(0), column_back(1), column_back(2), fixed((1, local)),
-         pl.BlockSpec((1,) + state_shape, lambda i, *_: (chunks - 1 - i, 0, 0, 0)), fixed(state_shape),
-         fixed(state_shape)],
-        [column_back(0), column_back(0), column_back(0), fixed((1, local))],
-        [jax.ShapeDtypeStruct((rows, local), BF16)] * 3 + [jax.ShapeDtypeStruct((1, local), F32)],
-        [pltpu.VMEM(state_shape, F32), pltpu.VMEM(state_shape, F32)], 12 * work, 6 * moved,
-    )(valid, grad_mixed, pre, pre, pre, gap, states, state_end, grad_end)
-
-    grad_four = jnp.concatenate([grad_query, grad_forget, grad_value, grad_outgate], axis=1)
-    owner = jnp.logical_or(place == 0, place == tp - 1)
-    gap_row = lax.dynamic_update_slice(jnp.zeros((tp * local,), F32), gap_part[0], (place * local,))
-    small = jnp.zeros((8, width), F32)
-    small = small.at[1].set(jnp.where(owner, ffn_gain_part[0], 0.0))
-    small = small.at[2, :HEAD_DIM].set(head_part[0]).at[3, : tp * local].set(gap_row)
-    jobs, operands, sums_mix = [VectorJob(small)], [grad_four, w_four], None
+
+    jobs, sums_ffn = scattered([grad_w_both, grad_w_down], [0, 1])
+    if ctx == 2:
+        jobs.append(MixBackJob(valid, grad_branch, w_out, mixed, pre, states, gap, head_row, state_end))
+    result, _, *more = line_sum(
+        "sum_feed", (0, 1, NN), [middle], ffn_row, 0, output_rows, 5, jobs, [hidden, w_back]
+    )
+    result = result.reshape(groups, span, width)
+    if ctx == 2:
+        out_both, out_down, grad_query, grad_forget, grad_value, grad_outgate, gap_part, head_part = more
+    else:
+        out_both, out_down = sums_ffn
+        grad_gated = dot(grad_branch, w_out, NT)
+        grad_outgate, grad_mixed, head_part, local_begin = plain_call(
+            functools.partial(span_begin_kernel, heads, length), "span_begin", (chunks,),
+            [column_back(0), column_back(0), column_back(0), column_back(1), column_back(3), fixed((1, local)),
+             fixed((1, HEAD_DIM))],
+            [column_back(0), column_back(0), fixed((1, HEAD_DIM)), fixed(state_shape)],
+            [
+                jax.ShapeDtypeStruct((rows, local), BF16),
+                jax.ShapeDtypeStruct((rows, local), BF16),
+                jax.ShapeDtypeStruct((1, HEAD_DIM), F32),
+                jax.ShapeDtypeStruct(state_shape, F32),
+            ],
+            [], 3 * work, 6 * moved,
+        )(valid, grad_gated, mixed, pre, pre, pre, gap, head_row)
+        grad_end = from_later(local_begin, span_decay, "ctx")
+        grad_query, grad_forget, grad_value, gap_part = plain_call(
+            functools.partial(mix_back_kernel, heads, length), "mix_back", (chunks,),
+            [column_back(0), column_back(0), column_back(1), column_back(2), fixed((1, local)),
+             pl.BlockSpec((1,) + state_shape, lambda i, *_: (chunks - 1 - i, 0, 0, 0)), fixed(state_shape),
+             fixed(state_shape)],
+            [column_back(0), column_back(0), column_back(0), fixed((1, local))],
+            [jax.ShapeDtypeStruct((rows, local), BF16)] * 3 + [jax.ShapeDtypeStruct((1, local), F32)],
+            [pltpu.VMEM(state_shape, F32), pltpu.VMEM(state_shape, F32)], 12 * work, 6 * moved,
+        )(valid, grad_mixed, pre, pre, pre, gap, states, state_end, grad_end)
+
+    grad_four = (grad_query, grad_forget, grad_value, grad_outgate)
+    jobs, operands, sums_mix = [VectorJob(ffn_gain_part, head_part, gap_part)], [grad_four, w_four], None
     if ctx == 2:
         shapes = [(width, 4 * local), (local, width)]
         jobs.append(ProductScatterJob([(2, 0), (3, 4)], shapes, [0, 1]))
         operands += [normed, gated, grad_branch]
     else:
-        grads = [dot(normed, grad_four, TN).astype(BF16), dot(gated, grad_branch, TN).astype(BF16)]
+        grads = [dot(normed, jnp.concatenate(grad_four, axis=1), TN).astype(BF16), dot(gated, grad_branch, TN).astype(BF16)]
         _, sums_mix = scattered(grads, [0, 1])
     input_grad, _, sums, *more = line_sum(
         "sum_norm_one", (0, 1, NT), [x, grad_middle], norm_row, 0, input_grad_rows, 4, jobs, operands

time: 678 us -> 619 us (0.913)
  Pallas kernels: 594 us -> 565 us
  other arithmetic: 10.2 us -> 0 us
    pallas_call x2 -> x0, Pallas kernels: 27.7 us -> none  [the longest x1 17 us: per_device(): plain_call(functools.partial(mix_back_kernel, heads, length), 'mix_back',...]
    concatenate x2 -> x0, other arithmetic: 9.35 us -> none  [the longest x1 5.55 us: per_device(): grad_both = jnp.concatenate([grad_gate, grad_up], axis=1)]
    dot_general x3 -> x2, matrix products: 38.9 us -> 32.4 us  [dot(): lax.dot_general(left, right, (dims, ((), ())), preferred_element_type=F32)]
  transfers between devices with their start and end apart: 2 -> 1, of which waited for: 1 -> 1; matrix products, arithmetic and copies ran while one was open for 1% -> 0% of each run, Pallas kernels for 0% -> 0%
where the time goes in v4:
time: 619 us; the launch traced here: 618 us
  Pallas kernels  565 us (91%)
  matrix products  32.4 us (5%)
  local copies, waits for them, and re-layouts  16 us (3%)
    pallas_call x4, Pallas kernels, line_sum(): pl.pallas_call(kernel, out_shape=[jax.ShapeDtypeStruct((rows, width), BF1...  486 us
    pallas_call x1, Pallas kernels, project(): pl.pallas_call(kernel, out_shape=[jax.ShapeDtypeStruct((rows, total), F32...  56.5 us
    dot_general x2, matrix products, dot(): lax.dot_general(left, right, (dims, ((), ())), preferred_element_type=F32)  32.4 us
    pallas_call x1, Pallas kernels, per_device(): plain_call(functools.partial(mix_kernel, heads, length), 'mix', (chunks,)...  12.9 us
  transfers between devices with their start and end apart: 1, of which 1 were waited for; matrix products, arithmetic and copies ran while one was open for 0% of the time, Pallas kernels for 0%

profile of v4, /device:TPU:0, one launch (start us, length us, event | category | flops | bytes accessed | tf_op | source)
XLA Modules:
  0.0 617.7 jit_solution(1241821505548409993)
XLA Ops:
  1.3 56.5 %project.1 = (f32[1024,2048]{1,0:T(8,128)}, bf16[1024,2048]{1,0:T(8,128)(2,1)}, bf16[1024,2048]{1,0:T(8,128)(2,1)}, bf16[2048,2048]{1,0:T(8,128)(2,1)}, bf16[512,2048]{1,0:T(8,128)(2,1)}) custom-call(s32[1]{0:T(128)S(6)} %min.6.valid_ref.refs_6_, f32[1,2048]{1,0:T(1,128)} %bitcast.27, bf16[1024,2048]{1,0:T(8,128)(2,1)} %bitcast.18, ...), custom_call_target="tpu_custom_call" | custom-call | tf_op jit(solution)/shard_map/project/pallas_call | solution.py:412
  57.8 9.7 %span_end.1 = f32[4,128,128]{2,1,0:T(8,128)} custom-call(s32[1]{0:T(128)S(6)} %min.6.valid_ref.refs_6_, f32[1024,2048]{1,0:T(8,128)} %get-tuple-element.45.forget_ref.value_ref.query_ref.gate_ref.refs_10_, f32[1024,2048]{1,0:T(8,128)} %get-tuple-element.45.forget_ref.value_ref.query_ref.gate_ref.refs_10_, f32[1,512]{1,0:T(1,128)} %bitcast.29), custom_call_target="tpu_custom_call" | custom-call | flops 402653184 | bytes 4194304 | tf_op jit(solution)/shard_map/span_end/pallas_call | solution.py:1458
  67.4 2.4 collective-permute-start
  69.8 0.8 collective-permute-done.start_ref
  70.6 12.9 %mix.1 = (bf16[1024,512]{1,0:T(8,128)(2,1)}, f32[1024,512]{1,0:T(8,128)}, f32[8,4,128,128]{3,2,1,0:T(8,128)}, f32[4,128,128]{2,1,0:T(8,128)}) custom-call(s32[1]{0:T(128)S(6)} %min.6.valid_ref.refs_6_, f32[1024,2048]{1,0:T(8,128)} %get-tuple-element.45.forget_ref.value_ref.query_ref.gate_ref.refs_10_, ...), custom_call_target="tpu_custom_call" | custom-call | flops 805306368 | bytes 12582912 | tf_op jit(solution)/shard_map/mix/pallas_call | solution.py:1470
  83.5 117.6 %sum_branch.1 = (bf16[1024,2048]{1,0:T(8,128)(2,1)}, f32[512,2048]{1,0:T(8,128)}, f32[8,2048]{1,0:T(8,128)}, bf16[2048,2816]{1,0:T(8,128)(2,1)}, bf16[1408,2048]{1,0:T(8,128)(2,1)}) custom-call(f32[1,2048]{1,0:T(1,128)} %bitcast.24, bf16[1024,2048]{1,0:T(8,128)(2,1)} %bitcast.19, bf16[1024,512]{1,0:T(8,128)(2,1)} %get-tuple-element.46.refs_2_.refs_9_, ...), custom_call_target="tpu_custom_call" | custom-call | tf_op jit(solution)/shard_map/sum_branch/pallas_call | solution.py:1161
  201.2 0.0 copy-start
  201.2 0.0 copy-start.1
  201.2 18.8 %fusion.4 = f32[1024,2816]{1,0:T(8,128)} fusion(bf16[1024,2048]{1,0:T(8,128)(2,1)} %get-tuple-element.49.refs_8_, bf16[2048,2816]{1,0:T(8,128)(2,1)} %get-tuple-element.50.refs_5_), kind=kOutput, calls=%fused_computation.10 | convolution fusion | flops 11811160064 | bytes 27262976 | tf_op jit(solution)/shard_map/dot_general | solution.py:21
  220.0 0.0 copy-done
  220.0 0.0 copy-done.1
  220.0 13.5 %multiply_convert_fusion = (bf16[1024,1408]{1,0:T(8,128)(2,1)}, bf16[1024,1408]{1,0:T(8,128)(2,1)}, bf16[1024,1408]{1,0:T(8,128)(2,1)}) fusion(f32[1024,2816]{1,0:T(8,128)} %fusion.4, bf16[1024,2048]{1,0:T(8,128)(2,1)S(1)} %copy-done, bf16[1408,2048]{1,0:T(8,128)(2,1)S(1)} %copy-done.1), kind=kOutput, calls=%fused_computation | convolution fusion | flops 5927206912 | bytes 30146560 | tf_op jit(solution)/shard_map/dot_general | solution.py:21
  233.6 125.3 %sum_norm_two.1 = (bf16[1024,2048]{1,0:T(8,128)(2,1)}, f32[512,2048]{1,0:T(8,128)}, f32[8,2048]{1,0:T(8,128)}, bf16[1408,2048]{1,0:T(8,128)(2,1)}, bf16[2048,2816]{1,0:T(8,128)(2,1)}) custom-call(f32[1,2048]{1,0:T(1,128)} %bitcast.25, f32[512,2048]{1,0:T(8,128)} %get-tuple-element.48.refs_1_, bf16[1024,2048]{1,0:T(8,128)(2,1)} %get-tuple-element.52.refs_2_.refs_7_, ...), custom_call_target="tpu_custom_call" | custom-call | tf_op jit(solution)/shard_map/sum_norm_two/pallas_call | solution.py:1161
  358.9 117.5 %sum_feed.1 = (bf16[1024,2048]{1,0:T(8,128)(2,1)}, f32[8,2048]{1,0:T(8,128)}, f32[256,2816]{1,0:T(8,128)}, f32[1408,256]{1,0:T(8,128)}, bf16[1024,512]{1,0:T(8,1...) custom-call(f32[1,2048]{1,0:T(1,128)} %bitcast.26, ...), custom_call_target="tpu_custom_call" | custom-call | tf_op jit(solution)/shard_map/sum_feed/pallas_call | solution.py:1161
  476.4 125.2 %sum_norm_one.1 = (bf16[1024,2048]{1,0:T(8,128)(2,1)}, f32[8,2048]{1,0:T(8,128)}, f32[8,2048]{1,0:T(8,128)}, f32[256,2048]{1,0:T(8,128)}, f32[512,256]{1,0:T(8,128)}) custom-call(f32[1,2048]{1,0:T(1,128)} %bitcast.28, bf16[1024,2048]{1,0:T(8,128)(2,1)} %bitcast.20, f32[512,2048]{1,0:T(8,128)} %get-tuple-element.60.refs_2_, ...), custom_call_target="tpu_custom_call" | custom-call | tf_op jit(solution)/shard_map/sum_norm_one/pallas_call | solution.py:1161
  601.7 0.0 copy-start.4
  601.7 1.3 slice_bitcast_fusion
  603.0 1.6 fusion.3
  604.6 0.0 copy-start.2
  604.6 3.0 fusion.2
  607.6 0.0 copy-done.4
  607.6 1.8 fusion.1
  609.4 0.6 constant_dynamic-slice_fusion
  609.9 0.0 copy-done.2
  609.9 0.0 copy-start.3
  609.9 2.1 copy.34
  612.1 1.6 copy-done.3
  613.6 0.0 copy-start.6
  613.6 0.0 copy-start.5
  613.7 2.1 copy.35
  615.7 0.0 copy-done.6
  615.8 0.8 copy.36
  616.5 0.1 copy-done.5
  616.6 1.1 copy.37
Async XLA Ops:
  67.4 3.1 collective-permute-start
  201.2 18.9 %copy-start = (bf16[1024,2048]{1,0:T(8,128)(2,1)S(1)}, bf16[1024,2048]{1,0:T(8,128)(2,1)}, u32[]{:S(2)}) copy-start(bf16[1024,2048]{1,0:T(8,128)(2,1)} %get-tuple-element.52.refs_2_.refs_7_) | copy-start | bytes 12582916
  201.2 18.9 %copy-start.1 = (bf16[1408,2048]{1,0:T(8,128)(2,1)S(1)}, bf16[1408,2048]{1,0:T(8,128)(2,1)}, u32[]{:S(2)}) copy-start(bf16[1408,2048]{1,0:T(8,128)(2,1)} %get-tuple-element.51.refs_3_) | copy-start | bytes 17301508
  601.7 5.9 copy-start.4
  604.6 5.4 copy-start.2
  609.9 3.7 copy-start.3
  613.6 2.1 copy-start.6
  613.6 3.0 copy-start.5

commit v5 on v4

--- a/solution.py
+++ b/solution.py
@@ -439,38 +439,142 @@
     )(valid, gain, x, cotangent, *shards, w_out_shard)
 
 
-class GatherJob:
-    def __init__(self, shards, out_shapes, where):
-        self.size = lax.axis_size("fsdp")
-        self.inputs, self.in_specs = shards, [WHOLE] * len(shards)
-        self.out_shape = [jax.ShapeDtypeStruct(s, BF16) for s in out_shapes]
-        self.out_specs = [ANY] * len(out_shapes)
-        self.scratch = RingGather.scratch(len(shards), self.size)
-        self.where = where
-
-    def bind(self, ins, outs, scratch):
-        self.job = RingGather(ins, outs, self.where, scratch, self.size, self.size == 4)
-
-    def peers(self):
-        return self.job.peers()
+class Job:
+    first = 0
 
     def tasks(self):
         return []
 
+    def follow(self, step, ways):
+        pass
+
+
+class ForwardJob(Job):
+    def __init__(self, shards, grad_low, rows_in_group, first):
+        self.size = lax.axis_size("fsdp")
+        self.rows, self.width = grad_low.shape
+        self.ff = shards[0].shape[1]
+        self.group, self.first = rows_in_group, first
+        self.inputs, self.in_specs = [*shards, grad_low], [ANY] * 4
+        self.out_shape = [
+            jax.ShapeDtypeStruct((self.width, 2 * self.ff), BF16),
+            jax.ShapeDtypeStruct((self.ff, self.width), BF16),
+            *[jax.ShapeDtypeStruct((self.rows, self.ff), BF16)] * 3,
+        ]
+        self.out_specs = [ANY] * 5
+        self.scratch = [
+            pltpu.VMEM((self.width, 2 * self.ff), BF16),
+            pltpu.VMEM((self.ff, self.width), BF16),
+            pltpu.VMEM((self.rows, self.width), BF16),
+            pltpu.VMEM((2, self.group, 2 * self.ff), F32),
+            pltpu.VMEM((2, 3, self.group, self.ff), BF16),
+            pltpu.SemaphoreType.DMA((3,)),
+            pltpu.SemaphoreType.DMA((2, 3)),
+            *RingGather.scratch(2, self.size),
+            *RingGather.scratch(1, self.size),
+        ]
+
+    def bind(self, ins, outs, scratch):
+        self.grad_low = ins[3]
+        self.both_out, self.back_out, *self.outs = outs
+        self.both, self.back, self.grad_here, self.products, self.stage, self.sem, self.stage_sem = scratch[:7]
+        size = self.size
+        self.inward = RingGather(ins[:2], [self.both], [(0, 0, 0), (0, 0, self.ff)], scratch[7:12], size, size == 4)
+        self.outward = RingGather(ins[2:3], [self.back], [(0, 1, 0)], scratch[12:], size, size == 4)
+
+    def peers(self):
+        return self.inward.peers()
+
     def cuts(self, steps):
-        return [((2 * steps - 2) * (i + 1)) // self.size for i in range(self.size - 1)]
+        ring = self.size - 1
+        ahead = [((16 * (i + 1)) // ring * steps) // 20 for i in range(ring)]
+        return ahead + [((16 + (9 * (i + 1)) // ring) * steps) // 20 for i in range(ring)]
+
+    def load(self):
+        return pltpu.make_async_copy(self.grad_low, self.grad_here, self.sem.at[0])
+
+    def keep(self):
+        return [
+            pltpu.make_async_copy(self.both, self.both_out, self.sem.at[1]),
+            pltpu.make_async_copy(self.back, self.back_out, self.sem.at[2]),
+        ]
 
     def start(self):
-        self.job.start()
+        self.inward.start()
+        self.load().start()
 
     def advance(self, number):
-        self.job.advance(number)
+        ring = self.size - 1
+        if number < ring:
+            self.inward.advance(number)
+            if number == max(0, ring - 2):
+                self.outward.start()
+            return
+        self.outward.advance(number - ring)
+        if number == 2 * ring - 1:
+            for step in range(ring):
+                self.inward.wait_across(range(2), step)
+                self.outward.wait_across(range(1), step)
+            for i in range(2):
+                self.inward.local_copy(i).wait()
+            self.outward.local_copy(0).wait()
+            self.load().wait()
+            for copy in self.keep():
+                copy.start()
+
+    def save(self, way, k, at):
+        return pltpu.make_async_copy(self.stage.at[way, k], self.outs[k].at[at, :], self.stage_sem.at[way, k])
+
+    def follow(self, step, ways):
+        normed, begins, periods, groups, bases = ways
+
+        @pl.loop(0, 2)
+        def _(way):
+            begin, period, base = (jnp.where(way == 0, pair[0], pair[1]) for pair in (begins, periods, bases))
+            k = step - begin
+            g = lax.div(k, period)
+            part = lax.rem(k, period)
+            busy = jnp.logical_and(k >= 0, g < groups)
+            at = pl.ds(pl.multiple_of(base + g * self.group, self.group), self.group)
+
+            @pl.when(jnp.logical_and(busy, part == 0))
+            def _():
+                product_tile(normed, self.both, NN, at, self.products.at[way])
+
+            @pl.when(jnp.logical_and(busy, part == 1))
+            def _():
+                @pl.when(g > 0)
+                def _():
+                    for n in range(3):
+                        self.save(way, n, at).wait()
+
+                grad_rows = self.grad_here[at, :]
+                products, stage, ff = self.products.at[way], self.stage.at[way], self.ff
+                wide = min(512, ff)
+                for start in range(0, ff, wide):
+                    length = min(wide, ff - start)
+                    cols = slice(start, start + length)
+                    gate, up = products[:, cols], products[:, ff + start : ff + start + length]
+                    grad = dot(grad_rows, self.back[cols, :], NT)
+                    sig = sigmoid(gate)
+                    value = gate * sig
+                    stage[0, :, cols] = (value * up).astype(BF16)
+                    stage[1, :, cols] = (grad * up * slope(gate, sig)).astype(BF16)
+                    stage[2, :, cols] = (grad * value).astype(BF16)
+                for n in range(3):
+                    self.save(way, n, at).start()
 
     def finish(self):
-        self.job.finish()
-
-
-class ScatterJob(GatherJob):
+        for way in range(2):
+            for n in range(3):
+                self.save(way, n, pl.ds(0, self.group)).wait()
+        for copy in self.keep():
+            copy.wait()
+        self.inward.finish(range(2))
+        self.outward.finish(range(1))
+
+
+class ScatterJob(Job):
     def __init__(self, grads, dims):
         self.size = lax.axis_size("fsdp")
         self.dims = dims
@@ -485,12 +589,24 @@
             ins, outs, self.dims, scratch[:-5], scratch[-5:], self.size, self.size == 4
         )
 
+    def peers(self):
+        return self.job.peers()
+
+    def start(self):
+        self.job.start()
+
+    def advance(self, number):
+        self.job.advance(number)
+
+    def finish(self):
+        self.job.finish()
+
     def cuts(self, steps):
         first, last = (2 * steps) // 5, 2 * steps - 2
         return [first + ((last - first) * i) // (self.size - 1) for i in range(self.size)]
 
 
-class ProductJob:
+class ProductJob(Job):
     def __init__(self, left_at, right_at, dims, shape, tile):
         self.left_at, self.right_at, self.dims, self.shape, self.tile = left_at, right_at, dims, shape, tile
         self.inputs, self.in_specs = [], []
@@ -612,7 +728,7 @@
             job.across(i, offset).start()
 
 
-class MixBackJob:
+class MixBackJob(Job):
     def __init__(self, valid, grad_branch, w_out, mixed, pre, states, gap, gain, state_end):
         self.rows, self.width = grad_branch.shape
         self.local = w_out.shape[0]
@@ -791,7 +907,7 @@
         self.across().wait_send()
 
 
-class VectorJob:
+class VectorJob(Job):
     def __init__(self, full, short, split):
         self.axes = [(axis, lax.axis_size(axis)) for axis in ("ctx", "fsdp", "tp")]
         self.inputs, self.in_specs = [full, short, split], [WHOLE] * 3
@@ -1081,6 +1197,14 @@
                     back(way, k).start()
 
         steps = count + skew * (size - 2)
+        extra, followed = 0, None
+        for job in jobs:
+            if isinstance(job, ForwardJob):
+                slowest = max(job.first, per_group + skew * (size - 2))
+                extra = max(0, slowest + (groups - 1) * per_group + 2 - steps, job.first + 2 * groups - steps)
+                arrivals = [jnp.maximum(job.first, per_group + skew * away[1 - way]) for way in range(2)]
+                begins = [jnp.where(owner[way], job.first, arrivals[way]) for way in range(2)]
+                followed = out_ref, begins, [jnp.where(o, 2, per_group) for o in owner], groups, base
         for job in vector:
             job.extra = lambda: jnp.where(
                 lax.broadcasted_iota(jnp.int32, (8, width), 0) == 0, gain_part_ref[...], 0.0
@@ -1093,7 +1217,7 @@
         acts = sorted((cut, n, i) for n, job in enumerate(jobs) for i, cut in enumerate(job.cuts(steps)))
         bounds = {t[0] for t in tasks} | {t[0] + t[1] for t in tasks}
         for number, (act, lead) in enumerate([(add, away), (spread, (away[1], away[0]))]):
-            base_step, high = number * steps, (number + 1) * steps
+            base_step, high = number * steps, (number + 1) * steps + (extra if number else 0)
             low = min([base_step] + [t[0] for t in tasks if number == 0])
             here = [a for a in acts if low <= a[0] < high]
             edges = sorted({low, high} | {a[0] for a in here} | {e for e in bounds if low < e < high})
@@ -1110,6 +1234,9 @@
                     each_way(step, lead, act)
                     for t in active:
                         t[2](step + base_step - t[0])
+                    for job in jobs:
+                        if number and right - base_step > job.first:
+                            job.follow(step, followed)
 
         for first_step, tiles, act, needs in tasks:
             done = min(max(2 * steps - first_step, 0), tiles)
@@ -1480,27 +1607,11 @@
         [pltpu.VMEM(state_shape, F32)], 6 * work, 6 * moved,
     )(valid, pre, pre, pre, pre, gap, head_row, start)
 
-    normed_two, middle, _, w_both, w_back = line_sum(
+    normed_two, middle, _, w_both, w_back, hidden, grad_gate, grad_up = line_sum(
         "sum_branch", (0, 1, NN), [x], ffn_row, 1, middle_rows, 2,
-        [
-            GatherJob(
-                [w_gate, w_up, w_down],
-                [(fsdp * w_gate.shape[0], 2 * ff), (ff, width)],
-                [(0, 0, 0), (0, 0, ff), (1, 1, 0)],
-            )
-        ],
-        [gated, w_out],
+        [ForwardJob([w_gate, w_up, w_down], grad_low, min(128, rows // 2), 5)], [gated, w_out],
     )
 
-    both = dot(normed_two, w_both)
-    gate_hidden, up_hidden = both[:, :ff], both[:, ff:]
-    sig = jax.nn.sigmoid(gate_hidden)
-    act = gate_hidden * sig
-    hidden = (act * up_hidden).astype(BF16)
-
-    grad_hidden = dot(grad_low, w_back, NT)
-    grad_gate = (grad_hidden * up_hidden * slope(gate_hidden, sig)).astype(BF16)
-    grad_up = (grad_hidden * act).astype(BF16)
     both_axes = ("fsdp", "ctx")
 
     def scattered(grads, dims):

time: 619 us -> 605 us (0.977)
  matrix products: 32.4 us -> 0 us
  Pallas kernels: 565 us -> 583 us
    dot_general x2 -> x0, matrix products: 32.4 us -> none  [dot(): lax.dot_general(left, right, (dims, ((), ())), preferred_element_type=F32)]
    pallas_call x4, Pallas kernels: 486 us -> 504 us  [line_sum(): pl.pallas_call(kernel, out_shape=[jax.ShapeDtypeStruct((rows, width), BF1...]
where the time goes in v5:
time: 605 us; the launch traced here: 604 us
  Pallas kernels  583 us (96%)
  local copies, waits for them, and re-layouts  16.8 us (3%)
    pallas_call x4, Pallas kernels, line_sum(): pl.pallas_call(kernel, out_shape=[jax.ShapeDtypeStruct((rows, width), BF1...  504 us
    pallas_call x1, Pallas kernels, project(): pl.pallas_call(kernel, out_shape=[jax.ShapeDtypeStruct((rows, total), F32...  56.6 us
    pallas_call x1, Pallas kernels, per_device(): plain_call(functools.partial(mix_kernel, heads, length), 'mix', (chunks,)...  12.9 us
  transfers between devices with their start and end apart: 1, of which 1 were waited for; matrix products, arithmetic and copies ran while one was open for 0% of the time, Pallas kernels for 0%

profile of v5, /device:TPU:0, one launch (start us, length us, event | category | flops | bytes accessed | tf_op | source)
XLA Modules:
  0.0 604.1 jit_solution(5457596162892738687)
XLA Ops:
  1.3 56.6 %project.1 = (f32[1024,2048]{1,0:T(8,128)}, bf16[1024,2048]{1,0:T(8,128)(2,1)}, bf16[1024,2048]{1,0:T(8,128)(2,1)}, bf16[2048,2048]{1,0:T(8,128)(2,1)}, bf16[512,2048]{1,0:T(8,128)(2,1)}) custom-call(s32[1]{0:T(128)S(6)} %min.6.valid_ref.refs_6_, f32[1,2048]{1,0:T(1,128)} %bitcast.23, bf16[1024,2048]{1,0:T(8,128)(2,1)} %bitcast.14, ...), custom_call_target="tpu_custom_call" | custom-call | tf_op jit(solution)/shard_map/project/pallas_call | solution.py:412
  57.9 9.7 %span_end.1 = f32[4,128,128]{2,1,0:T(8,128)} custom-call(s32[1]{0:T(128)S(6)} %min.6.valid_ref.refs_6_, f32[1024,2048]{1,0:T(8,128)} %get-tuple-element.48.forget_ref.value_ref.query_ref.gate_ref.refs_10_, f32[1024,2048]{1,0:T(8,128)} %get-tuple-element.48.forget_ref.value_ref.query_ref.gate_ref.refs_10_, f32[1,512]{1,0:T(1,128)} %bitcast.25), custom_call_target="tpu_custom_call" | custom-call | flops 402653184 | bytes 4194304 | tf_op jit(solution)/shard_map/span_end/pallas_call | solution.py:1585
  67.6 2.4 collective-permute-start
  69.9 0.8 collective-permute-done.start_ref
  70.7 12.9 %mix.1 = (bf16[1024,512]{1,0:T(8,128)(2,1)}, f32[1024,512]{1,0:T(8,128)}, f32[8,4,128,128]{3,2,1,0:T(8,128)}, f32[4,128,128]{2,1,0:T(8,128)}) custom-call(s32[1]{0:T(128)S(6)} %min.6.valid_ref.refs_6_, f32[1024,2048]{1,0:T(8,128)} %get-tuple-element.48.forget_ref.value_ref.query_ref.gate_ref.refs_10_, ...), custom_call_target="tpu_custom_call" | custom-call | flops 805306368 | bytes 12582912 | tf_op jit(solution)/shard_map/mix/pallas_call | solution.py:1597
  83.6 130.3 %sum_branch.1 = (bf16[1024,2048]{1,0:T(8,128)(2,1)}, f32[512,2048]{1,0:T(8,128)}, f32[8,2048]{1,0:T(8,128)}, bf16[2048,2816]{1,0:T(8,128)(2,1)}, bf16[1408,2048]...) custom-call(f32[1,2048]{1,0:T(1,128)} %bitcast.20, ...), custom_call_target="tpu_custom_call" | custom-call | tf_op jit(solution)/shard_map/sum_branch/pallas_call | solution.py:1288
  214.0 128.7 %sum_norm_two.1 = (bf16[1024,2048]{1,0:T(8,128)(2,1)}, f32[512,2048]{1,0:T(8,128)}, f32[8,2048]{1,0:T(8,128)}, bf16[1408,2048]{1,0:T(8,128)(2,1)}, bf16[2048,2816]{1,0:T(8,128)(2,1)}) custom-call(f32[1,2048]{1,0:T(1,128)} %bitcast.21, f32[512,2048]{1,0:T(8,128)} %get-tuple-element.52.refs_1_, bf16[1024,2048]{1,0:T(8,128)(2,1)} %get-tuple-element.51.refs_7_.refs_2_, ...), custom_call_target="tpu_custom_call" | custom-call | tf_op jit(solution)/shard_map/sum_norm_two/pallas_call | solution.py:1288
  342.7 119.7 %sum_feed.1 = (bf16[1024,2048]{1,0:T(8,128)(2,1)}, f32[8,2048]{1,0:T(8,128)}, f32[256,2816]{1,0:T(8,128)}, f32[1408,256]{1,0:T(8,128)}, bf16[1024,512]{1,0:T(8,1...) custom-call(f32[1,2048]{1,0:T(1,128)} %bitcast.22, ...), custom_call_target="tpu_custom_call" | custom-call | tf_op jit(solution)/shard_map/sum_feed/pallas_call | solution.py:1288
  462.5 124.9 %sum_norm_one.1 = (bf16[1024,2048]{1,0:T(8,128)(2,1)}, f32[8,2048]{1,0:T(8,128)}, f32[8,2048]{1,0:T(8,128)}, f32[256,2048]{1,0:T(8,128)}, f32[512,256]{1,0:T(8,128)}) custom-call(f32[1,2048]{1,0:T(1,128)} %bitcast.24, bf16[1024,2048]{1,0:T(8,128)(2,1)} %bitcast.16, f32[512,2048]{1,0:T(8,128)} %get-tuple-element.66.refs_2_, ...), custom_call_target="tpu_custom_call" | custom-call | tf_op jit(solution)/shard_map/sum_norm_one/pallas_call | solution.py:1288
  587.4 0.0 copy-start.2
  587.4 1.3 slice_bitcast_fusion
  588.7 1.6 fusion.2
  590.3 2.9 fusion.1
  593.1 0.0 copy-done.2
  593.1 0.0 copy-start
  593.1 1.8 fusion
  594.9 0.6 constant_dynamic-slice_fusion
  595.5 0.9 copy-done
  596.4 0.0 copy-start.1
  596.4 2.1 copy.34
  598.5 1.6 copy-done.1
  600.1 0.0 copy-start.4
  600.1 0.0 copy-start.3
  600.1 2.1 copy.35
  602.2 0.0 copy-done.4
  602.2 0.8 copy.36
  603.0 0.1 copy-done.3
  603.0 1.1 copy.37
Async XLA Ops:
  67.6 3.1 collective-permute-start
  587.4 5.8 copy-start.2
  593.1 3.2 copy-start
  596.4 3.7 copy-start.1
  600.1 2.1 copy-start.4
  600.1 3.0 copy-start.3

commit v6 on v5

--- a/solution.py
+++ b/solution.py
@@ -166,11 +166,11 @@
 
 
 class RingScatter:
-    def __init__(self, grads, outs, dims, scratch, sems, size, folded):
-        self.grads, self.outs, self.dims, self.size, self.folded = grads, outs, dims, size, folded
+    def __init__(self, grads, results, dims, scratch, sems, size, folded):
+        self.grads, self.results, self.dims, self.size, self.folded = grads, results, dims, size, folded
         count = len(grads)
-        self.own, self.came, self.passed = scratch[:count], scratch[count : 2 * count], scratch[2 * count :]
-        self.pair_send, self.pair_recv, self.local, self.ring_send, self.ring_recv = sems
+        self.own, self.came, self.passed, self.outs = (scratch[n * count : (n + 1) * count] for n in range(4))
+        self.pair_send, self.pair_recv, self.local, self.ring_send, self.ring_recv, self.saved = sems
         self.place = ring_place(lax.axis_index("fsdp"), size, folded)
         self.core = lax.axis_index("ctx")
 
@@ -251,6 +251,15 @@
                 self.add(i, way, step)
                 if step < self.size - 1:
                     self.ring(i, way, step).start()
+                else:
+                    self.save(i, way).start()
+
+    def save(self, i, way):
+        half = self.outs[i].shape[0] // 2
+        rows = pl.ds(way * half, half)
+        return pltpu.make_async_copy(
+            self.outs[i].at[rows, :], self.results[i].at[rows, :], self.saved.at[2 * i + way]
+        )
 
     def add(self, i, way, step):
         half = self.outs[i].shape[0] // 2
@@ -274,6 +283,7 @@
             for offset in range(self.size):
                 self.across(i, offset).wait_send()
             for way in range(2):
+                self.save(i, way).wait()
                 for step in range(self.size - 1):
                     self.ring(i, way, step).wait_send()
 
@@ -285,13 +295,14 @@
     @staticmethod
     def buffers(shapes, size):
         full = [pltpu.VMEM((size,) + s, BF16) for s in shapes]
-        return full + full + [pltpu.VMEM((2, size - 1, s[0] // 2, s[1]), BF16) for s in shapes]
+        passed = [pltpu.VMEM((2, size - 1, s[0] // 2, s[1]), BF16) for s in shapes]
+        return full + full + passed + [pltpu.VMEM(s, F32) for s in shapes]
 
     @staticmethod
     def scratch(count, size):
         return [pltpu.SemaphoreType.DMA((count * size,)) for _ in range(3)] + [
             pltpu.SemaphoreType.DMA((count * 2 * (size - 1),)) for _ in range(2)
-        ]
+        ] + [pltpu.SemaphoreType.DMA((2 * count,))]
 
 
 def meet(peers):
@@ -418,7 +429,7 @@
             jax.ShapeDtypeStruct((width, total), BF16),
             jax.ShapeDtypeStruct((w_out_shard.shape[0], width), BF16),
         ],
-        in_specs=[pl.BlockSpec(memory_space=pltpu.SMEM), WHOLE, ANY, ANY] + [WHOLE] * (count + 1),
+        in_specs=[pl.BlockSpec(memory_space=pltpu.SMEM), WHOLE, ANY, ANY] + [ANY] * count + [WHOLE],
         out_specs=[ANY] * 5,
         scratch_shapes=[
             pltpu.VMEM((rows, width), BF16),
@@ -581,12 +592,12 @@
         shapes = [RingScatter.out_shape(g, d, self.size) for g, d in zip(grads, dims)]
         self.inputs, self.in_specs = grads, [ANY] * len(grads)
         self.out_shape = [jax.ShapeDtypeStruct(s, F32) for s in shapes]
-        self.out_specs = [WHOLE] * len(grads)
+        self.out_specs = [ANY] * len(grads)
         self.scratch = RingScatter.buffers(shapes, self.size) + RingScatter.scratch(len(grads), self.size)
 
     def bind(self, ins, outs, scratch):
         self.job = RingScatter(
-            ins, outs, self.dims, scratch[:-5], scratch[-5:], self.size, self.size == 4
+            ins, outs, self.dims, scratch[:-6], scratch[-6:], self.size, self.size == 4
         )
 
     def peers(self):
@@ -678,15 +689,16 @@
         shapes = [RingScatter.out_shape(jax.ShapeDtypeStruct(s, BF16), d, self.size) for s, d in zip(shapes, dims)]
         self.inputs, self.in_specs = [], []
         self.out_shape = [jax.ShapeDtypeStruct(s, F32) for s in shapes]
-        self.out_specs = [WHOLE] * len(shapes)
+        self.out_specs = [ANY] * len(shapes)
         self.scratch = [pltpu.VMEM((2, self.size) + s, BF16) for s in shapes]
         self.scratch += [pltpu.VMEM((self.size,) + s, BF16) for s in shapes]
         self.scratch += [pltpu.VMEM((2, self.size - 1, s[0] // 2, s[1]), BF16) for s in shapes]
+        self.scratch += [pltpu.VMEM(s, F32) for s in shapes]
         self.scratch += RingScatter.scratch(len(shapes), self.size)
 
     def bind(self, ins, outs, scratch):
         self.job = RingScatter(
-            [None] * len(outs), outs, self.dims, scratch[:-5], scratch[-5:], self.size, self.size == 4
+            [None] * len(outs), outs, self.dims, scratch[:-6], scratch[-6:], self.size, self.size == 4
         )
 
     def cuts(self, steps):
@@ -1013,11 +1025,12 @@
         half_refs = take(len(halves))
         operand_refs = take(len(pieces))
         job_ins = [take(len(job.inputs)) for job in jobs]
-        (out_ref,) = take(1)
+        (result_ref,) = take(1)
         own_refs = take(n_out)
         (gain_part_ref,) = take(1)
         job_outs = [take(len(job.out_shape)) for job in jobs]
         part_here, came, sum_send, sum_recv, back_send, back_recv, operand_sem, half_sem, own_sem, part_sem = take(10)
+        out_ref, out_sem = take(2)
         half_here = take(len(halves))
         operand_here = take(len(operands))
         own_here = take(n_out)
@@ -1099,6 +1112,9 @@
                 device_id_type=BY_AXIS,
             )
 
+        def save(way, k):
+            return pltpu.make_async_copy(out_ref.at[at(way, k), :], result_ref.at[at(way, k), :], out_sem.at[way, k])
+
         def own_copy(k):
             where = pl.ds(pl.multiple_of(k * chunk, chunk), chunk)
             return pltpu.make_async_copy(own_here[0].at[where, :], own_refs[0].at[where, :], own_sem.at[k])
@@ -1179,6 +1195,7 @@
                         half_here, gain_ref[...], own_here[0] if n_out else None, gain_part_ref, own, total
                     )
                     back(way, k).start()
+                    save(way, k).start()
                     if n_out:
                         own_copy(k).start()
 
@@ -1195,6 +1212,8 @@
                 @pl.when(jnp.logical_not(source[way]))
                 def _():
                     back(way, k).start()
+
+                save(way, k).start()
 
         steps = count + skew * (size - 2)
         extra, followed = 0, None
@@ -1253,6 +1272,10 @@
 
         for way in range(2):
 
+            @pl.loop(0, count)
+            def _(k):
+                save(way, k).wait()
+
             @pl.when(jnp.logical_not(owner[way]))
             def _():
                 @pl.loop(0, count)
@@ -1281,6 +1304,8 @@
         pltpu.SemaphoreType.DMA((max(1, len(halves)),)),
         pltpu.SemaphoreType.DMA((count,)),
         pltpu.SemaphoreType.DMA((2, groups)),
+        pltpu.VMEM((rows, width), BF16),
+        pltpu.SemaphoreType.DMA((2, count)),
         *[pltpu.VMEM((half, width), h.dtype) for h in halves],
         *[pltpu.VMEM(shape, o[0].dtype) for shape, o in zip(operand_shapes, operands)],
         *[pltpu.VMEM((half, width), F32)] * n_out,
@@ -1292,7 +1317,7 @@
         + [jax.ShapeDtypeStruct((8, width), F32)]
         + [shape for job in jobs for shape in job.out_shape],
         in_specs=[ANY] * (not product) + [WHOLE] + [ANY] * (len(halves) + len(pieces)) + [spec for job in jobs for spec in job.in_specs],
-        out_specs=[WHOLE] + [ANY] * n_out + [WHOLE] + [spec for job in jobs for spec in job.out_specs],
+        out_specs=[ANY] + [ANY] * n_out + [WHOLE] + [spec for job in jobs for spec in job.out_specs],
         scratch_shapes=scratch + [shape for job in jobs for shape in job.scratch],
         compiler_params=pltpu.CompilerParams(
             collective_id=collective_id, has_side_effects=True, vmem_limit_bytes=VMEM_BYTES

time: 605 us -> 599 us (0.990)
  no operation moved by 1% of the time
where the time goes in v6:
time: 599 us; the launch traced here: 598 us
  Pallas kernels  577 us (96%)
  local copies, waits for them, and re-layouts  16.8 us (3%)
    pallas_call x4, Pallas kernels, line_sum(): pl.pallas_call(kernel, out_shape=[jax.ShapeDtypeStruct((rows, width), BF1...  498 us
    pallas_call x1, Pallas kernels, project(): pl.pallas_call(kernel, out_shape=[jax.ShapeDtypeStruct((rows, total), F32...  56.2 us
    pallas_call x1, Pallas kernels, per_device(): plain_call(functools.partial(mix_kernel, heads, length), 'mix', (chunks,)...  12.9 us
  transfers between devices with their start and end apart: 1, of which 1 were waited for; matrix products, arithmetic and copies ran while one was open for 0% of the time, Pallas kernels for 0%

profile of v6, /device:TPU:0, one launch (start us, length us, event | category | flops | bytes accessed | tf_op | source)
XLA Modules:
  0.0 598.2 jit_solution(3660509623223397444)
XLA Ops:
  1.3 56.2 %project.1 = (f32[1024,2048]{1,0:T(8,128)}, bf16[1024,2048]{1,0:T(8,128)(2,1)}, bf16[1024,2048]{1,0:T(8,128)(2,1)}, bf16[2048,2048]{1,0:T(8,128)(2,1)}, bf16[512,2048]{1,0:T(8,128)(2,1)}) custom-call(s32[1]{0:T(128)S(6)} %min.6.valid_ref.refs_6_, f32[1,2048]{1,0:T(1,128)} %bitcast.23, bf16[1024,2048]{1,0:T(8,128)(2,1)} %bitcast.14, ...), custom_call_target="tpu_custom_call" | custom-call | tf_op jit(solution)/shard_map/project/pallas_call | solution.py:423
  57.5 9.7 %span_end.1 = f32[4,128,128]{2,1,0:T(8,128)} custom-call(s32[1]{0:T(128)S(6)} %min.6.valid_ref.refs_6_, f32[1024,2048]{1,0:T(8,128)} %get-tuple-element.48.forget_ref.value_ref.query_ref.gate_ref.refs_10_, f32[1024,2048]{1,0:T(8,128)} %get-tuple-element.48.forget_ref.value_ref.query_ref.gate_ref.refs_10_, f32[1,512]{1,0:T(1,128)} %bitcast.25), custom_call_target="tpu_custom_call" | custom-call | flops 402653184 | bytes 4194304 | tf_op jit(solution)/shard_map/span_end/pallas_call | solution.py:1610
  67.1 2.4 collective-permute-start
  69.5 0.8 collective-permute-done.start_ref
  70.3 12.9 %mix.1 = (bf16[1024,512]{1,0:T(8,128)(2,1)}, f32[1024,512]{1,0:T(8,128)}, f32[8,4,128,128]{3,2,1,0:T(8,128)}, f32[4,128,128]{2,1,0:T(8,128)}) custom-call(s32[1]{0:T(128)S(6)} %min.6.valid_ref.refs_6_, f32[1024,2048]{1,0:T(8,128)} %get-tuple-element.48.forget_ref.value_ref.query_ref.gate_ref.refs_10_, ...), custom_call_target="tpu_custom_call" | custom-call | flops 805306368 | bytes 12582912 | tf_op jit(solution)/shard_map/mix/pallas_call | solution.py:1622
  83.2 129.4 %sum_branch.1 = (bf16[1024,2048]{1,0:T(8,128)(2,1)}, f32[512,2048]{1,0:T(8,128)}, f32[8,2048]{1,0:T(8,128)}, bf16[2048,2816]{1,0:T(8,128)(2,1)}, bf16[1408,2048]...) custom-call(f32[1,2048]{1,0:T(1,128)} %bitcast.20, ...), custom_call_target="tpu_custom_call" | custom-call | tf_op jit(solution)/shard_map/sum_branch/pallas_call | solution.py:1313
  212.6 128.1 %sum_norm_two.1 = (bf16[1024,2048]{1,0:T(8,128)(2,1)}, f32[512,2048]{1,0:T(8,128)}, f32[8,2048]{1,0:T(8,128)}, bf16[1408,2048]{1,0:T(8,128)(2,1)}, bf16[2048,2816]{1,0:T(8,128)(2,1)}) custom-call(f32[1,2048]{1,0:T(1,128)} %bitcast.21, f32[512,2048]{1,0:T(8,128)} %get-tuple-element.52.refs_1_, bf16[1024,2048]{1,0:T(8,128)(2,1)} %get-tuple-element.51.refs_7_.refs_2_, ...), custom_call_target="tpu_custom_call" | custom-call | tf_op jit(solution)/shard_map/sum_norm_two/pallas_call | solution.py:1313
  340.7 116.9 %sum_feed.1 = (bf16[1024,2048]{1,0:T(8,128)(2,1)}, f32[8,2048]{1,0:T(8,128)}, f32[256,2816]{1,0:T(8,128)}, f32[1408,256]{1,0:T(8,128)}, bf16[1024,512]{1,0:T(8,1...) custom-call(f32[1,2048]{1,0:T(1,128)} %bitcast.22, ...), custom_call_target="tpu_custom_call" | custom-call | tf_op jit(solution)/shard_map/sum_feed/pallas_call | solution.py:1313
  457.6 123.9 %sum_norm_one.1 = (bf16[1024,2048]{1,0:T(8,128)(2,1)}, f32[8,2048]{1,0:T(8,128)}, f32[8,2048]{1,0:T(8,128)}, f32[256,2048]{1,0:T(8,128)}, f32[512,256]{1,0:T(8,128)}) custom-call(f32[1,2048]{1,0:T(1,128)} %bitcast.24, bf16[1024,2048]{1,0:T(8,128)(2,1)} %bitcast.16, f32[512,2048]{1,0:T(8,128)} %get-tuple-element.66.refs_2_, ...), custom_call_target="tpu_custom_call" | custom-call | tf_op jit(solution)/shard_map/sum_norm_one/pallas_call | solution.py:1313
  581.5 0.0 copy-start.2
  581.5 1.3 slice_bitcast_fusion
  582.8 1.6 fusion.2
  584.4 2.9 fusion.1
  587.2 0.0 copy-done.2
  587.2 0.0 copy-start
  587.2 1.8 fusion
  589.0 0.6 constant_dynamic-slice_fusion
  589.6 0.9 copy-done
  590.5 0.0 copy-start.1
  590.5 2.1 copy.34
  592.6 1.6 copy-done.1
  594.2 0.0 copy-start.4
  594.2 0.0 copy-start.3
  594.2 2.1 copy.35
  596.3 0.0 copy-done.4
  596.3 0.8 copy.36
  597.1 0.1 copy-done.3
  597.1 1.1 copy.37
Async XLA Ops:
  67.1 3.1 collective-permute-start
  581.5 5.8 copy-start.2
  587.2 3.2 copy-start
  590.5 3.7 copy-start.1
  594.2 2.1 copy-start.4
  594.2 3.0 copy-start.3

commit v7 on v6

--- a/solution.py
+++ b/solution.py
@@ -992,7 +992,7 @@
 
 
 def line_sum(
-    name, part, halves, gain, n_out, epilogue, collective_id, jobs=(), operands=(), chunk=32, skew=2
+    name, part, halves, gain, n_out, epilogue, collective_id, jobs=(), operands=(), chunk=32, skew=2, group=128
 ):
     size = lax.axis_size("tp")
     product = isinstance(part, tuple)
@@ -1008,7 +1008,7 @@
     half = rows // 2
     chunk = min(chunk, half)
     count = half // chunk
-    group = min(128, half)
+    group = min(group, half)
     groups = half // group
     per_group = group // chunk
     vector = [job for job in jobs if isinstance(job, VectorJob)]
@@ -1649,7 +1649,7 @@
     grad_branch, grad_middle, ffn_gain_part, grad_w_down, grad_w_both = line_sum(
         "sum_norm_two", (0, 1, NT), [middle, grad_low], ffn_row, 1, grad_middle_rows, 3,
         [ProductJob(2, 3, TN, (ff, width), 128), ProductJob(4, 0, TN, (width, 2 * ff), 128)],
-        [(grad_gate, grad_up), w_both, hidden, grad_low, normed_two],
+        [(grad_gate, grad_up), w_both, hidden, grad_low, normed_two], group=256,
     )
 
     jobs, sums_ffn = scattered([grad_w_both, grad_w_down], [0, 1])

time: 599 us -> 593 us (0.990)
  Pallas kernels: 577 us -> 571 us
    pallas_call x4, Pallas kernels: 498 us -> 492 us  [line_sum(): pl.pallas_call(kernel, out_shape=[jax.ShapeDtypeStruct((rows, width), BF1...]
where the time goes in v7:
time: 593 us; the launch traced here: 592 us
  Pallas kernels  571 us (96%)
  local copies, waits for them, and re-layouts  16.8 us (3%)
    pallas_call x4, Pallas kernels, line_sum(): pl.pallas_call(kernel, out_shape=[jax.ShapeDtypeStruct((rows, width), BF1...  492 us
    pallas_call x1, Pallas kernels, project(): pl.pallas_call(kernel, out_shape=[jax.ShapeDtypeStruct((rows, total), F32...  56.2 us
    pallas_call x1, Pallas kernels, per_device(): plain_call(functools.partial(mix_kernel, heads, length), 'mix', (chunks,)...  12.9 us
  transfers between devices with their start and end apart: 1, of which 1 were waited for; matrix products, arithmetic and copies ran while one was open for 0% of the time, Pallas kernels for 0%

profile of v7, /device:TPU:0, one launch (start us, length us, event | category | flops | bytes accessed | tf_op | source)
XLA Modules:
  0.0 592.0 jit_solution(17005034961371310327)
XLA Ops:
  1.3 56.2 %project.1 = (f32[1024,2048]{1,0:T(8,128)}, bf16[1024,2048]{1,0:T(8,128)(2,1)}, bf16[1024,2048]{1,0:T(8,128)(2,1)}, bf16[2048,2048]{1,0:T(8,128)(2,1)}, bf16[512,2048]{1,0:T(8,128)(2,1)}) custom-call(s32[1]{0:T(128)S(6)} %min.6.valid_ref.refs_6_, f32[1,2048]{1,0:T(1,128)} %bitcast.23, bf16[1024,2048]{1,0:T(8,128)(2,1)} %bitcast.14, ...), custom_call_target="tpu_custom_call" | custom-call | tf_op jit(solution)/shard_map/project/pallas_call | solution.py:423
  57.5 9.7 %span_end.1 = f32[4,128,128]{2,1,0:T(8,128)} custom-call(s32[1]{0:T(128)S(6)} %min.6.valid_ref.refs_6_, f32[1024,2048]{1,0:T(8,128)} %get-tuple-element.48.forget_ref.value_ref.query_ref.gate_ref.refs_10_, f32[1024,2048]{1,0:T(8,128)} %get-tuple-element.48.forget_ref.value_ref.query_ref.gate_ref.refs_10_, f32[1,512]{1,0:T(1,128)} %bitcast.25), custom_call_target="tpu_custom_call" | custom-call | flops 402653184 | bytes 4194304 | tf_op jit(solution)/shard_map/span_end/pallas_call | solution.py:1610
  67.1 2.4 collective-permute-start
  69.5 0.8 collective-permute-done.start_ref
  70.3 12.9 %mix.1 = (bf16[1024,512]{1,0:T(8,128)(2,1)}, f32[1024,512]{1,0:T(8,128)}, f32[8,4,128,128]{3,2,1,0:T(8,128)}, f32[4,128,128]{2,1,0:T(8,128)}) custom-call(s32[1]{0:T(128)S(6)} %min.6.valid_ref.refs_6_, f32[1024,2048]{1,0:T(8,128)} %get-tuple-element.48.forget_ref.value_ref.query_ref.gate_ref.refs_10_, ...), custom_call_target="tpu_custom_call" | custom-call | flops 805306368 | bytes 12582912 | tf_op jit(solution)/shard_map/mix/pallas_call | solution.py:1622
  83.2 129.4 %sum_branch.1 = (bf16[1024,2048]{1,0:T(8,128)(2,1)}, f32[512,2048]{1,0:T(8,128)}, f32[8,2048]{1,0:T(8,128)}, bf16[2048,2816]{1,0:T(8,128)(2,1)}, bf16[1408,2048]...) custom-call(f32[1,2048]{1,0:T(1,128)} %bitcast.20, ...), custom_call_target="tpu_custom_call" | custom-call | tf_op jit(solution)/shard_map/sum_branch/pallas_call | solution.py:1313
  212.6 121.7 %sum_norm_two.1 = (bf16[1024,2048]{1,0:T(8,128)(2,1)}, f32[512,2048]{1,0:T(8,128)}, f32[8,2048]{1,0:T(8,128)}, bf16[1408,2048]{1,0:T(8,128)(2,1)}, bf16[2048,2816]{1,0:T(8,128)(2,1)}) custom-call(f32[1,2048]{1,0:T(1,128)} %bitcast.21, f32[512,2048]{1,0:T(8,128)} %get-tuple-element.52.refs_1_, bf16[1024,2048]{1,0:T(8,128)(2,1)} %get-tuple-element.51.refs_7_.refs_2_, ...), custom_call_target="tpu_custom_call" | custom-call | tf_op jit(solution)/shard_map/sum_norm_two/pallas_call | solution.py:1313
  334.3 117.0 %sum_feed.1 = (bf16[1024,2048]{1,0:T(8,128)(2,1)}, f32[8,2048]{1,0:T(8,128)}, f32[256,2816]{1,0:T(8,128)}, f32[1408,256]{1,0:T(8,128)}, bf16[1024,512]{1,0:T(8,1...) custom-call(f32[1,2048]{1,0:T(1,128)} %bitcast.22, ...), custom_call_target="tpu_custom_call" | custom-call | tf_op jit(solution)/shard_map/sum_feed/pallas_call | solution.py:1313
  451.4 123.9 %sum_norm_one.1 = (bf16[1024,2048]{1,0:T(8,128)(2,1)}, f32[8,2048]{1,0:T(8,128)}, f32[8,2048]{1,0:T(8,128)}, f32[256,2048]{1,0:T(8,128)}, f32[512,256]{1,0:T(8,128)}) custom-call(f32[1,2048]{1,0:T(1,128)} %bitcast.24, bf16[1024,2048]{1,0:T(8,128)(2,1)} %bitcast.16, f32[512,2048]{1,0:T(8,128)} %get-tuple-element.66.refs_2_, ...), custom_call_target="tpu_custom_call" | custom-call | tf_op jit(solution)/shard_map/sum_norm_one/pallas_call | solution.py:1313
  575.3 0.0 copy-start.2
  575.3 1.3 slice_bitcast_fusion
  576.6 1.6 fusion.2
  578.2 2.9 fusion.1
  581.1 0.0 copy-done.2
  581.1 0.0 copy-start
  581.1 1.8 fusion
  582.8 0.6 constant_dynamic-slice_fusion
  583.4 0.9 copy-done
  584.3 0.0 copy-start.1
  584.3 2.1 copy.34
  586.4 1.6 copy-done.1
  588.0 0.0 copy-start.4
  588.0 0.0 copy-start.3
  588.0 2.1 copy.35
  590.1 0.0 copy-done.4
  590.1 0.8 copy.36
  590.9 0.1 copy-done.3
  590.9 1.1 copy.37
Async XLA Ops:
  67.1 3.1 collective-permute-start
  575.3 5.8 copy-start.2
  581.1 3.2 copy-start
  584.3 3.7 copy-start.1
  588.0 2.1 copy-start.4
  588.0 3.0 copy-start.3
